TPU v7x, 128 devices: a whole 4x4x4 slice. The times are simulated.
128 devices in a mesh: layer: 4 (over z), panel: 32 (over x, y, core).
Axes of the slice: x: 4, y: 4, z: 4, core: 2. Of those that a mesh axis runs over, the one named last changes fastest.
Arguments:
- reflections: float32 [32, 1024, 1024], P(None, 'panel'), may hold values from -0.95 to 0.95
- wave_decay: float32 [32, 1024], replicated, may hold values from 0.3 to 3
- thickness: float32 [4], P('layer'), may hold values from 0.4 to 1
- material: int32 [4], P('layer'), may hold values from 0 to 31
Outputs:
- stack_blocks: float32 [4, 1024, 1024], P('layer', 'panel')
All inputs are finite; a program needn't handle non-finite values.
Results may differ from a plain program's by a relative error of at most 0.00014.
Values sent between devices are 32-bit elements; how exact they have to be, the bound alone decides.
No kernel may reach another device: no remote copies, remote signals or barrier semaphores. Data moves between devices by JAX's collectives and lax.ppermute only.
A program may use at most 128 MiB of HBM per device.

v0:
```python
import jax
import jax.numpy as jnp
from jax import lax
from jax.sharding import PartitionSpec as P

TERMS = 6


def swapped(block, axis, bit):
    count = lax.axis_size(axis)
    route = []
    for low in range(count):
        high = low | 1 << bit
        if high != low and high < count:
            route += [(low, high), (high, low)]
    return lax.ppermute(block, axis, route)


def product(left_side, right_side):
    return jnp.dot(
        left_side, right_side, precision=lax.Precision.HIGHEST, preferred_element_type=jnp.float32
    )


def series_sum(start_rows, factor_one, factor_two):
    term_now = start_rows
    summed = start_rows
    for _ in range(TERMS - 1):
        term_now = product(product(term_now, factor_one), factor_two)
        summed = summed + term_now
    return summed


def local(reflections, wave_decay, thickness, material):
    panel_rows = reflections.shape[1]
    order_full = reflections.shape[2]
    row_start = lax.axis_index("panel") * panel_rows
    chosen = material[0]
    refl_rows = lax.dynamic_index_in_dim(reflections, chosen, 0, keepdims=False)
    decays = jnp.exp(
        -lax.dynamic_index_in_dim(wave_decay, chosen, 0, keepdims=False) * thickness[0]
    )
    refl_full = lax.all_gather(refl_rows, "panel", axis=0, tiled=True)
    scaled_refl = decays[:, None] * refl_full
    row_ids = row_start + jnp.arange(panel_rows, dtype=jnp.int32)
    identity_rows = jnp.where(
        row_ids[:, None] == jnp.arange(order_full, dtype=jnp.int32)[None, :], 1.0, 0.0
    ).astype(jnp.float32)
    summed = series_sum(identity_rows, scaled_refl, scaled_refl)
    numer = decays[:, None] * refl_full * decays[None, :] - refl_full
    reflect_block = product(summed, numer)
    scaled_sum = summed * decays[None, :]
    trans_block = scaled_sum - product(product(scaled_sum, refl_full), refl_full)
    blocks = (reflect_block, trans_block, trans_block, reflect_block)
    depth_count = lax.axis_size("layer").bit_length() - 1
    for depth_level in range(depth_count):
        partner_blocks = swapped((blocks[0], blocks[1], blocks[2], blocks[3]), "layer", depth_level)
        is_right = lax.axis_index("layer") // 2**depth_level % 2 == 1
        front_part = tuple((jnp.where(is_right, partner_blocks[i], blocks[i]) for i in range(4)))
        back_part = tuple((jnp.where(is_right, blocks[i], partner_blocks[i]) for i in range(4)))
        back_refl_full, front_refl_full, front_trans_full, back_trans_full = (
            lax.all_gather(back_part[0], "panel", axis=0, tiled=True),
            lax.all_gather(front_part[3], "panel", axis=0, tiled=True),
            lax.all_gather(front_part[2], "panel", axis=0, tiled=True),
            lax.all_gather(back_part[1], "panel", axis=0, tiled=True),
        )
        upper_chain = series_sum(front_part[1], back_refl_full, front_refl_full)
        lower_chain = series_sum(back_part[2], front_refl_full, back_refl_full)
        block_one = front_part[0] + product(product(upper_chain, back_refl_full), front_trans_full)
        block_two = product(upper_chain, back_trans_full)
        block_three = product(lower_chain, front_trans_full)
        block_four = back_part[3] + product(product(lower_chain, front_refl_full), back_trans_full)
        blocks = (block_one, block_two, block_three, block_four)
    stacked = jnp.stack(blocks)
    block_count = stacked.shape[0] // lax.axis_size("layer")
    return lax.dynamic_slice_in_dim(stacked, lax.axis_index("layer") * block_count, block_count, 0)


def solution(mesh):
    placed = (P(None, "panel", None), P(), P("layer"), P("layer"))
    return jax.shard_map(
        local, mesh=mesh, in_specs=placed, out_specs=P("layer", "panel", None), check_vma=False
    )
```

profile of v0, /device:TPU:1, one launch (start us, length us, event | category | flops | bytes accessed | tf_op | source)
XLA Modules:
  0.0 528.1 jit_solution(8382436333740291440)
XLA Ops:
  10.3 48.9 %all-gather.27.cloned.1.call-done = f32[1,1024,1024]{2,1,0:T(8,128)} async-done(((f32[1,32,1024]{2,1,0:T(8,128)}), f32[1,1024,1024]{2,1,0:T(8,128)}) %all-gather.27.cloned.1.call-update) | async-done | bytes 4194320 | tf_op jit(solution)/shard_map/all_gather | solution.py:43
  59.2 5.0 fusion.10
  64.3 2.7 fusion.34
  66.9 2.7 fusion.33
  69.6 2.7 fusion.32
  72.3 2.7 fusion.31
  75.0 2.9 fusion.30
  77.9 2.7 fusion.29
  80.6 2.7 fusion.28
  83.3 2.7 fusion.27
  85.9 2.7 convolution_add_fusion.2
  88.6 15.6 %fusion.4 = f32[32,1024]{1,0:T(8,128)S(1)} fusion(f32[32,1024]{1,0:T(8,128)S(1)} %convolution_add_fusion.2, f32[1,1024,1024]{2,1,0:T(8,128)S(1)} %copy-done, f32[1024]{0:T(1024)S(1)} %bitcast.161), kind=kOutput, calls=%fused_computation.6 | convolution fusion | flops 405798912 | bytes 4460544 | tf_op jit(solution)/shard_map/dot_general | solution.py:20
  105.6 3.6 collective-permute-done
  110.7 4.8 fusion.2
  115.5 2.5 fusion.7
  119.4 2.5 collective-permute-done.1
  123.3 32.9 %all-gather.11.cloned.1.call-done = f32[1024,1024]{1,0:T(8,128)} async-done(((f32[32,1024]{1,0:T(8,128)}), f32[1024,1024]{1,0:T(8,128)}) %all-gather.11.cloned.1.call-update) | async-done | bytes 4194320 | tf_op jit(solution)/shard_map/all_gather | solution.py:62
  156.2 4.7 fusion.35
  161.0 42.9 %all-gather.13.cloned.1.call-done = f32[1024,1024]{1,0:T(8,128)} async-done(((f32[32,1024]{1,0:T(8,128)}), f32[1024,1024]{1,0:T(8,128)}) %all-gather.13.cloned.1.call-update) | async-done | bytes 4194320 | tf_op jit(solution)/shard_map/all_gather | solution.py:63
  203.9 4.8 fusion.36
  213.7 2.5 fusion.39
  216.2 2.9 fusion.40
  219.1 2.5 fusion.41
  226.6 2.5 add_add_fusion.3
  231.6 19.9 %all-gather.15.cloned.1.call-done = f32[1024,1024]{1,0:T(8,128)} async-done(((f32[32,1024]{1,0:T(8,128)}), f32[1024,1024]{1,0:T(8,128)}) %all-gather.15.cloned.1.call-update) | async-done | bytes 4194320 | tf_op jit(solution)/shard_map/all_gather | solution.py:64
  251.5 4.8 convolution_add_fusion.1
  256.3 2.9 collective-permute-start.2
  259.3 3.5 collective-permute-done.2
  263.5 4.8 fusion.46
  273.4 2.5 fusion.49
  278.3 2.9 fusion.51
  281.2 2.5 fusion.52
  283.7 2.5 fusion.53
  288.7 2.5 add_add_fusion.2
  291.2 2.5 fusion.55
  293.7 5.3 all-gather.17.cloned.1.call-done
  299.0 4.8 convolution_add_fusion
  303.8 2.9 collective-permute-start.4
  306.8 3.5 collective-permute-done.4
  311.0 4.7 fusion.45
  315.7 2.9 collective-permute-start.3
  321.1 25.4 %all-gather.19.cloned.1.call-done = f32[1024,1024]{1,0:T(8,128)} async-done(((f32[32,1024]{1,0:T(8,128)}), f32[1024,1024]{1,0:T(8,128)}) %all-gather.19.cloned.1.call-update) | async-done | bytes 4194320 | tf_op jit(solution)/shard_map/all_gather | solution.py:62
  346.5 4.7 fusion.23
  351.1 43.0 %all-gather.21.cloned.1.call-done = f32[1024,1024]{1,0:T(8,128)} async-done(((f32[32,1024]{1,0:T(8,128)}), f32[1024,1024]{1,0:T(8,128)}) %all-gather.21.cloned.1.call-update) | async-done | bytes 4194320 | tf_op jit(solution)/shard_map/all_gather | solution.py:63
  394.1 4.8 fusion.56
  406.4 2.9 fusion.60
  409.3 2.5 fusion.61
  416.8 3.0 broadcast_select_fusion.5
  419.9 4.8 fusion.65
  424.8 3.1 collective-permute-start.5
  427.9 3.5 collective-permute-done.5
  431.4 4.7 fusion.24
  436.1 2.5 fusion.66
  441.1 2.5 fusion.68
  446.1 2.7 fusion.70
  451.2 2.5 fusion.72
  456.2 3.0 add_add_fusion
  459.3 5.0 fusion.64
  464.3 2.7 fusion.74
  467.1 4.8 convolution_bitcast_fusion.1
  471.9 2.5 add_bitcast_fusion
  474.4 38.6 %all-gather.23.cloned.1.call-done = f32[1024,1024]{1,0:T(8,128)} async-done(((f32[32,1024]{1,0:T(8,128)}), f32[1024,1024]{1,0:T(8,128)}) %all-gather.23.cloned.1.call-update) | async-done | bytes 4194320 | tf_op jit(solution)/shard_map/all_gather | solution.py:64
  513.0 4.8 convolution_bitcast_fusion
  517.9 2.5 add_bitcast_fusion.1
  (82 shorter events, 57.6 us)
Async XLA Ops:
  6.5 52.7 %all-gather.27.cloned.1.call-start = ((), (), s32[]{:S(2)}) async-start(), calls=%async_computation.8 | async-start | bytes 4325376 | tf_op jit(solution)/shard_map/all_gather | solution.py:43
  8.8 147.4 %all-gather.11.cloned.1.call-start = ((), (), s32[]{:S(2)}) async-start(), calls=%async_computation | async-start | bytes 4325376 | tf_op jit(solution)/shard_map/all_gather | solution.py:62
  59.2 5.0 copy-start
  104.2 4.9 collective-permute-start
  109.9 94.0 %all-gather.13.cloned.1.call-start = ((), (), s32[]{:S(2)}) async-start(), calls=%async_computation.1 | async-start | bytes 4325376 | tf_op jit(solution)/shard_map/all_gather | solution.py:63
  110.6 140.8 %all-gather.15.cloned.1.call-start = ((), (), s32[]{:S(2)}) async-start(), calls=%async_computation.2 | async-start | bytes 4325376 | tf_op jit(solution)/shard_map/all_gather | solution.py:64
  110.7 4.8 copy-start.1
  118.0 3.9 collective-permute-start.1
  122.7 176.3 %all-gather.17.cloned.1.call-start = ((), (), s32[]{:S(2)}) async-start(), calls=%async_computation.3 | async-start | bytes 4325376 | tf_op jit(solution)/shard_map/all_gather | solution.py:65
  123.3 223.2 %all-gather.19.cloned.1.call-start = ((), (), s32[]{:S(2)}) async-start(), calls=%async_computation.4 | async-start | bytes 4325376 | tf_op jit(solution)/shard_map/all_gather | solution.py:62
  203.9 4.8 copy-start.2
  203.9 7.3 %copy-start.4 = (f32[1024,1024]{1,0:T(8,128)S(1)}, f32[1024,1024]{1,0:T(8,128)}, u32[]{:S(2)}) copy-start(f32[1024,1024]{1,0:T(8,128)} %all-gather.13.cloned.1.call-done) | copy-start | bytes 12582916
  221.6 5.0 copy-start.14
  226.6 24.9 %copy-start.16 = (f32[32,1024]{1,0:T(8,128)S(1)}, f32[32,1024]{1,0:T(8,128)}, u32[]{:S(2)}) copy-start(f32[32,1024]{1,0:T(8,128)} %get-tuple-element.12) | copy-start | bytes 393220
  229.1 34.4 %copy-start.13 = (f32[32,1024]{1,0:T(8,128)S(1)}, f32[32,1024]{1,0:T(8,128)}, u32[]{:S(2)}) copy-start(f32[32,1024]{1,0:T(8,128)} %get-tuple-element.9) | copy-start | bytes 393220
  256.3 6.4 %collective-permute-start.2 = (f32[32,1024]{1,0:T(8,128)S(1)}, f32[32,1024]{1,0:T(8,128)S(1)}, u32[]{:S(2)}, u32[]{:S(2)}) collective-permute-start(f32[32,1024]{1,0:T(8,128)S(1)} %convolution_add_fusion.1), channel_id=1, source_target_pairs={{0,64},{64,0},{32,96},{96,32},{1,65},{65,1},{33,97},{97,33},{2,66}... | collective-permute-start | bytes 393224 | tf_op jit(solution)/shard_map/ppermute | solution.py:16
  263.4 130.7 %all-gather.21.cloned.1.call-start = ((), (), s32[]{:S(2)}) async-start(), calls=%async_computation.5 | async-start | bytes 4325376 | tf_op jit(solution)/shard_map/all_gather | solution.py:63
  263.5 4.8 copy-start.3
  263.5 7.3 %copy-start.5 = (f32[1024,1024]{1,0:T(8,128)S(1)}, f32[1024,1024]{1,0:T(8,128)}, u32[]{:S(2)}) copy-start(f32[1024,1024]{1,0:T(8,128)} %all-gather.13.cloned.1.call-done) | copy-start | bytes 12582916
  288.7 10.3 %copy-start.15 = (f32[32,1024]{1,0:T(8,128)S(1)}, f32[32,1024]{1,0:T(8,128)}, u32[]{:S(2)}) copy-start(f32[32,1024]{1,0:T(8,128)} %get-tuple-element.11) | copy-start | bytes 393220
  303.8 6.4 %collective-permute-start.4 = (f32[32,1024]{1,0:T(8,128)S(1)}, f32[32,1024]{1,0:T(8,128)S(1)}, u32[]{:S(2)}, u32[]{:S(2)}) collective-permute-start(f32[32,1024]{1,0:T(8,128)S(1)} %convolution_add_fusion), channel_id=1, source_target_pairs={{0,64},{64,0},{32,96},{96,32},{1,65},{65,1},{33,97},{97,33},{2,66}... | collective-permute-start | bytes 393224 | tf_op jit(solution)/shard_map/ppermute | solution.py:16
  310.9 156.2 %all-gather.25.cloned.1.call-start = ((), (), s32[]{:S(2)}) async-start(), calls=%async_computation.7 | async-start | bytes 4325376 | tf_op jit(solution)/shard_map/all_gather | solution.py:65
  315.7 5.4 %collective-permute-start.3 = (f32[32,1024]{1,0:T(8,128)S(1)}, f32[32,1024]{1,0:T(8,128)S(1)}, u32[]{:S(2)}, u32[]{:S(2)}) collective-permute-start(f32[32,1024]{1,0:T(8,128)S(1)} %fusion.45), channel_id=1, source_target_pairs={{0,64},{64,0},{32,96},{96,32},{1,65},{65,1},{33,97},{97,33},{2,66}... | collective-permute-start | bytes 393224 | tf_op jit(solution)/shard_map/ppermute | solution.py:16
  394.1 4.8 copy-start.6
  394.1 7.3 %copy-start.8 = (f32[1024,1024]{1,0:T(8,128)S(1)}, f32[1024,1024]{1,0:T(8,128)}, u32[]{:S(2)}) copy-start(f32[1024,1024]{1,0:T(8,128)} %all-gather.21.cloned.1.call-done) | copy-start | bytes 12582916
  419.9 93.2 %all-gather.23.cloned.1.call-start = ((), (), s32[]{:S(2)}) async-start(), calls=%async_computation.6 | async-start | bytes 4325376 | tf_op jit(solution)/shard_map/all_gather | solution.py:64
  419.9 16.1 %copy-start.7 = (f32[1024,1024]{1,0:T(8,128)S(1)}, f32[1024,1024]{1,0:T(8,128)}, u32[]{:S(2)}) copy-start(f32[1024,1024]{1,0:T(8,128)} %all-gather.19.cloned.1.call-done) | copy-start | bytes 12582916
  424.8 13.8 %copy-start.9 = (f32[1024,1024]{1,0:T(8,128)S(1)}, f32[1024,1024]{1,0:T(8,128)}, u32[]{:S(2)}) copy-start(f32[1024,1024]{1,0:T(8,128)} %all-gather.21.cloned.1.call-done) | copy-start | bytes 12582916
  424.8 6.6 %collective-permute-start.5 = (f32[32,1024]{1,0:T(8,128)S(1)}, f32[32,1024]{1,0:T(8,128)S(1)}, u32[]{:S(2)}, u32[]{:S(2)}) collective-permute-start(f32[32,1024]{1,0:T(8,128)S(1)} %fusion.65), channel_id=1, source_target_pairs={{0,64},{64,0},{32,96},{96,32},{1,65},{65,1},{33,97},{97,33},{2,66}... | collective-permute-start | bytes 393224 | tf_op jit(solution)/shard_map/ppermute | solution.py:16
  459.3 5.0 copy-start.10
  467.1 4.8 copy-start.11
  513.0 4.8 copy-start.12
Sparse Core Ops, SparseCore 0:
  9.6 49.5 all-gather.26
  110.0 46.1 all-gather.10
  158.5 45.3 all-gather.12
  206.0 45.4 all-gather.14
  253.6 45.3 all-gather.16
  301.1 45.3 all-gather.18
  348.7 45.3 all-gather.20
  420.0 45.3 all-gather.24
  467.7 45.3 all-gather.22
where the time goes:
time: 537 us; the launch traced here: 528 us
  waiting for transfers between devices  277 us (52%)
  matrix products  214 us (40%)
  between operations  15.5 us (3%)
  starting transfers between devices  15 us (3%)
    dot_general x65, matrix products, product(): jnp.dot(left_side, right_side, precision=lax.Precision.HIGHEST, preferred...  214 us
    all_gather x2, waiting for transfers between devices, local(): lax.all_gather(front_part[3], 'panel', axis=0, tiled=True)  85.9 us
    all_gather x2, waiting for transfers between devices, local(): lax.all_gather(front_part[2], 'panel', axis=0, tiled=True)  58.4 us
    all_gather x2, waiting for transfers between devices, local(): lax.all_gather(back_part[0], 'panel', axis=0, tiled=True)  58.3 us
    all_gather x1, waiting for transfers between devices, local(): refl_full = lax.all_gather(refl_rows, 'panel', axis=0, tiled=True)  48.9 us
    ppermute x6, waiting for transfers between devices, swapped(): return lax.ppermute(block, axis, route)  19 us
    ppermute x6, starting transfers between devices, swapped(): return lax.ppermute(block, axis, route)  14.7 us
  transfers between devices with their start and end apart: 15, of which 14 were waited for; matrix products, arithmetic and copies ran while one was open for 26% of the time, Pallas kernels for 0%

commit v1 on v0

v1 whole, which is shorter than its diff:
```python
import jax
import jax.numpy as jnp
from jax import lax
from jax.experimental import pallas as pl
from jax.experimental.pallas import tpu as pltpu
from jax.sharding import PartitionSpec as P

TERMS = 6
CHUNKS = 8
VMEM_BYTES = 56 * 1024 * 1024


def halves(value):
    high = value.astype(jnp.bfloat16)
    low = (value - high.astype(jnp.float32)).astype(jnp.bfloat16)
    return high, low


def product(rows, high_ref, low_ref):
    count = rows.shape[0]
    high, low = halves(rows)
    both = jnp.concatenate([high, low], axis=0)
    by_high = jnp.dot(both, high_ref[...], preferred_element_type=jnp.float32)
    by_low = jnp.dot(high, low_ref[...], preferred_element_type=jnp.float32)
    return by_high[:count] + (by_high[count:] + by_low)


def fetch(source, slot, stage, sems):
    per_chunk = source.shape[0] // CHUNKS
    for c in range(CHUNKS):
        part = pl.ds(c * per_chunk, per_chunk)
        pltpu.make_async_copy(source.at[part, slot], stage.at[part], sems.at[c]).start()


def split(source, slot, stage, sems, high_ref, low_ref):
    panels, panel_rows, order = stage.shape
    per_chunk = panels // CHUNKS
    chunk_rows = per_chunk * panel_rows

    def body(c, carry):
        part = pl.ds(c * per_chunk, per_chunk)
        pltpu.make_async_copy(source.at[part, slot], stage.at[part], sems.at[c]).wait()
        high, low = halves(stage[part].reshape(chunk_rows, order))
        rows = pl.ds(pl.multiple_of(c * chunk_rows, chunk_rows), chunk_rows)
        high_ref[rows, :] = high
        low_ref[rows, :] = low
        return carry

    lax.fori_loop(0, CHUNKS, body, 0)


def layer_kernel(full, own, decay_row, decay_col, eye, refl_out, trans_out, stage, high, low, sems):
    fetch(full, 0, stage, sems)
    split(full, 0, stage, sems, high, low)
    decays = decay_row[...]
    term = product(decay_col[...] * own[...] * decays, high, low)

    def body(k, carry):
        term, summed = carry
        term = product(term * decays, high, low)
        term = product(term * decays, high, low)
        return term, summed + term

    _, summed = lax.fori_loop(0, TERMS - 2, body, (term, eye[...] + term))
    count = summed.shape[0]
    scaled = summed * decays
    both = product(jnp.concatenate([scaled, summed], axis=0), high, low)
    refl_out[...] = both[:count] * decays - both[count:]
    trans_out[...] = scaled - product(both[:count], high, low)


def pair_kernel(full, start_own, start_oth, own_refl, refl_out, trans_out, stage, high, low, sems):
    for slot in (1, 0, 2):
        fetch(full, slot, stage.at[slot], sems.at[slot])
    split(full, 1, stage.at[1], sems.at[1], high.at[1], low.at[1])
    split(full, 0, stage.at[0], sems.at[0], high.at[0], low.at[0])
    split(full, 2, stage.at[2], sems.at[2], high.at[2], low.at[2])
    count = start_own.shape[0]
    first = product(start_own[...], high.at[1], low.at[1])
    both = jnp.concatenate([first, start_oth[...]], axis=0)

    def body(k, carry):
        both, summed = carry
        both = product(both, high.at[0], low.at[0])
        both = product(both, high.at[1], low.at[1])
        return both, summed + both

    _, summed = lax.fori_loop(0, TERMS - 1, body, (both, both))
    done = product(summed, high.at[2], low.at[2])
    refl_out[...] = own_refl[...] + done[:count]
    trans_out[...] = done[count:]


def last_kernel(full, start, base, weights, out, stage, high, low, sems):
    for slot in (0, 1, 2):
        fetch(full, slot, stage.at[slot], sems.at[slot])
    for slot in (0, 1, 2):
        split(full, slot, stage.at[slot], sems.at[slot], high.at[slot], low.at[slot])
    term = start[...]
    half = product(term, high.at[0], low.at[0])

    def body(k, carry):
        half, term_sum, half_sum = carry
        term = product(half, high.at[1], low.at[1])
        half = product(term, high.at[0], low.at[0])
        return half, term_sum + term, half_sum + half

    _, term_sum, half_sum = lax.fori_loop(0, TERMS - 1, body, (half, term, half))
    chosen = jnp.where(weights[...] > 0.0, half_sum, term_sum)
    out[...] = base[...] + product(chosen, high.at[2], low.at[2])


def call(kernel, slots, outs, panels, panel_rows, order, full, *small):
    lead = (slots,) if slots > 1 else ()
    rows = jax.ShapeDtypeStruct((panel_rows, order), jnp.float32)
    return pl.pallas_call(
        kernel,
        out_shape=(rows,) * outs if outs > 1 else rows,
        in_specs=[pl.BlockSpec(memory_space=pl.ANY)]
        + [pl.BlockSpec(memory_space=pltpu.VMEM)] * len(small),
        out_specs=(pl.BlockSpec(memory_space=pltpu.VMEM),) * outs
        if outs > 1
        else pl.BlockSpec(memory_space=pltpu.VMEM),
        scratch_shapes=[
            pltpu.VMEM(lead + (panels, panel_rows, order), jnp.float32),
            pltpu.VMEM(lead + (order, order), jnp.bfloat16),
            pltpu.VMEM(lead + (order, order), jnp.bfloat16),
            pltpu.SemaphoreType.DMA(lead + (CHUNKS,)),
        ],
        compiler_params=pltpu.CompilerParams(vmem_limit_bytes=VMEM_BYTES),
    )(full, *small)


def gathered(*rows):
    return lax.all_gather(jnp.stack(rows), "panel", axis=0, tiled=False)


def local(reflections, wave_decay, thickness, material):
    panel_rows = reflections.shape[1]
    order = reflections.shape[2]
    panels = order // panel_rows
    sizes = (panels, panel_rows, order)
    row_start = lax.axis_index("panel") * panel_rows
    layer = lax.axis_index("layer")
    chosen = material[0]
    refl_rows = lax.dynamic_index_in_dim(reflections, chosen, 0, keepdims=False)
    decays = jnp.exp(
        -lax.dynamic_index_in_dim(wave_decay, chosen, 0, keepdims=False) * thickness[0]
    )
    own_decays = lax.dynamic_slice_in_dim(decays, row_start, panel_rows)
    row_ids = row_start + jnp.arange(panel_rows, dtype=jnp.int32)
    eye = jnp.where(
        row_ids[:, None] == jnp.arange(order, dtype=jnp.int32)[None, :], 1.0, 0.0
    ).astype(jnp.float32)
    refl, trans = call(
        layer_kernel, 1, 2, *sizes, gathered(refl_rows), refl_rows, decays[None, :], own_decays[:, None], eye
    )
    oth = lax.ppermute(jnp.stack([refl, trans]), "layer", [(0, 1), (1, 0), (2, 3), (3, 2)])
    refl, trans = call(
        pair_kernel, 3, 2, *sizes, gathered(refl, oth[0], trans), trans, oth[1], refl
    )
    inner = (layer == 1) | (layer == 2)
    near = lax.ppermute(jnp.stack([refl, trans]), "layer", [(1, 0), (2, 3)])
    cross = lax.ppermute(refl, "layer", [(1, 2), (2, 1)])
    far = lax.ppermute(jnp.where(inner, refl, trans), "layer", [(0, 2), (2, 0), (1, 3), (3, 1)])
    first = jnp.where(inner, cross, far)
    second = jnp.where(inner, refl, near[0])
    closing = jnp.where(inner, far, trans)
    start = jnp.where(inner, trans, near[1])
    base = jnp.where(inner, 0.0, refl)
    pick = jnp.full((1, order), jnp.where(inner, 0.0, 1.0), jnp.float32)
    out = call(last_kernel, 3, 1, *sizes, gathered(first, second, closing), start, base, pick)
    return out[None]


def solution(mesh):
    placed = (P(None, "panel", None), P(), P("layer"), P("layer"))
    return jax.shard_map(
        local, mesh=mesh, in_specs=placed, out_specs=P("layer", "panel", None), check_vma=False
    )
```

time: 537 us -> 269 us (0.50); the launches traced: 528 us -> 269 us
  matrix products: 214 us -> 0 us
  waiting for transfers between devices: 277 us -> 191 us
  Pallas kernels: 0 us -> 44.1 us
  starting transfers between devices: 15 us -> 5.1 us
    dot_general x65 -> x0, matrix products: 214 us -> none  [product(): jnp.dot(left_side, right_side, precision=lax.Precision.HIGHEST, preferred...]
    all_gather x9 -> x3, waiting for transfers between devices: 257 us -> 173 us  [gathered(): return lax.all_gather(jnp.stack(rows), 'panel', axis=0, tiled=False)]
    pallas_call x0 -> x3, Pallas kernels: none -> 44.1 us  [call(): pl.pallas_call(kernel, out_shape=(rows,) * outs if outs > 1 else rows, in...]
    ppermute x6 -> x4, starting transfers between devices: 14.7 us -> 5.01 us  [the longest x1 1.7 us: local(): lax.ppermute(jnp.where(inner, refl, trans), 'layer', [(0, 2), (2, 0), (1,...]
    ppermute x6 -> x4, waiting for transfers between devices: 19 us -> 17.6 us  [the longest x1 7.54 us: local(): near = lax.ppermute(jnp.stack([refl, trans]), 'layer', [(1, 0), (2, 3)])]
  transfers between devices with their start and end apart: 15 -> 7, of which waited for: 14 -> 6; matrix products, arithmetic and copies ran while one was open for 26% -> 2% of each run, Pallas kernels for 0% -> 0%
where the time goes in v1:
time: 269 us
  waiting for transfers between devices  191 us (71%)
  Pallas kernels  44.1 us (16%)
  between operations  14.5 us (5%)
  other arithmetic  8.71 us (3%)
  local copies, waits for them, and re-layouts  5.21 us (2%)
  starting transfers between devices  5.1 us (2%)
    all_gather x3, waiting for transfers between devices, gathered(): return lax.all_gather(jnp.stack(rows), 'panel', axis=0, tiled=False)  173 us
    pallas_call x3, Pallas kernels, call(): pl.pallas_call(kernel, out_shape=(rows,) * outs if outs > 1 else rows, in...  44.1 us
    ppermute x1, waiting for transfers between devices, local(): near = lax.ppermute(jnp.stack([refl, trans]), 'layer', [(1, 0), (2, 3)])  7.54 us
    ppermute x1, waiting for transfers between devices, local(): lax.ppermute(jnp.stack([refl, trans]), 'layer', [(0, 1), (1, 0), (2, 3),...  6.39 us
  transfers between devices with their start and end apart: 7, of which 6 were waited for; matrix products, arithmetic and copies ran while one was open for 2% of the time, Pallas kernels for 0%

profile of v1, /device:TPU:1, one launch (start us, length us, event | category | flops | bytes accessed | tf_op | source)
XLA Modules:
  0.0 268.5 jit_solution(16434253599075470278)
XLA Ops:
  6.5 0.0 all-gather.7.cloned.1.call-start
  7.2 1.6 constant_dynamic-slice_fusion.1
  8.8 0.0 all-gather.7.cloned.1.call-update
  8.8 0.0 all-gather.9.cloned.1.call-start
  9.5 0.8 multiply_exponential_fusion.decay_row
  10.3 0.0 copy-start
  10.3 0.1 fusion.4
  10.4 0.7 copy.6.decay_col
  11.1 1.6 fusion.5.own
  12.6 0.7 fusion.3.eye
  13.4 45.8 %all-gather.7.cloned.1.call-done = f32[32,32,1024]{2,1,0:T(8,128)} async-done(((f32[1,32,1024]{2,1,0:T(8,128)}), f32[32,32,1024]{2,1,0:T(8,128)}) %all-gather.7.cloned.1.call-update) | async-done | bytes 4194320 | tf_op jit(solution)/shard_map/all_gather | solution.py:135
  59.2 0.0 copy-done
  59.2 12.6 %shard_map.46 = (f32[32,1024]{1,0:T(8,128)}, f32[32,1024]{1,0:T(8,128)}) custom-call(f32[32,1,32,1024]{3,2,1,0:T(8,128)} %bitcast.38, f32[32,1024]{1,0:T(8,128)} %fusion.5.own, f32[1,1024]{1,0:T(1,128)} %copy-done, f32[32,1]{1,0:T(8,128)} %copy.6.decay_col, f32[32,1024]{1,0:T(8,128)} %fusion.3.eye), custom_call_target="tpu_custom_call" | custom-call | tf_op jit(solution)/shard_map/pallas_call | solution.py:116
  71.8 1.0 pad_maximum_fusion.2
  72.8 1.4 collective-permute-start
  74.1 6.4 %collective-permute-done = f32[2,32,1024]{2,1,0:T(8,128)S(1)} collective-permute-done((f32[2,32,1024]{2,1,0:T(8,128)S(1)}, f32[2,32,1024]{2,1,0:T(8,128)S(1)}, u32[]{:S(2)}, u32[]{:S(2)}) %collective-permute-start) | collective-permute-done | bytes 262176 | tf_op jit(solution)/shard_map/ppermute | solution.py:158
  80.5 0.7 slice_bitcast_fusion.2
  81.2 1.8 pad_maximum_fusion
  83.0 0.0 all-gather.9.cloned.1.call-update
  83.0 0.0 all-gather.11.cloned.1.call-start
  83.0 63.1 %all-gather.9.cloned.1.call-done = f32[96,32,1024]{2,1,0:T(8,128)} async-done(((f32[3,32,1024]{2,1,0:T(8,128)}), f32[96,32,1024]{2,1,0:T(8,128)}) %all-gather.9.cloned.1.call-update) | async-done | bytes 12582928 | tf_op jit(solution)/shard_map/all_gather | solution.py:135
  146.2 15.5 %shard_map.47 = (f32[32,1024]{1,0:T(8,128)}, f32[32,1024]{1,0:T(8,128)}) custom-call(f32[32,3,32,1024]{3,2,1,0:T(8,128)} %bitcast.37, f32[32,1024]{1,0:T(8,128)} %get-tuple-element.10.start_own, f32[32,1024]{1,0:T(8,128)} %get-tuple-element.16.start_oth, f32[32,1024]{1,0:T(8,128)} %get-tuple-element.9.own_refl), custom_call_target="tpu_custom_call" | custom-call | tf_op jit(solution)/shard_map/pallas_call | solution.py:116
  161.7 1.0 pad_maximum_fusion.3
  162.7 1.3 collective-permute-start.3
  164.0 0.7 collective-permute-start.1
  164.7 7.5 %collective-permute-done.3 = f32[2,32,1024]{2,1,0:T(8,128)S(1)} collective-permute-done((f32[2,32,1024]{2,1,0:T(8,128)S(1)}, f32[2,32,1024]{2,1,0:T(8,128)S(1)}, u32[]{:S(2)}, u32[]{:S(2)}) %collective-permute-start.3) | collective-permute-done | bytes 262176 | tf_op jit(solution)/shard_map/ppermute | solution.py:163
  172.2 1.7 fusion
  173.9 1.7 collective-permute-start.2
  175.6 0.0 collective-permute-done.1
  175.6 3.6 %collective-permute-done.2 = f32[32,1024]{1,0:T(8,128)S(1)} collective-permute-done((f32[32,1024]{1,0:T(8,128)S(1)}, f32[32,1024]{1,0:T(8,128)S(1)}, u32[]{:S(2)}, u32[]{:S(2)}) %collective-permute-start.2) | collective-permute-done | bytes 131104 | tf_op jit(solution)/shard_map/ppermute | solution.py:165
  179.3 0.9 select_bitcast_fusion.1
  180.2 0.8 pad_maximum_fusion.1
  181.0 0.0 all-gather.11.cloned.1.call-update
  181.0 64.3 %all-gather.11.cloned.1.call-done = f32[96,32,1024]{2,1,0:T(8,128)} async-done(((f32[3,32,1024]{2,1,0:T(8,128)}), f32[96,32,1024]{2,1,0:T(8,128)}) %all-gather.11.cloned.1.call-update) | async-done | bytes 12582928 | tf_op jit(solution)/shard_map/all_gather | solution.py:135
  245.3 0.6 broadcast_in_dim.25.weights
  245.9 16.0 %shard_map.48 = f32[32,1024]{1,0:T(8,128)} custom-call(f32[32,3,32,1024]{3,2,1,0:T(8,128)} %bitcast.36, f32[32,1024]{1,0:T(8,128)} %get-tuple-element.13.start, f32[32,1024]{1,0:T(8,128)} %get-tuple-element.18.base, f32[1,1024]{1,0:T(1,128)} %broadcast_in_dim.25.weights), custom_call_target="tpu_custom_call" | custom-call | tf_op jit(solution)/shard_map/pallas_call | solution.py:116
  (1 shorter events, 0.0 us)
Async XLA Ops:
  6.5 52.7 %all-gather.7.cloned.1.call-start = ((), (), s32[]{:S(2)}) async-start(), calls=%async_computation | async-start | bytes 4325376 | tf_op jit(solution)/shard_map/all_gather | solution.py:135
  8.8 137.4 %all-gather.9.cloned.1.call-start = ((), (), s32[]{:S(2)}) async-start(), calls=%async_computation.1 | async-start | bytes 12976128 | tf_op jit(solution)/shard_map/all_gather | solution.py:135
  10.3 48.9 %copy-start = (f32[1,1024]{1,0:T(1,128)}, f32[1,1024]{1,0:T(1,128)S(1)}, u32[]{:S(2)}) copy-start(f32[1,1024]{1,0:T(1,128)S(1)} %multiply_exponential_fusion.decay_row) | copy-start | bytes 12292
  72.8 7.7 %collective-permute-start = (f32[2,32,1024]{2,1,0:T(8,128)S(1)}, f32[2,32,1024]{2,1,0:T(8,128)S(1)}, u32[]{:S(2)}, u32[]{:S(2)}) collective-permute-start(f32[2,32,1024]{2,1,0:T(8,128)S(1)} %pad_maximum_fusion.2), channel_id=1, source_target_pairs={{0,32},{32,0},{64,96},{96,64},{1,33},{33,1},{65,97},{97,65},{2,34}... | collective-permute-start | bytes 786440 | tf_op jit(solution)/shard_map/ppermute | solution.py:158
  83.0 162.3 %all-gather.11.cloned.1.call-start = ((), (), s32[]{:S(2)}) async-start(), calls=%async_computation.2 | async-start | bytes 12976128 | tf_op jit(solution)/shard_map/all_gather | solution.py:135
  162.7 9.5 %collective-permute-start.3 = (f32[2,32,1024]{2,1,0:T(8,128)S(1)}, f32[2,32,1024]{2,1,0:T(8,128)S(1)}, u32[]{:S(2)}, u32[]{:S(2)}) collective-permute-start(f32[2,32,1024]{2,1,0:T(8,128)S(1)} %pad_maximum_fusion.3), channel_id=1, source_target_pairs={{32,0},{64,96},{33,1},{65,97},{34,2},{66,98},{35,3},{67,99},{36,4}... | collective-permute-start | bytes 786440 | tf_op jit(solution)/shard_map/ppermute | solution.py:163
  164.0 11.6 %collective-permute-start.1 = (f32[32,1024]{1,0:T(8,128)}, f32[32,1024]{1,0:T(8,128)S(1)}, u32[]{:S(2)}, u32[]{:S(2)}) collective-permute-start(f32[32,1024]{1,0:T(8,128)} %get-tuple-element.11), channel_id=1, source_target_pairs={{32,64},{64,32},{33,65},{65,33},{34,66},{66,34},{35,67},{67,35},{3... | collective-permute-start | bytes 393224 | tf_op jit(solution)/shard_map/ppermute | solution.py:164
  173.9 5.3 %collective-permute-start.2 = (f32[32,1024]{1,0:T(8,128)S(1)}, f32[32,1024]{1,0:T(8,128)S(1)}, u32[]{:S(2)}, u32[]{:S(2)}) collective-permute-start(f32[32,1024]{1,0:T(8,128)S(1)} %get-tuple-element.15), channel_id=1, source_target_pairs={{0,64},{64,0},{32,96},{96,32},{1,65},{65,1},{33,97},{97,33},{2,66}... | collective-permute-start | bytes 393224 | tf_op jit(solution)/shard_map/ppermute | solution.py:165
Sparse Core Ops, SparseCore 0:
  9.6 49.5 all-gather.6
  83.1 62.9 all-gather.8
  181.1 64.1 all-gather.10

commit v2 on v0

v2 whole, which is shorter than its diff:
```python
import jax
import jax.numpy as jnp
from jax import lax
from jax.experimental import pallas as pl
from jax.experimental.pallas import tpu as pltpu
from jax.sharding import PartitionSpec as P

TERMS = 6
SIDE = 4
STEPS = (1, 3, 2)
PIECES = 2 * SIDE
MATRIX_BYTES = 4 * 1024 * 1024


def halves(value):
    high = value.astype(jnp.bfloat16)
    low = (value - high.astype(jnp.float32)).astype(jnp.bfloat16)
    return high, low


def product(rows, high_ref, low_ref):
    count = rows.shape[0]
    high, low = halves(rows)
    both = jnp.concatenate([high, low], axis=0)
    by_high = jnp.dot(both, high_ref[...], preferred_element_type=jnp.float32)
    by_low = jnp.dot(high, low_ref[...], preferred_element_type=jnp.float32)
    return by_high[:count] + (by_high[count:] + by_low)


def split(pieces, places, high_ref, low_ref):
    lines, slots, panel_rows, _ = pieces[0].shape
    for i, piece in enumerate(pieces):

        def body(j, carry, i=i, piece=piece):
            rows = pl.ds(pl.multiple_of(places[i * lines + j] * panel_rows, panel_rows), panel_rows)
            for slot in range(slots):
                high, low = halves(piece[j, slot])
                high_ref[slot, rows, :] = high
                low_ref[slot, rows, :] = low
            return carry

        lax.fori_loop(0, lines, body, 0)


def layer_kernel(*refs):
    pieces, refs = refs[:PIECES], refs[PIECES:]
    places, facts, thickness, own, wave_decay, refl_out, trans_out, high, low = refs
    split(pieces, places, high, low)
    rows, order = own.shape
    decays = jnp.exp(-wave_decay[pl.ds(facts[1], 1), :] * thickness[0])
    row_ids = facts[0] + lax.broadcasted_iota(jnp.int32, (rows, order), 0)
    eye = row_ids == lax.broadcasted_iota(jnp.int32, (rows, order), 1)
    own_decays = jnp.sum(jnp.where(eye, decays, 0.0), axis=1, keepdims=True)
    term = product(own_decays * own[...] * decays, high.at[0], low.at[0])

    def body(k, carry):
        term, summed = carry
        term = product(term * decays, high.at[0], low.at[0])
        term = product(term * decays, high.at[0], low.at[0])
        return term, summed + term

    _, summed = lax.fori_loop(0, TERMS - 2, body, (term, jnp.where(eye, 1.0, 0.0) + term))
    scaled = summed * decays
    both = product(jnp.concatenate([scaled, summed], axis=0), high.at[0], low.at[0])
    refl_out[...] = both[:rows] * decays - both[rows:]
    trans_out[...] = scaled - product(both[:rows], high.at[0], low.at[0])


def pair_chain(*refs):
    pieces, refs = refs[:PIECES], refs[PIECES:]
    places, start_own, start_oth, out, high, low = refs
    split(pieces, places, high, low)
    first = product(start_own[...], high.at[1], low.at[1])
    both = jnp.concatenate([first, start_oth[...]], axis=0)

    def body(k, carry):
        both, summed = carry
        both = product(both, high.at[0], low.at[0])
        both = product(both, high.at[1], low.at[1])
        return both, summed + both

    _, out[...] = lax.fori_loop(0, TERMS - 1, body, (both, both))


def pair_close(*refs):
    pieces, refs = refs[:PIECES], refs[PIECES:]
    places, inner, summed, own_refl, refl_out, trans_out, far_out, high, low = refs
    split(pieces, places, high, low)
    rows = own_refl.shape[0]
    done = product(summed[...], high.at[0], low.at[0])
    refl, trans = own_refl[...] + done[:rows], done[rows:]
    refl_out[...] = refl
    trans_out[...] = trans
    far_out[...] = jnp.where(inner[0] == 1, refl, trans)


def last_chain(*refs):
    pieces, refs = refs[:PIECES], refs[PIECES:]
    places, inner, start, out, high, low = refs
    split(pieces, places, high, low)
    first, second = 1 - inner[0], inner[0]
    term = start[...]
    half = product(term, high.at[first], low.at[first])

    def body(k, carry):
        half, term_sum, half_sum = carry
        term = product(half, high.at[second], low.at[second])
        half = product(term, high.at[first], low.at[first])
        return half, term_sum + term, half_sum + half

    _, term_sum, half_sum = lax.fori_loop(0, TERMS - 1, body, (half, term, half))
    out[...] = jnp.where(inner[0] == 1, term_sum, half_sum)


def last_close(*refs):
    pieces, refs = refs[:PIECES], refs[PIECES:]
    places, inner, summed, own_refl, out, high, low = refs
    split(pieces, places, high, low)
    base = jnp.where(inner[0] == 1, 0.0, own_refl[...])
    out[...] = base + product(summed[...], high.at[0], low.at[0])


def call(kernel, steps, outs, pieces, tables, small, placed=True):
    lines, slots, _, order = pieces[0].shape
    vmem = pl.BlockSpec(memory_space=pltpu.VMEM)
    here = [pltpu.with_memory_space_constraint(a, pltpu.VMEM) for a in (*pieces, *small)]
    out_shape = tuple(
        pltpu.VMEM(shape, jnp.float32) if placed else jax.ShapeDtypeStruct(shape, jnp.float32) for shape in outs
    )
    return pl.pallas_call(
        kernel,
        out_shape=out_shape,
        in_specs=[vmem] * len(pieces) + [pl.BlockSpec(memory_space=pltpu.SMEM)] * len(tables) + [vmem] * len(small),
        out_specs=(vmem,) * len(outs),
        scratch_shapes=[pltpu.VMEM((slots, order, order), jnp.bfloat16)] * 2,
        cost_estimate=pl.CostEstimate(
            flops=steps * 6 * 64 * order * order, transcendentals=0, bytes_accessed=steps * MATRIX_BYTES
        ),
        compiler_params=pltpu.CompilerParams(vmem_limit_bytes=(slots + 3) * MATRIX_BYTES),
    )(*here[: len(pieces)], *tables, *here[len(pieces) :])


def panel_of(x, y, core):
    return (x % SIDE * SIDE + y % SIDE) * 2 + core


def moved(block, phase, step):
    route = []
    for x in range(SIDE):
        for y in range(SIDE):
            for core in range(2):
                along_x = core == phase
                target = panel_of(x + step, y, core) if along_x else panel_of(x, y + step, core)
                route.append((panel_of(x, y, core), target))
    return lax.ppermute(block, "panel", route)


def line_of(rows):
    return [rows] + [moved(rows, 0, step) for step in STEPS]


def spread(line):
    return [line] + [moved(line, 1, step) for step in STEPS]


def flipped(pieces):
    flip = [(i, i ^ 1) for i in range(2 * SIDE * SIDE)]
    return pieces + [lax.ppermute(piece, "panel", flip) for piece in pieces]


def places_of(panel):
    x, y, core = panel // (2 * SIDE), panel // 2 % SIDE, panel % 2
    back = jnp.array((0,) + STEPS, jnp.int32)
    found = []
    for owner in (core, 1 - core):
        outer, inner = back[:, None], back[None, :]
        along_x = panel_of(x - inner + SIDE, y - outer + SIDE, 0)
        along_y = panel_of(x - outer + SIDE, y - inner + SIDE, 1)
        found.append(jnp.where(owner == 0, along_x, along_y).reshape(-1))
    return jnp.concatenate(found)


def gather_two_and_one(rows):
    line = line_of(rows)
    mine = spread(jnp.stack([block[:2] for block in line]))
    rest = jnp.stack([block[2:] for block in line])
    rest, *_ = lax.optimization_barrier((rest, *mine[1:]))
    return flipped(mine), spread(rest)


def after(pieces, value):
    *pieces, value = lax.optimization_barrier((*pieces, value))
    return flipped(pieces), value


def local(reflections, wave_decay, thickness, material):
    panel_rows = reflections.shape[1]
    order = reflections.shape[2]
    rows = (panel_rows, order)
    panel = lax.axis_index("panel")
    layer = lax.axis_index("layer")
    places = places_of(panel)
    inner = (layer == 1) | (layer == 2)
    inner_flag = inner.astype(jnp.int32)[None]
    facts = jnp.stack([panel * panel_rows, material[0]])
    own = lax.dynamic_index_in_dim(reflections, material[0], 0, keepdims=False)
    refl, trans = call(
        layer_kernel, 2 * TERMS, (rows, rows), flipped(spread(jnp.stack(line_of(own[None])))),
        (places, facts, thickness), (own, wave_decay),
    )
    pairs = [(0, 1), (1, 0), (2, 3), (3, 2)]
    oth_refl = lax.ppermute(refl, "layer", pairs)
    oth_trans = lax.ppermute(trans, "layer", pairs)
    pieces, closing = gather_two_and_one(jnp.stack([refl, oth_refl, trans]))
    (summed,) = call(pair_chain, 2 * TERMS, ((2 * panel_rows, order),), pieces, (places,), (trans, oth_trans))
    closing, summed = after(closing, summed)
    refl, trans, away = call(
        pair_close, 2, (rows, rows, rows), closing, (places, inner_flag), (summed, refl)
    )
    near = lax.ppermute(refl, "layer", [(1, 0), (2, 3)])
    cross = lax.ppermute(refl, "layer", [(1, 2), (2, 1)])
    far = lax.ppermute(away, "layer", [(0, 2), (2, 0), (1, 3), (3, 1)])
    near_trans = lax.ppermute(trans, "layer", [(1, 0), (2, 3)])
    pieces, closing = gather_two_and_one(
        jnp.stack(
            [jnp.where(inner, cross, near), jnp.where(inner, refl, far), jnp.where(inner, far, trans)]
        )
    )
    start = jnp.where(inner, trans, near_trans)
    (summed,) = call(last_chain, 2 * TERMS, (rows,), pieces, (places, inner_flag), (start,))
    closing, summed = after(closing, summed)
    (out,) = call(last_close, 2, (rows,), closing, (places, inner_flag), (summed, refl), placed=False)
    return out[None]


def solution(mesh):
    placed = (P(None, "panel", None), P(), P("layer"), P("layer"))
    return jax.shard_map(
        local, mesh=mesh, in_specs=placed, out_specs=P("layer", "panel", None), check_vma=False
    )
```

time: 537 us -> 203 us (0.38); the launches traced: 528 us -> 203 us
  matrix products: 214 us -> 0 us
  waiting for transfers between devices: 277 us -> 92.1 us
  starting transfers between devices: 15 us -> 67.8 us
  Pallas kernels: 0 us -> 36.1 us
  between operations: 15.5 us -> 1.62 us
    all_gather x9 -> x0, waiting for transfers between devices: 257 us -> none  [the longest x2 85.9 us: local(): lax.all_gather(front_part[3], 'panel', axis=0, tiled=True)]
    dot_general x65 -> x0, matrix products: 214 us -> none  [product(): jnp.dot(left_side, right_side, precision=lax.Precision.HIGHEST, preferred...]
    ppermute x6 -> x50, waiting for transfers between devices: 19 us -> 92.1 us  [the longest x24 71.7 us: moved(): return lax.ppermute(block, 'panel', route)]
    ppermute x6 -> x50, starting transfers between devices: 14.7 us -> 67.8 us  [the longest x24 28.5 us: moved(): return lax.ppermute(block, 'panel', route)]
    pallas_call x0 -> x5, Pallas kernels: none -> 36.1 us  [call(): pl.pallas_call(kernel, out_shape=out_shape, in_specs=[vmem] * len(pieces)...]
  transfers between devices with their start and end apart: 15 -> 50, of which waited for: 14 -> 28; matrix products, arithmetic and copies ran while one was open for 26% -> 2% of each run, Pallas kernels for 0% -> 10%
where the time goes in v2:
time: 203 us
  waiting for transfers between devices  92.1 us (45%)
  starting transfers between devices  67.8 us (33%)
  Pallas kernels  36.1 us (18%)
  local copies, waits for them, and re-layouts  3.98 us (2%)
    ppermute x24, waiting for transfers between devices, moved(): return lax.ppermute(block, 'panel', route)  71.7 us
    pallas_call x5, Pallas kernels, call(): pl.pallas_call(kernel, out_shape=out_shape, in_specs=[vmem] * len(pieces)...  36.1 us
    ppermute x24, starting transfers between devices, moved(): return lax.ppermute(block, 'panel', route)  28.5 us
    ppermute x20, starting transfers between devices, flipped(): return pieces + [lax.ppermute(piece, 'panel', flip) for piece in pieces]  27.4 us
    ppermute x20, waiting for transfers between devices, flipped(): return pieces + [lax.ppermute(piece, 'panel', flip) for piece in pieces]  6.7 us
    ppermute x1, starting transfers between devices, local(): far = lax.ppermute(away, 'layer', [(0, 2), (2, 0), (1, 3), (3, 1)])  5.47 us
  transfers between devices with their start and end apart: 50, of which 28 were waited for; matrix products, arithmetic and copies ran while one was open for 2% of the time, Pallas kernels for 10%

profile of v2, /device:TPU:1, one launch (start us, length us, event | category | flops | bytes accessed | tf_op | source)
XLA Modules:
  0.0 202.9 jit_solution(9396930232707812111)
XLA Ops:
  0.7 0.9 constant_dynamic-slice_fusion
  1.6 2.2 %collective-permute-start = (f32[1,32,1024]{2,1,0:T(8,128)S(1)}, f32[1,32,1024]{2,1,0:T(8,128)S(1)}, u32[]{:S(2)}, u32[]{:S(2)}) collective-permute-start(f32[1,32,1024]{2,1,0:T(8,128)S(1)} %constant_dynamic-slice_fusion), channel_id=1, source_target_pairs={{0,8},{1,3},{2,10},{3,5},{4,12},{5,7},{6,14},{7,1},{8,16},{9,11},{... | collective-permute-start | bytes 393224 | tf_op jit(solution)/shard_map/ppermute | solution.py:155
  3.8 1.5 collective-permute-start.1
  5.3 1.6 collective-permute-start.2
  6.9 0.9 fusion.8
  7.9 2.7 %collective-permute-done.2 = f32[1,32,1024]{2,1,0:T(8,128)S(1)} collective-permute-done((f32[1,32,1024]{2,1,0:T(8,128)S(1)}, f32[1,32,1024]{2,1,0:T(8,128)S(1)}, u32[]{:S(2)}, u32[]{:S(2)}) %collective-permute-start.2) | collective-permute-done | bytes 131104 | tf_op jit(solution)/shard_map/ppermute | solution.py:155
  10.7 1.3 collective-permute-start.3
  11.9 1.6 collective-permute-start.4
  13.6 1.4 collective-permute-start.5
  15.6 3.3 %collective-permute-start.6 = (f32[4,1,32,1024]{3,2,1,0:T(8,128)S(1)}, f32[4,1,32,1024]{3,2,1,0:T(8,128)S(1)}, u32[]{:S(2)}, u32[]{:S(2)}) collective-permute-start(f32[4,1,32,1024]{3,2,1,0:T(8,128)S(1)} %pad_maximum_fusion.2.refs_0_), channel_id=1, source_target_pairs={{0,1},{1,0},{2,3},{3,2},{4,5},{5,4},{6,7},{7,6},{8,9},{9,8},{10,11... | collective-permute-start | bytes 1572872 | tf_op jit(solution)/shard_map/ppermute | solution.py:168
  18.9 1.5 collective-permute-done.3.refs_1_
  20.4 2.9 %collective-permute-start.7 = (f32[4,1,32,1024]{3,2,1,0:T(8,128)S(1)}, f32[4,1,32,1024]{3,2,1,0:T(8,128)S(1)}, u32[]{:S(2)}, u32[]{:S(2)}) collective-permute-start(f32[4,1,32,1024]{3,2,1,0:T(8,128)S(1)} %collective-permute-done.3.refs_1_), channel_id=1, source_target_pairs={{0,1},{1,0},{2,3},{3,2},{4,5},{5,4},{6,7},{7,6},{8,9},{9,8},{10,11... | collective-permute-start | bytes 1572872 | tf_op jit(solution)/shard_map/ppermute | solution.py:168
  23.3 2.0 %collective-permute-done.4.refs_2_ = f32[4,1,32,1024]{3,2,1,0:T(8,128)S(1)} collective-permute-done((f32[4,1,32,1024]{3,2,1,0:T(8,128)S(1)}, f32[4,1,32,1024]{3,2,1,0:T(8,128)S(1)}, u32[]{:S(2)}, u32[]{:S(2)}) %collective-permute-start.4) | collective-permute-done | bytes 524320 | tf_op jit(solution)/shard_map/ppermute | solution.py:155
  25.3 1.8 collective-permute-done.5.refs_3_
  27.2 3.1 %collective-permute-start.9 = (f32[4,1,32,1024]{3,2,1,0:T(8,128)S(1)}, f32[4,1,32,1024]{3,2,1,0:T(8,128)}, u32[]{:S(2)}, u32[]{:S(2)}) collective-permute-start(f32[4,1,32,1024]{3,2,1,0:T(8,128)S(1)} %collective-permute-done.5.refs_3_), channel_id=1, source_target_pairs={{0,1},{1,0},{2,3},{3,2},{4,5},{5,4},{6,7},{7,6},{8,9},{9,8},{10,11... | collective-permute-start | bytes 1572872 | tf_op jit(solution)/shard_map/ppermute | solution.py:168
  31.3 0.9 fusion.7.refs_11_
  32.2 0.9 copy-done
  33.1 10.5 %shard_map.55 = (f32[32,1024]{1,0:T(8,128)S(1)}, f32[32,1024]{1,0:T(8,128)S(1)}) custom-call(f32[4,1,32,1024]{3,2,1,0:T(8,128)S(1)} %pad_maximum_fusion.2.refs_0_, f32[4,1,32,1024]{3,2,1,0:T(8,128)S(1)} %collective-permute-done.3.refs_1_, f32[4,1,32,1024]{3,2,1,0:T(8,128)S(1)} %collective-permute-done.4.refs_2_, ...), custom_call_target="tpu_custom_call" | custom-call | flops 4831838208 | bytes 50331648 | tf_op jit(solution)/shard_map/pallas_call | solution.py:130
  43.7 1.7 collective-permute-start.10
  45.4 3.7 %collective-permute-done.10 = f32[32,1024]{1,0:T(8,128)S(1)} collective-permute-done((f32[32,1024]{1,0:T(8,128)S(1)}, f32[32,1024]{1,0:T(8,128)S(1)}, u32[]{:S(2)}, u32[]{:S(2)}) %collective-permute-start.10) | collective-permute-done | bytes 131104 | tf_op jit(solution)/shard_map/ppermute | solution.py:212
  49.2 1.4 collective-permute-start.13
  50.6 2.2 %collective-permute-start.12 = (f32[3,32,1024]{2,1,0:T(8,128)S(1)}, f32[3,32,1024]{2,1,0:T(8,128)S(1)}, u32[]{:S(2)}, u32[]{:S(2)}) collective-permute-start(f32[3,32,1024]{2,1,0:T(8,128)S(1)} %pad_maximum_fusion.5), channel_id=1, source_target_pairs={{0,24},{1,7},{2,26},{3,1},{4,28},{5,3},{6,30},{7,5},{8,0},{9,15},{... | collective-permute-start | bytes 1179656 | tf_op jit(solution)/shard_map/ppermute | solution.py:155
  52.8 4.9 %collective-permute-done.13 = f32[3,32,1024]{2,1,0:T(8,128)S(1)} collective-permute-done((f32[3,32,1024]{2,1,0:T(8,128)S(1)}, f32[3,32,1024]{2,1,0:T(8,128)S(1)}, u32[]{:S(2)}, u32[]{:S(2)}) %collective-permute-start.13) | collective-permute-done | bytes 393248 | tf_op jit(solution)/shard_map/ppermute | solution.py:155
  57.7 3.8 %collective-permute-done.12 = f32[3,32,1024]{2,1,0:T(8,128)S(1)} collective-permute-done((f32[3,32,1024]{2,1,0:T(8,128)S(1)}, f32[3,32,1024]{2,1,0:T(8,128)S(1)}, u32[]{:S(2)}, u32[]{:S(2)}) %collective-permute-start.12) | collective-permute-done | bytes 393248 | tf_op jit(solution)/shard_map/ppermute | solution.py:155
  62.1 2.7 %collective-permute-start.15 = (f32[4,2,32,1024]{3,2,1,0:T(8,128)S(1)}, f32[4,2,32,1024]{3,2,1,0:T(8,128)S(1)}, u32[]{:S(2)}, u32[]{:S(2)}) collective-permute-start(f32[4,2,32,1024]{3,2,1,0:T(8,128)S(1)} %pad_maximum_fusion.refs_0_), channel_id=1, source_target_pairs={{0,6},{1,25},{2,0},{3,27},{4,2},{5,29},{6,4},{7,31},{8,14},{9,1},{... | collective-permute-start | bytes 3145736 | tf_op jit(solution)/shard_map/ppermute | solution.py:155
  64.8 2.8 %collective-permute-start.20 = (f32[4,2,32,1024]{3,2,1,0:T(8,128)S(1)}, f32[4,2,32,1024]{3,2,1,0:T(8,128)S(1)}, u32[]{:S(2)}, u32[]{:S(2)}) collective-permute-start(f32[4,2,32,1024]{3,2,1,0:T(8,128)S(1)} %pad_maximum_fusion.refs_0_), channel_id=1, source_target_pairs={{0,1},{1,0},{2,3},{3,2},{4,5},{5,4},{6,7},{7,6},{8,9},{9,8},{10,11... | collective-permute-start | bytes 3145736 | tf_op jit(solution)/shard_map/ppermute | solution.py:168
  67.6 20.9 %collective-permute-done.14.refs_1_ = f32[4,2,32,1024]{3,2,1,0:T(8,128)S(1)} collective-permute-done((f32[4,2,32,1024]{3,2,1,0:T(8,128)S(1)}, f32[4,2,32,1024]{3,2,1,0:T(8,128)S(1)}, u32[]{:S(2)}, u32[]{:S(2)}) %collective-permute-start.14) | collective-permute-done | bytes 1048608 | tf_op jit(solution)/shard_map/ppermute | solution.py:155
  88.5 2.0 collective-permute-start.22
  90.5 1.0 collective-permute-start.23
  91.5 1.5 collective-permute-start.24
  93.1 3.6 %collective-permute-done.24.refs_10_ = f32[32,1024]{1,0:T(8,128)S(1)} collective-permute-done((f32[32,1024]{1,0:T(8,128)S(1)}, f32[32,1024]{1,0:T(8,128)S(1)}, u32[]{:S(2)}, u32[]{:S(2)}) %collective-permute-start.24) | collective-permute-done | bytes 131104 | tf_op jit(solution)/shard_map/ppermute | solution.py:213
  96.7 2.6 %collective-permute-start.18 = (f32[4,1,32,1024]{3,2,1,0:T(8,128)S(1)}, f32[4,1,32,1024]{3,2,1,0:T(8,128)S(1)}, u32[]{:S(2)}, u32[]{:S(2)}) collective-permute-start(f32[4,1,32,1024]{3,2,1,0:T(8,128)S(1)} %pad_maximum_fusion.3.refs_0_), channel_id=1, source_target_pairs={{0,6},{1,25},{2,0},{3,27},{4,2},{5,29},{6,4},{7,31},{8,14},{9,1},{... | collective-permute-start | bytes 1572872 | tf_op jit(solution)/shard_map/ppermute | solution.py:155
  99.7 9.9 %shard_map.56.refs_10_ = f32[64,1024]{1,0:T(8,128)S(1)} custom-call(f32[4,2,32,1024]{3,2,1,0:T(8,128)S(1)} %pad_maximum_fusion.refs_0_, f32[4,2,32,1024]{3,2,1,0:T(8,128)S(1)} %collective-permute-done.14.refs_1_, f32[4,2,32,1024]{3,2,1,0:T(8,128)S(1)} %collective-permute-done.15.refs_2_, f32[4,2,32,1024]{3,2,1,0:T(8,128)S(1)} %collective-permute-done.16.refs_3_, ...), custom_call_target="tpu_custom_call" | custom-call | flops 4831838208 | bytes 50331648 | tf_op jit(solution)/shard_map/pallas_call | solution.py:130
  109.5 2.3 %collective-permute-done.17.refs_1_ = f32[4,1,32,1024]{3,2,1,0:T(8,128)S(1)} collective-permute-done((f32[4,1,32,1024]{3,2,1,0:T(8,128)S(1)}, f32[4,1,32,1024]{3,2,1,0:T(8,128)S(1)}, u32[]{:S(2)}, u32[]{:S(2)}) %collective-permute-start.17) | collective-permute-done | bytes 524320 | tf_op jit(solution)/shard_map/ppermute | solution.py:155
  111.8 2.5 %collective-permute-start.25 = (f32[4,1,32,1024]{3,2,1,0:T(8,128)S(1)}, f32[4,1,32,1024]{3,2,1,0:T(8,128)S(1)}, u32[]{:S(2)}, u32[]{:S(2)}) collective-permute-start(f32[4,1,32,1024]{3,2,1,0:T(8,128)S(1)} %pad_maximum_fusion.3.refs_0_), channel_id=1, source_target_pairs={{0,1},{1,0},{2,3},{3,2},{4,5},{5,4},{6,7},{7,6},{8,9},{9,8},{10,11... | collective-permute-start | bytes 1572872 | tf_op jit(solution)/shard_map/ppermute | solution.py:168
  114.8 1.0 collective-permute-done.25.refs_4_
  115.8 1.5 collective-permute-done.26.refs_5_
  117.4 0.8 collective-permute-done.28.refs_7_
  118.2 2.6 %shard_map.57 = (f32[32,1024]{1,0:T(8,128)S(1)}, f32[32,1024]{1,0:T(8,128)S(1)}, f32[32,1024]{1,0:T(8,128)S(1)}) custom-call(f32[4,1,32,1024]{3,2,1,0:T(8,128)S(1)} %pad_maximum_fusion.3.refs_0_, f32[4,1,32,1024]{3,2,1,0:T(8,128)S(1)} %collective-permute-done.17.refs_1_, f32[4,1,32,1024]{3,2,1,0:T(8,128)S(1)} %collective-permute-done.18.refs_2_, ...), custom_call_target="tpu_custom_call" | custom-call | flops 805306368 | bytes 8388608 | tf_op jit(solution)/shard_map/pallas_call | solution.py:130
  120.8 0.7 collective-permute-start.30
  121.5 1.3 collective-permute-start.31
  122.8 5.5 %collective-permute-start.29 = (f32[32,1024]{1,0:T(8,128)S(1)}, f32[32,1024]{1,0:T(8,128)S(1)}, u32[]{:S(2)}, u32[]{:S(2)}) collective-permute-start(f32[32,1024]{1,0:T(8,128)S(1)} %get-tuple-element.30), channel_id=1, source_target_pairs={{0,64},{64,0},{32,96},{96,32},{1,65},{65,1},{33,97},{97,33},{2,66}... | collective-permute-start | bytes 393224 | tf_op jit(solution)/shard_map/ppermute | solution.py:222
  128.3 1.3 collective-permute-start.45
  129.6 0.8 collective-permute-done.31
  130.4 3.8 %collective-permute-done.29 = f32[32,1024]{1,0:T(8,128)S(1)} collective-permute-done((f32[32,1024]{1,0:T(8,128)S(1)}, f32[32,1024]{1,0:T(8,128)S(1)}, u32[]{:S(2)}, u32[]{:S(2)}) %collective-permute-start.29) | collective-permute-done | bytes 131104 | tf_op jit(solution)/shard_map/ppermute | solution.py:222
  134.2 1.8 collective-permute-done.45
  136.1 0.7 collective-permute-start.34
  136.8 2.9 %collective-permute-start.33 = (f32[3,32,1024]{2,1,0:T(8,128)S(1)}, f32[3,32,1024]{2,1,0:T(8,128)S(1)}, u32[]{:S(2)}, u32[]{:S(2)}) collective-permute-start(f32[3,32,1024]{2,1,0:T(8,128)S(1)} %pad_maximum_fusion.6), channel_id=1, source_target_pairs={{0,24},{1,7},{2,26},{3,1},{4,28},{5,3},{6,30},{7,5},{8,0},{9,15},{... | collective-permute-start | bytes 1179656 | tf_op jit(solution)/shard_map/ppermute | solution.py:155
  139.7 4.9 %collective-permute-done.34 = f32[3,32,1024]{2,1,0:T(8,128)S(1)} collective-permute-done((f32[3,32,1024]{2,1,0:T(8,128)S(1)}, f32[3,32,1024]{2,1,0:T(8,128)S(1)}, u32[]{:S(2)}, u32[]{:S(2)}) %collective-permute-start.34) | collective-permute-done | bytes 393248 | tf_op jit(solution)/shard_map/ppermute | solution.py:155
  144.6 4.0 %collective-permute-done.33 = f32[3,32,1024]{2,1,0:T(8,128)S(1)} collective-permute-done((f32[3,32,1024]{2,1,0:T(8,128)S(1)}, f32[3,32,1024]{2,1,0:T(8,128)S(1)}, u32[]{:S(2)}, u32[]{:S(2)}) %collective-permute-start.33) | collective-permute-done | bytes 393248 | tf_op jit(solution)/shard_map/ppermute | solution.py:155
  149.0 2.7 %collective-permute-start.36 = (f32[4,2,32,1024]{3,2,1,0:T(8,128)S(1)}, f32[4,2,32,1024]{3,2,1,0:T(8,128)S(1)}, u32[]{:S(2)}, u32[]{:S(2)}) collective-permute-start(f32[4,2,32,1024]{3,2,1,0:T(8,128)S(1)} %pad_maximum_fusion.1.refs_0_), channel_id=1, source_target_pairs={{0,6},{1,25},{2,0},{3,27},{4,2},{5,29},{6,4},{7,31},{8,14},{9,1},{... | collective-permute-start | bytes 3145736 | tf_op jit(solution)/shard_map/ppermute | solution.py:155
  151.8 3.1 %collective-permute-start.41 = (f32[4,2,32,1024]{3,2,1,0:T(8,128)S(1)}, f32[4,2,32,1024]{3,2,1,0:T(8,128)S(1)}, u32[]{:S(2)}, u32[]{:S(2)}) collective-permute-start(f32[4,2,32,1024]{3,2,1,0:T(8,128)S(1)} %pad_maximum_fusion.1.refs_0_), channel_id=1, source_target_pairs={{0,1},{1,0},{2,3},{3,2},{4,5},{5,4},{6,7},{7,6},{8,9},{9,8},{10,11... | collective-permute-start | bytes 3145736 | tf_op jit(solution)/shard_map/ppermute | solution.py:168
  154.9 20.5 %collective-permute-done.35.refs_1_ = f32[4,2,32,1024]{3,2,1,0:T(8,128)S(1)} collective-permute-done((f32[4,2,32,1024]{3,2,1,0:T(8,128)S(1)}, f32[4,2,32,1024]{3,2,1,0:T(8,128)S(1)}, u32[]{:S(2)}, u32[]{:S(2)}) %collective-permute-start.35) | collective-permute-done | bytes 1048608 | tf_op jit(solution)/shard_map/ppermute | solution.py:155
  175.4 2.5 %collective-permute-start.43 = (f32[4,2,32,1024]{3,2,1,0:T(8,128)S(1)}, f32[4,2,32,1024]{3,2,1,0:T(8,128)S(1)}, u32[]{:S(2)}, u32[]{:S(2)}) collective-permute-start(f32[4,2,32,1024]{3,2,1,0:T(8,128)S(1)} %collective-permute-done.36.refs_2_), channel_id=1, source_target_pairs={{0,1},{1,0},{2,3},{3,2},{4,5},{5,4},{6,7},{7,6},{8,9},{9,8},{10,11... | collective-permute-start | bytes 3145736 | tf_op jit(solution)/shard_map/ppermute | solution.py:168
  177.9 1.0 collective-permute-start.44
  179.2 2.6 %collective-permute-start.39 = (f32[4,1,32,1024]{3,2,1,0:T(8,128)S(1)}, f32[4,1,32,1024]{3,2,1,0:T(8,128)S(1)}, u32[]{:S(2)}, u32[]{:S(2)}) collective-permute-start(f32[4,1,32,1024]{3,2,1,0:T(8,128)S(1)} %pad_maximum_fusion.4.refs_0_), channel_id=1, source_target_pairs={{0,6},{1,25},{2,0},{3,27},{4,2},{5,29},{6,4},{7,31},{8,14},{9,1},{... | collective-permute-start | bytes 1572872 | tf_op jit(solution)/shard_map/ppermute | solution.py:155
  182.1 10.4 %shard_map.58.refs_10_ = f32[32,1024]{1,0:T(8,128)S(1)} custom-call(f32[4,2,32,1024]{3,2,1,0:T(8,128)S(1)} %pad_maximum_fusion.1.refs_0_, f32[4,2,32,1024]{3,2,1,0:T(8,128)S(1)} %collective-permute-done.35.refs_1_, f32[4,2,32,1024]{3,2,1,0:T(8,128)S(1)} %collective-permute-done.36.refs_2_, f32[4,2,32,1024]{3,2,1,0:T(8,128)S(1)} %collective-permute-done.37.refs_3_, ...), custom_call_target="tpu_custom_call" | custom-call | flops 4831838208 | bytes 50331648 | tf_op jit(solution)/shard_map/pallas_call | solution.py:130
  192.5 1.7 collective-permute-done.38.refs_1_
  194.3 2.2 %collective-permute-start.46 = (f32[4,1,32,1024]{3,2,1,0:T(8,128)S(1)}, f32[4,1,32,1024]{3,2,1,0:T(8,128)S(1)}, u32[]{:S(2)}, u32[]{:S(2)}) collective-permute-start(f32[4,1,32,1024]{3,2,1,0:T(8,128)S(1)} %pad_maximum_fusion.4.refs_0_), channel_id=1, source_target_pairs={{0,1},{1,0},{2,3},{3,2},{4,5},{5,4},{6,7},{7,6},{8,9},{9,8},{10,11... | collective-permute-start | bytes 1572872 | tf_op jit(solution)/shard_map/ppermute | solution.py:168
  197.0 1.0 collective-permute-done.46.refs_4_
  198.0 0.7 collective-permute-done.47.refs_5_
  198.8 0.7 collective-permute-done.48.refs_6_
  199.5 0.7 collective-permute-done.49.refs_7_
  200.3 2.7 %shard_map.59 = f32[32,1024]{1,0:T(8,128)} custom-call(f32[4,1,32,1024]{3,2,1,0:T(8,128)S(1)} %pad_maximum_fusion.4.refs_0_, f32[4,1,32,1024]{3,2,1,0:T(8,128)S(1)} %collective-permute-done.38.refs_1_, f32[4,1,32,1024]{3,2,1,0:T(8,128)S(1)} %collective-permute-done.39.refs_2_, f32[4,1,32,1024]{3,2,1,0:T(8,128)S(1)} %collective-permute-done.40.refs_3_, ...), custom_call_target="tpu_custom_call" | custom-call | flops 805306368 | bytes 8388608 | tf_op jit(solution)/shard_map/pallas_call | solution.py:130
  (75 shorter events, 4.8 us)
Async XLA Ops:
  1.6 6.3 %collective-permute-start = (f32[1,32,1024]{2,1,0:T(8,128)S(1)}, f32[1,32,1024]{2,1,0:T(8,128)S(1)}, u32[]{:S(2)}, u32[]{:S(2)}) collective-permute-start(f32[1,32,1024]{2,1,0:T(8,128)S(1)} %constant_dynamic-slice_fusion), channel_id=1, source_target_pairs={{0,8},{1,3},{2,10},{3,5},{4,12},{5,7},{6,14},{7,1},{8,16},{9,11},{... | collective-permute-start | bytes 393224 | tf_op jit(solution)/shard_map/ppermute | solution.py:155
  3.8 4.1 %collective-permute-start.1 = (f32[1,32,1024]{2,1,0:T(8,128)S(1)}, f32[1,32,1024]{2,1,0:T(8,128)S(1)}, u32[]{:S(2)}, u32[]{:S(2)}) collective-permute-start(f32[1,32,1024]{2,1,0:T(8,128)S(1)} %constant_dynamic-slice_fusion), channel_id=1, source_target_pairs={{0,24},{1,7},{2,26},{3,1},{4,28},{5,3},{6,30},{7,5},{8,0},{9,15},{... | collective-permute-start | bytes 393224 | tf_op jit(solution)/shard_map/ppermute | solution.py:155
  5.3 5.3 %collective-permute-start.2 = (f32[1,32,1024]{2,1,0:T(8,128)S(1)}, f32[1,32,1024]{2,1,0:T(8,128)S(1)}, u32[]{:S(2)}, u32[]{:S(2)}) collective-permute-start(f32[1,32,1024]{2,1,0:T(8,128)S(1)} %constant_dynamic-slice_fusion), channel_id=1, source_target_pairs={{0,16},{1,5},{2,18},{3,7},{4,20},{5,1},{6,22},{7,3},{8,24},{9,13},... | collective-permute-start | bytes 393224 | tf_op jit(solution)/shard_map/ppermute | solution.py:155
  10.7 9.7 %collective-permute-start.3 = (f32[4,1,32,1024]{3,2,1,0:T(8,128)S(1)}, f32[4,1,32,1024]{3,2,1,0:T(8,128)S(1)}, u32[]{:S(2)}, u32[]{:S(2)}) collective-permute-start(f32[4,1,32,1024]{3,2,1,0:T(8,128)S(1)} %pad_maximum_fusion.2.refs_0_), channel_id=1, source_target_pairs={{0,2},{1,9},{2,4},{3,11},{4,6},{5,13},{6,0},{7,15},{8,10},{9,17},{... | collective-permute-start | bytes 1572872 | tf_op jit(solution)/shard_map/ppermute | solution.py:155
  11.9 13.4 %collective-permute-start.4 = (f32[4,1,32,1024]{3,2,1,0:T(8,128)S(1)}, f32[4,1,32,1024]{3,2,1,0:T(8,128)S(1)}, u32[]{:S(2)}, u32[]{:S(2)}) collective-permute-start(f32[4,1,32,1024]{3,2,1,0:T(8,128)S(1)} %pad_maximum_fusion.2.refs_0_), channel_id=1, source_target_pairs={{0,6},{1,25},{2,0},{3,27},{4,2},{5,29},{6,4},{7,31},{8,14},{9,1},{... | collective-permute-start | bytes 1572872 | tf_op jit(solution)/shard_map/ppermute | solution.py:155
  13.6 13.6 %collective-permute-start.5 = (f32[4,1,32,1024]{3,2,1,0:T(8,128)S(1)}, f32[4,1,32,1024]{3,2,1,0:T(8,128)S(1)}, u32[]{:S(2)}, u32[]{:S(2)}) collective-permute-start(f32[4,1,32,1024]{3,2,1,0:T(8,128)S(1)} %pad_maximum_fusion.2.refs_0_), channel_id=1, source_target_pairs={{0,4},{1,17},{2,6},{3,19},{4,0},{5,21},{6,2},{7,23},{8,12},{9,25},... | collective-permute-start | bytes 1572872 | tf_op jit(solution)/shard_map/ppermute | solution.py:155
  15.6 16.6 %collective-permute-start.6 = (f32[4,1,32,1024]{3,2,1,0:T(8,128)S(1)}, f32[4,1,32,1024]{3,2,1,0:T(8,128)S(1)}, u32[]{:S(2)}, u32[]{:S(2)}) collective-permute-start(f32[4,1,32,1024]{3,2,1,0:T(8,128)S(1)} %pad_maximum_fusion.2.refs_0_), channel_id=1, source_target_pairs={{0,1},{1,0},{2,3},{3,2},{4,5},{5,4},{6,7},{7,6},{8,9},{9,8},{10,11... | collective-permute-start | bytes 1572872 | tf_op jit(solution)/shard_map/ppermute | solution.py:168
  20.4 11.8 %collective-permute-start.7 = (f32[4,1,32,1024]{3,2,1,0:T(8,128)S(1)}, f32[4,1,32,1024]{3,2,1,0:T(8,128)S(1)}, u32[]{:S(2)}, u32[]{:S(2)}) collective-permute-start(f32[4,1,32,1024]{3,2,1,0:T(8,128)S(1)} %collective-permute-done.3.refs_1_), channel_id=1, source_target_pairs={{0,1},{1,0},{2,3},{3,2},{4,5},{5,4},{6,7},{7,6},{8,9},{9,8},{10,11... | collective-permute-start | bytes 1572872 | tf_op jit(solution)/shard_map/ppermute | solution.py:168
  25.3 6.9 %collective-permute-start.8 = (f32[4,1,32,1024]{3,2,1,0:T(8,128)S(1)}, f32[4,1,32,1024]{3,2,1,0:T(8,128)}, u32[]{:S(2)}, u32[]{:S(2)}) collective-permute-start(f32[4,1,32,1024]{3,2,1,0:T(8,128)S(1)} %collective-permute-done.4.refs_2_), channel_id=1, source_target_pairs={{0,1},{1,0},{2,3},{3,2},{4,5},{5,4},{6,7},{7,6},{8,9},{9,8},{10,11... | collective-permute-start | bytes 1572872 | tf_op jit(solution)/shard_map/ppermute | solution.py:168
  27.2 5.1 %collective-permute-start.9 = (f32[4,1,32,1024]{3,2,1,0:T(8,128)S(1)}, f32[4,1,32,1024]{3,2,1,0:T(8,128)}, u32[]{:S(2)}, u32[]{:S(2)}) collective-permute-start(f32[4,1,32,1024]{3,2,1,0:T(8,128)S(1)} %collective-permute-done.5.refs_3_), channel_id=1, source_target_pairs={{0,1},{1,0},{2,3},{3,2},{4,5},{5,4},{6,7},{7,6},{8,9},{9,8},{10,11... | collective-permute-start | bytes 1572872 | tf_op jit(solution)/shard_map/ppermute | solution.py:168
  32.2 0.9 copy-start
  43.7 5.5 %collective-permute-start.10 = (f32[32,1024]{1,0:T(8,128)S(1)}, f32[32,1024]{1,0:T(8,128)S(1)}, u32[]{:S(2)}, u32[]{:S(2)}) collective-permute-start(f32[32,1024]{1,0:T(8,128)S(1)} %get-tuple-element.23.refs_11_), channel_id=1, source_target_pairs={{0,32},{32,0},{64,96},{96,64},{1,33},{33,1},{65,97},{97,65},{2,34}... | collective-permute-start | bytes 393224 | tf_op jit(solution)/shard_map/ppermute | solution.py:212
  49.2 8.5 %collective-permute-start.13 = (f32[3,32,1024]{2,1,0:T(8,128)S(1)}, f32[3,32,1024]{2,1,0:T(8,128)S(1)}, u32[]{:S(2)}, u32[]{:S(2)}) collective-permute-start(f32[3,32,1024]{2,1,0:T(8,128)S(1)} %pad_maximum_fusion.5), channel_id=1, source_target_pairs={{0,16},{1,5},{2,18},{3,7},{4,20},{5,1},{6,22},{7,3},{8,24},{9,13},... | collective-permute-start | bytes 1179656 | tf_op jit(solution)/shard_map/ppermute | solution.py:155
  50.6 10.9 %collective-permute-start.12 = (f32[3,32,1024]{2,1,0:T(8,128)S(1)}, f32[3,32,1024]{2,1,0:T(8,128)S(1)}, u32[]{:S(2)}, u32[]{:S(2)}) collective-permute-start(f32[3,32,1024]{2,1,0:T(8,128)S(1)} %pad_maximum_fusion.5), channel_id=1, source_target_pairs={{0,24},{1,7},{2,26},{3,1},{4,28},{5,3},{6,30},{7,5},{8,0},{9,15},{... | collective-permute-start | bytes 1179656 | tf_op jit(solution)/shard_map/ppermute | solution.py:155
  52.8 9.1 %collective-permute-start.11 = (f32[3,32,1024]{2,1,0:T(8,128)S(1)}, f32[3,32,1024]{2,1,0:T(8,128)S(1)}, u32[]{:S(2)}, u32[]{:S(2)}) collective-permute-start(f32[3,32,1024]{2,1,0:T(8,128)S(1)} %pad_maximum_fusion.5), channel_id=1, source_target_pairs={{0,8},{1,3},{2,10},{3,5},{4,12},{5,7},{6,14},{7,1},{8,16},{9,11},{... | collective-permute-start | bytes 1179656 | tf_op jit(solution)/shard_map/ppermute | solution.py:155
  62.0 26.5 %collective-permute-start.14 = (f32[4,2,32,1024]{3,2,1,0:T(8,128)S(1)}, f32[4,2,32,1024]{3,2,1,0:T(8,128)S(1)}, u32[]{:S(2)}, u32[]{:S(2)}) collective-permute-start(f32[4,2,32,1024]{3,2,1,0:T(8,128)S(1)} %pad_maximum_fusion.refs_0_), channel_id=1, source_target_pairs={{0,2},{1,9},{2,4},{3,11},{4,6},{5,13},{6,0},{7,15},{8,10},{9,17},{... | collective-permute-start | bytes 3145736 | tf_op jit(solution)/shard_map/ppermute | solution.py:155
  62.1 26.4 %collective-permute-start.15 = (f32[4,2,32,1024]{3,2,1,0:T(8,128)S(1)}, f32[4,2,32,1024]{3,2,1,0:T(8,128)S(1)}, u32[]{:S(2)}, u32[]{:S(2)}) collective-permute-start(f32[4,2,32,1024]{3,2,1,0:T(8,128)S(1)} %pad_maximum_fusion.refs_0_), channel_id=1, source_target_pairs={{0,6},{1,25},{2,0},{3,27},{4,2},{5,29},{6,4},{7,31},{8,14},{9,1},{... | collective-permute-start | bytes 3145736 | tf_op jit(solution)/shard_map/ppermute | solution.py:155
  64.8 25.7 %collective-permute-start.16 = (f32[4,2,32,1024]{3,2,1,0:T(8,128)S(1)}, f32[4,2,32,1024]{3,2,1,0:T(8,128)S(1)}, u32[]{:S(2)}, u32[]{:S(2)}) collective-permute-start(f32[4,2,32,1024]{3,2,1,0:T(8,128)S(1)} %pad_maximum_fusion.refs_0_), channel_id=1, source_target_pairs={{0,4},{1,17},{2,6},{3,19},{4,0},{5,21},{6,2},{7,23},{8,12},{9,25},... | collective-permute-start | bytes 3145736 | tf_op jit(solution)/shard_map/ppermute | solution.py:155
  64.8 32.0 %collective-permute-start.20 = (f32[4,2,32,1024]{3,2,1,0:T(8,128)S(1)}, f32[4,2,32,1024]{3,2,1,0:T(8,128)S(1)}, u32[]{:S(2)}, u32[]{:S(2)}) collective-permute-start(f32[4,2,32,1024]{3,2,1,0:T(8,128)S(1)} %pad_maximum_fusion.refs_0_), channel_id=1, source_target_pairs={{0,1},{1,0},{2,3},{3,2},{4,5},{5,4},{6,7},{7,6},{8,9},{9,8},{10,11... | collective-permute-start | bytes 3145736 | tf_op jit(solution)/shard_map/ppermute | solution.py:168
  88.5 10.9 %collective-permute-start.21 = (f32[4,2,32,1024]{3,2,1,0:T(8,128)S(1)}, f32[4,2,32,1024]{3,2,1,0:T(8,128)S(1)}, u32[]{:S(2)}, u32[]{:S(2)}) collective-permute-start(f32[4,2,32,1024]{3,2,1,0:T(8,128)S(1)} %collective-permute-done.14.refs_1_), channel_id=1, source_target_pairs={{0,1},{1,0},{2,3},{3,2},{4,5},{5,4},{6,7},{7,6},{8,9},{9,8},{10,11... | collective-permute-start | bytes 3145736 | tf_op jit(solution)/shard_map/ppermute | solution.py:168
  88.5 11.2 %collective-permute-start.22 = (f32[4,2,32,1024]{3,2,1,0:T(8,128)S(1)}, f32[4,2,32,1024]{3,2,1,0:T(8,128)S(1)}, u32[]{:S(2)}, u32[]{:S(2)}) collective-permute-start(f32[4,2,32,1024]{3,2,1,0:T(8,128)S(1)} %collective-permute-done.15.refs_2_), channel_id=1, source_target_pairs={{0,1},{1,0},{2,3},{3,2},{4,5},{5,4},{6,7},{7,6},{8,9},{9,8},{10,11... | collective-permute-start | bytes 3145736 | tf_op jit(solution)/shard_map/ppermute | solution.py:168
  90.5 9.2 %collective-permute-start.23 = (f32[4,2,32,1024]{3,2,1,0:T(8,128)S(1)}, f32[4,2,32,1024]{3,2,1,0:T(8,128)S(1)}, u32[]{:S(2)}, u32[]{:S(2)}) collective-permute-start(f32[4,2,32,1024]{3,2,1,0:T(8,128)S(1)} %collective-permute-done.16.refs_3_), channel_id=1, source_target_pairs={{0,1},{1,0},{2,3},{3,2},{4,5},{5,4},{6,7},{7,6},{8,9},{9,8},{10,11... | collective-permute-start | bytes 3145736 | tf_op jit(solution)/shard_map/ppermute | solution.py:168
  91.5 5.1 %collective-permute-start.24 = (f32[32,1024]{1,0:T(8,128)S(1)}, f32[32,1024]{1,0:T(8,128)S(1)}, u32[]{:S(2)}, u32[]{:S(2)}) collective-permute-start(f32[32,1024]{1,0:T(8,128)S(1)} %get-tuple-element.22.refs_9_), channel_id=1, source_target_pairs={{0,32},{32,0},{64,96},{96,64},{1,33},{33,1},{65,97},{97,65},{2,34}... | collective-permute-start | bytes 393224 | tf_op jit(solution)/shard_map/ppermute | solution.py:213
  96.6 15.2 %collective-permute-start.17 = (f32[4,1,32,1024]{3,2,1,0:T(8,128)S(1)}, f32[4,1,32,1024]{3,2,1,0:T(8,128)S(1)}, u32[]{:S(2)}, u32[]{:S(2)}) collective-permute-start(f32[4,1,32,1024]{3,2,1,0:T(8,128)S(1)} %pad_maximum_fusion.3.refs_0_), channel_id=1, source_target_pairs={{0,2},{1,9},{2,4},{3,11},{4,6},{5,13},{6,0},{7,15},{8,10},{9,17},{... | collective-permute-start | bytes 1572872 | tf_op jit(solution)/shard_map/ppermute | solution.py:155
  96.7 15.1 %collective-permute-start.18 = (f32[4,1,32,1024]{3,2,1,0:T(8,128)S(1)}, f32[4,1,32,1024]{3,2,1,0:T(8,128)S(1)}, u32[]{:S(2)}, u32[]{:S(2)}) collective-permute-start(f32[4,1,32,1024]{3,2,1,0:T(8,128)S(1)} %pad_maximum_fusion.3.refs_0_), channel_id=1, source_target_pairs={{0,6},{1,25},{2,0},{3,27},{4,2},{5,29},{6,4},{7,31},{8,14},{9,1},{... | collective-permute-start | bytes 1572872 | tf_op jit(solution)/shard_map/ppermute | solution.py:155
  99.3 12.5 %collective-permute-start.19 = (f32[4,1,32,1024]{3,2,1,0:T(8,128)S(1)}, f32[4,1,32,1024]{3,2,1,0:T(8,128)S(1)}, u32[]{:S(2)}, u32[]{:S(2)}) collective-permute-start(f32[4,1,32,1024]{3,2,1,0:T(8,128)S(1)} %pad_maximum_fusion.3.refs_0_), channel_id=1, source_target_pairs={{0,4},{1,17},{2,6},{3,19},{4,0},{5,21},{6,2},{7,23},{8,12},{9,25},... | collective-permute-start | bytes 1572872 | tf_op jit(solution)/shard_map/ppermute | solution.py:155
  111.8 4.0 %collective-permute-start.25 = (f32[4,1,32,1024]{3,2,1,0:T(8,128)S(1)}, f32[4,1,32,1024]{3,2,1,0:T(8,128)S(1)}, u32[]{:S(2)}, u32[]{:S(2)}) collective-permute-start(f32[4,1,32,1024]{3,2,1,0:T(8,128)S(1)} %pad_maximum_fusion.3.refs_0_), channel_id=1, source_target_pairs={{0,1},{1,0},{2,3},{3,2},{4,5},{5,4},{6,7},{7,6},{8,9},{9,8},{10,11... | collective-permute-start | bytes 1572872 | tf_op jit(solution)/shard_map/ppermute | solution.py:168
  114.3 3.0 %collective-permute-start.26 = (f32[4,1,32,1024]{3,2,1,0:T(8,128)S(1)}, f32[4,1,32,1024]{3,2,1,0:T(8,128)S(1)}, u32[]{:S(2)}, u32[]{:S(2)}) collective-permute-start(f32[4,1,32,1024]{3,2,1,0:T(8,128)S(1)} %collective-permute-done.17.refs_1_), channel_id=1, source_target_pairs={{0,1},{1,0},{2,3},{3,2},{4,5},{5,4},{6,7},{7,6},{8,9},{9,8},{10,11... | collective-permute-start | bytes 1572872 | tf_op jit(solution)/shard_map/ppermute | solution.py:168
  114.3 3.2 %collective-permute-start.27 = (f32[4,1,32,1024]{3,2,1,0:T(8,128)S(1)}, f32[4,1,32,1024]{3,2,1,0:T(8,128)}, u32[]{:S(2)}, u32[]{:S(2)}) collective-permute-start(f32[4,1,32,1024]{3,2,1,0:T(8,128)S(1)} %collective-permute-done.18.refs_2_), channel_id=1, source_target_pairs={{0,1},{1,0},{2,3},{3,2},{4,5},{5,4},{6,7},{7,6},{8,9},{9,8},{10,11... | collective-permute-start | bytes 1572872 | tf_op jit(solution)/shard_map/ppermute | solution.py:168
  114.8 3.4 %collective-permute-start.28 = (f32[4,1,32,1024]{3,2,1,0:T(8,128)S(1)}, f32[4,1,32,1024]{3,2,1,0:T(8,128)}, u32[]{:S(2)}, u32[]{:S(2)}) collective-permute-start(f32[4,1,32,1024]{3,2,1,0:T(8,128)S(1)} %collective-permute-done.19.refs_3_), channel_id=1, source_target_pairs={{0,1},{1,0},{2,3},{3,2},{4,5},{5,4},{6,7},{7,6},{8,9},{9,8},{10,11... | collective-permute-start | bytes 1572872 | tf_op jit(solution)/shard_map/ppermute | solution.py:168
  120.8 8.7 %collective-permute-start.30 = (f32[32,1024]{1,0:T(8,128)S(1)}, f32[32,1024]{1,0:T(8,128)S(1)}, u32[]{:S(2)}, u32[]{:S(2)}) collective-permute-start(f32[32,1024]{1,0:T(8,128)S(1)} %get-tuple-element.32.refs_11_), channel_id=1, source_target_pairs={{32,64},{64,32},{33,65},{65,33},{34,66},{66,34},{35,67},{67,35},{3... | collective-permute-start | bytes 393224 | tf_op jit(solution)/shard_map/ppermute | solution.py:221
  121.5 8.9 %collective-permute-start.31 = (f32[32,1024]{1,0:T(8,128)S(1)}, f32[32,1024]{1,0:T(8,128)S(1)}, u32[]{:S(2)}, u32[]{:S(2)}) collective-permute-start(f32[32,1024]{1,0:T(8,128)S(1)} %get-tuple-element.32.refs_11_), channel_id=1, source_target_pairs={{32,0},{64,96},{33,1},{65,97},{34,2},{66,98},{35,3},{67,99},{36,4}... | collective-permute-start | bytes 393224 | tf_op jit(solution)/shard_map/ppermute | solution.py:220
  122.8 11.4 %collective-permute-start.29 = (f32[32,1024]{1,0:T(8,128)S(1)}, f32[32,1024]{1,0:T(8,128)S(1)}, u32[]{:S(2)}, u32[]{:S(2)}) collective-permute-start(f32[32,1024]{1,0:T(8,128)S(1)} %get-tuple-element.30), channel_id=1, source_target_pairs={{0,64},{64,0},{32,96},{96,32},{1,65},{65,1},{33,97},{97,33},{2,66}... | collective-permute-start | bytes 393224 | tf_op jit(solution)/shard_map/ppermute | solution.py:222
  128.3 7.7 %collective-permute-start.45 = (f32[32,1024]{1,0:T(8,128)S(1)}, f32[32,1024]{1,0:T(8,128)S(1)}, u32[]{:S(2)}, u32[]{:S(2)}) collective-permute-start(f32[32,1024]{1,0:T(8,128)S(1)} %get-tuple-element.31), channel_id=1, source_target_pairs={{32,0},{64,96},{33,1},{65,97},{34,2},{66,98},{35,3},{67,99},{36,4}... | collective-permute-start | bytes 393224 | tf_op jit(solution)/shard_map/ppermute | solution.py:223
  136.1 8.5 %collective-permute-start.34 = (f32[3,32,1024]{2,1,0:T(8,128)S(1)}, f32[3,32,1024]{2,1,0:T(8,128)S(1)}, u32[]{:S(2)}, u32[]{:S(2)}) collective-permute-start(f32[3,32,1024]{2,1,0:T(8,128)S(1)} %pad_maximum_fusion.6), channel_id=1, source_target_pairs={{0,16},{1,5},{2,18},{3,7},{4,20},{5,1},{6,22},{7,3},{8,24},{9,13},... | collective-permute-start | bytes 1179656 | tf_op jit(solution)/shard_map/ppermute | solution.py:155
  136.8 11.8 %collective-permute-start.33 = (f32[3,32,1024]{2,1,0:T(8,128)S(1)}, f32[3,32,1024]{2,1,0:T(8,128)S(1)}, u32[]{:S(2)}, u32[]{:S(2)}) collective-permute-start(f32[3,32,1024]{2,1,0:T(8,128)S(1)} %pad_maximum_fusion.6), channel_id=1, source_target_pairs={{0,24},{1,7},{2,26},{3,1},{4,28},{5,3},{6,30},{7,5},{8,0},{9,15},{... | collective-permute-start | bytes 1179656 | tf_op jit(solution)/shard_map/ppermute | solution.py:155
  139.7 9.1 %collective-permute-start.32 = (f32[3,32,1024]{2,1,0:T(8,128)S(1)}, f32[3,32,1024]{2,1,0:T(8,128)S(1)}, u32[]{:S(2)}, u32[]{:S(2)}) collective-permute-start(f32[3,32,1024]{2,1,0:T(8,128)S(1)} %pad_maximum_fusion.6), channel_id=1, source_target_pairs={{0,8},{1,3},{2,10},{3,5},{4,12},{5,7},{6,14},{7,1},{8,16},{9,11},{... | collective-permute-start | bytes 1179656 | tf_op jit(solution)/shard_map/ppermute | solution.py:155
  148.9 26.5 %collective-permute-start.35 = (f32[4,2,32,1024]{3,2,1,0:T(8,128)S(1)}, f32[4,2,32,1024]{3,2,1,0:T(8,128)S(1)}, u32[]{:S(2)}, u32[]{:S(2)}) collective-permute-start(f32[4,2,32,1024]{3,2,1,0:T(8,128)S(1)} %pad_maximum_fusion.1.refs_0_), channel_id=1, source_target_pairs={{0,2},{1,9},{2,4},{3,11},{4,6},{5,13},{6,0},{7,15},{8,10},{9,17},{... | collective-permute-start | bytes 3145736 | tf_op jit(solution)/shard_map/ppermute | solution.py:155
  149.0 26.4 %collective-permute-start.36 = (f32[4,2,32,1024]{3,2,1,0:T(8,128)S(1)}, f32[4,2,32,1024]{3,2,1,0:T(8,128)S(1)}, u32[]{:S(2)}, u32[]{:S(2)}) collective-permute-start(f32[4,2,32,1024]{3,2,1,0:T(8,128)S(1)} %pad_maximum_fusion.1.refs_0_), channel_id=1, source_target_pairs={{0,6},{1,25},{2,0},{3,27},{4,2},{5,29},{6,4},{7,31},{8,14},{9,1},{... | collective-permute-start | bytes 3145736 | tf_op jit(solution)/shard_map/ppermute | solution.py:155
  151.7 26.2 %collective-permute-start.37 = (f32[4,2,32,1024]{3,2,1,0:T(8,128)S(1)}, f32[4,2,32,1024]{3,2,1,0:T(8,128)S(1)}, u32[]{:S(2)}, u32[]{:S(2)}) collective-permute-start(f32[4,2,32,1024]{3,2,1,0:T(8,128)S(1)} %pad_maximum_fusion.1.refs_0_), channel_id=1, source_target_pairs={{0,4},{1,17},{2,6},{3,19},{4,0},{5,21},{6,2},{7,23},{8,12},{9,25},... | collective-permute-start | bytes 3145736 | tf_op jit(solution)/shard_map/ppermute | solution.py:155
  151.8 27.4 %collective-permute-start.41 = (f32[4,2,32,1024]{3,2,1,0:T(8,128)S(1)}, f32[4,2,32,1024]{3,2,1,0:T(8,128)S(1)}, u32[]{:S(2)}, u32[]{:S(2)}) collective-permute-start(f32[4,2,32,1024]{3,2,1,0:T(8,128)S(1)} %pad_maximum_fusion.1.refs_0_), channel_id=1, source_target_pairs={{0,1},{1,0},{2,3},{3,2},{4,5},{5,4},{6,7},{7,6},{8,9},{9,8},{10,11... | collective-permute-start | bytes 3145736 | tf_op jit(solution)/shard_map/ppermute | solution.py:168
  175.4 6.4 %collective-permute-start.42 = (f32[4,2,32,1024]{3,2,1,0:T(8,128)S(1)}, f32[4,2,32,1024]{3,2,1,0:T(8,128)S(1)}, u32[]{:S(2)}, u32[]{:S(2)}) collective-permute-start(f32[4,2,32,1024]{3,2,1,0:T(8,128)S(1)} %collective-permute-done.35.refs_1_), channel_id=1, source_target_pairs={{0,1},{1,0},{2,3},{3,2},{4,5},{5,4},{6,7},{7,6},{8,9},{9,8},{10,11... | collective-permute-start | bytes 3145736 | tf_op jit(solution)/shard_map/ppermute | solution.py:168
  175.4 6.7 %collective-permute-start.43 = (f32[4,2,32,1024]{3,2,1,0:T(8,128)S(1)}, f32[4,2,32,1024]{3,2,1,0:T(8,128)S(1)}, u32[]{:S(2)}, u32[]{:S(2)}) collective-permute-start(f32[4,2,32,1024]{3,2,1,0:T(8,128)S(1)} %collective-permute-done.36.refs_2_), channel_id=1, source_target_pairs={{0,1},{1,0},{2,3},{3,2},{4,5},{5,4},{6,7},{7,6},{8,9},{9,8},{10,11... | collective-permute-start | bytes 3145736 | tf_op jit(solution)/shard_map/ppermute | solution.py:168
  177.9 4.2 %collective-permute-start.44 = (f32[4,2,32,1024]{3,2,1,0:T(8,128)S(1)}, f32[4,2,32,1024]{3,2,1,0:T(8,128)S(1)}, u32[]{:S(2)}, u32[]{:S(2)}) collective-permute-start(f32[4,2,32,1024]{3,2,1,0:T(8,128)S(1)} %collective-permute-done.37.refs_3_), channel_id=1, source_target_pairs={{0,1},{1,0},{2,3},{3,2},{4,5},{5,4},{6,7},{7,6},{8,9},{9,8},{10,11... | collective-permute-start | bytes 3145736 | tf_op jit(solution)/shard_map/ppermute | solution.py:168
  179.0 15.2 %collective-permute-start.38 = (f32[4,1,32,1024]{3,2,1,0:T(8,128)S(1)}, f32[4,1,32,1024]{3,2,1,0:T(8,128)S(1)}, u32[]{:S(2)}, u32[]{:S(2)}) collective-permute-start(f32[4,1,32,1024]{3,2,1,0:T(8,128)S(1)} %pad_maximum_fusion.4.refs_0_), channel_id=1, source_target_pairs={{0,2},{1,9},{2,4},{3,11},{4,6},{5,13},{6,0},{7,15},{8,10},{9,17},{... | collective-permute-start | bytes 1572872 | tf_op jit(solution)/shard_map/ppermute | solution.py:155
  179.2 15.0 %collective-permute-start.39 = (f32[4,1,32,1024]{3,2,1,0:T(8,128)S(1)}, f32[4,1,32,1024]{3,2,1,0:T(8,128)S(1)}, u32[]{:S(2)}, u32[]{:S(2)}) collective-permute-start(f32[4,1,32,1024]{3,2,1,0:T(8,128)S(1)} %pad_maximum_fusion.4.refs_0_), channel_id=1, source_target_pairs={{0,6},{1,25},{2,0},{3,27},{4,2},{5,29},{6,4},{7,31},{8,14},{9,1},{... | collective-permute-start | bytes 1572872 | tf_op jit(solution)/shard_map/ppermute | solution.py:155
  181.8 12.5 %collective-permute-start.40 = (f32[4,1,32,1024]{3,2,1,0:T(8,128)S(1)}, f32[4,1,32,1024]{3,2,1,0:T(8,128)S(1)}, u32[]{:S(2)}, u32[]{:S(2)}) collective-permute-start(f32[4,1,32,1024]{3,2,1,0:T(8,128)S(1)} %pad_maximum_fusion.4.refs_0_), channel_id=1, source_target_pairs={{0,4},{1,17},{2,6},{3,19},{4,0},{5,21},{6,2},{7,23},{8,12},{9,25},... | collective-permute-start | bytes 1572872 | tf_op jit(solution)/shard_map/ppermute | solution.py:155
  194.3 3.7 %collective-permute-start.46 = (f32[4,1,32,1024]{3,2,1,0:T(8,128)S(1)}, f32[4,1,32,1024]{3,2,1,0:T(8,128)S(1)}, u32[]{:S(2)}, u32[]{:S(2)}) collective-permute-start(f32[4,1,32,1024]{3,2,1,0:T(8,128)S(1)} %pad_maximum_fusion.4.refs_0_), channel_id=1, source_target_pairs={{0,1},{1,0},{2,3},{3,2},{4,5},{5,4},{6,7},{7,6},{8,9},{9,8},{10,11... | collective-permute-start | bytes 1572872 | tf_op jit(solution)/shard_map/ppermute | solution.py:168
  196.5 2.3 %collective-permute-start.47 = (f32[4,1,32,1024]{3,2,1,0:T(8,128)S(1)}, f32[4,1,32,1024]{3,2,1,0:T(8,128)S(1)}, u32[]{:S(2)}, u32[]{:S(2)}) collective-permute-start(f32[4,1,32,1024]{3,2,1,0:T(8,128)S(1)} %collective-permute-done.38.refs_1_), channel_id=1, source_target_pairs={{0,1},{1,0},{2,3},{3,2},{4,5},{5,4},{6,7},{7,6},{8,9},{9,8},{10,11... | collective-permute-start | bytes 1572872 | tf_op jit(solution)/shard_map/ppermute | solution.py:168
  196.5 3.0 %collective-permute-start.48 = (f32[4,1,32,1024]{3,2,1,0:T(8,128)S(1)}, f32[4,1,32,1024]{3,2,1,0:T(8,128)S(1)}, u32[]{:S(2)}, u32[]{:S(2)}) collective-permute-start(f32[4,1,32,1024]{3,2,1,0:T(8,128)S(1)} %collective-permute-done.39.refs_2_), channel_id=1, source_target_pairs={{0,1},{1,0},{2,3},{3,2},{4,5},{5,4},{6,7},{7,6},{8,9},{9,8},{10,11... | collective-permute-start | bytes 1572872 | tf_op jit(solution)/shard_map/ppermute | solution.py:168
  197.0 3.3 %collective-permute-start.49 = (f32[4,1,32,1024]{3,2,1,0:T(8,128)S(1)}, f32[4,1,32,1024]{3,2,1,0:T(8,128)S(1)}, u32[]{:S(2)}, u32[]{:S(2)}) collective-permute-start(f32[4,1,32,1024]{3,2,1,0:T(8,128)S(1)} %collective-permute-done.40.refs_3_), channel_id=1, source_target_pairs={{0,1},{1,0},{2,3},{3,2},{4,5},{5,4},{6,7},{7,6},{8,9},{9,8},{10,11... | collective-permute-start | bytes 1572872 | tf_op jit(solution)/shard_map/ppermute | solution.py:168

commit v3 on v2

--- a/solution.py
+++ b/solution.py
@@ -1,3 +1,5 @@
+import math
+
 import jax
 import jax.numpy as jnp
 from jax import lax
@@ -44,14 +46,22 @@
 
 def layer_kernel(*refs):
     pieces, refs = refs[:PIECES], refs[PIECES:]
-    places, facts, thickness, own, wave_decay, refl_out, trans_out, high, low = refs
+    wave_decay, places, facts, thickness, refl_out, trans_out, decays_out = refs[:7]
+    high_out, low_out, high, low, decay_row, sem, sems = refs[7:]
+    copy = pltpu.make_async_copy(wave_decay.at[pl.ds(facts[1], 1)], decay_row, sem)
+    copy.start()
     split(pieces, places, high, low)
-    rows, order = own.shape
-    decays = jnp.exp(-wave_decay[pl.ds(facts[1], 1), :] * thickness[0])
+    saves = [pltpu.make_async_copy(high, high_out, sems.at[0]), pltpu.make_async_copy(low, low_out, sems.at[1])]
+    for save in saves:
+        save.start()
+    copy.wait()
+    rows, order = pieces[0].shape[2:]
+    decays = jnp.exp(-decay_row[...] * thickness[0])
+    decays_out[...] = decays
     row_ids = facts[0] + lax.broadcasted_iota(jnp.int32, (rows, order), 0)
     eye = row_ids == lax.broadcasted_iota(jnp.int32, (rows, order), 1)
     own_decays = jnp.sum(jnp.where(eye, decays, 0.0), axis=1, keepdims=True)
-    term = product(own_decays * own[...] * decays, high.at[0], low.at[0])
+    term = product(own_decays * pieces[0][0, 0] * decays, high.at[0], low.at[0])
 
     def body(k, carry):
         term, summed = carry
@@ -64,30 +74,48 @@
     both = product(jnp.concatenate([scaled, summed], axis=0), high.at[0], low.at[0])
     refl_out[...] = both[:rows] * decays - both[rows:]
     trans_out[...] = scaled - product(both[:rows], high.at[0], low.at[0])
-
-
-def pair_chain(*refs):
-    pieces, refs = refs[:PIECES], refs[PIECES:]
-    places, start_own, start_oth, out, high, low = refs
-    split(pieces, places, high, low)
-    first = product(start_own[...], high.at[1], low.at[1])
-    both = jnp.concatenate([first, start_oth[...]], axis=0)
-
-    def body(k, carry):
+    for save in saves:
+        save.wait()
+
+
+def pair_kernel(*refs):
+    own_pieces, oth_pieces, refs = refs[:PIECES], refs[PIECES : 2 * PIECES], refs[2 * PIECES :]
+    high_in, low_in, places, inner, own_refl, own_trans, oth_trans, decay_row = refs[:8]
+    refl_out, trans_out, far_out, own_high, own_low, oth_high, oth_low, layer_high, layer_low, sems = refs[8:]
+    loads = [
+        pltpu.make_async_copy(high_in, layer_high, sems.at[0]),
+        pltpu.make_async_copy(low_in, layer_low, sems.at[1]),
+    ]
+    for load in loads:
+        load.start()
+    split(own_pieces, places, own_high, own_low)
+    split(oth_pieces, places, oth_high, oth_low)
+    first = product(own_trans[...], oth_high.at[0], oth_low.at[0])
+    both = jnp.concatenate([first, oth_trans[...]], axis=0)
+
+    def chain(k, carry):
         both, summed = carry
-        both = product(both, high.at[0], low.at[0])
-        both = product(both, high.at[1], low.at[1])
+        both = product(both, own_high.at[0], own_low.at[0])
+        both = product(both, oth_high.at[0], oth_low.at[0])
         return both, summed + both
 
-    _, out[...] = lax.fori_loop(0, TERMS - 1, body, (both, both))
-
-
-def pair_close(*refs):
-    pieces, refs = refs[:PIECES], refs[PIECES:]
-    places, inner, summed, own_refl, refl_out, trans_out, far_out, high, low = refs
-    split(pieces, places, high, low)
+    _, summed = lax.fori_loop(0, TERMS - 1, chain, (both, both))
+    decays = decay_row[...]
+    for load in loads:
+        load.wait()
+
+    def layer(rows):
+        return product(rows, layer_high.at[0], layer_low.at[0])
+
+    def series(k, carry):
+        term, summed = carry
+        term = layer(layer(term * decays) * decays)
+        return term, summed + term
+
+    _, summed = lax.fori_loop(0, TERMS - 1, series, (summed, summed))
+    scaled = summed * decays
+    done = scaled - layer(layer(scaled))
     rows = own_refl.shape[0]
-    done = product(summed[...], high.at[0], low.at[0])
     refl, trans = own_refl[...] + done[:rows], done[rows:]
     refl_out[...] = refl
     trans_out[...] = trans
@@ -120,24 +148,31 @@
     out[...] = base + product(summed[...], high.at[0], low.at[0])
 
 
-def call(kernel, steps, outs, pieces, tables, small, placed=True):
-    lines, slots, _, order = pieces[0].shape
+def call(kernel, room, steps, outs, pieces, tables, small, far=(), scratch=(), placed=True):
     vmem = pl.BlockSpec(memory_space=pltpu.VMEM)
     here = [pltpu.with_memory_space_constraint(a, pltpu.VMEM) for a in (*pieces, *small)]
-    out_shape = tuple(
-        pltpu.VMEM(shape, jnp.float32) if placed else jax.ShapeDtypeStruct(shape, jnp.float32) for shape in outs
-    )
+    far = [pltpu.with_memory_space_constraint(a, pltpu.HBM) for a in far]
+    used = sum(math.prod(a.shape) * 2 for a in scratch if len(a.shape) == 3)
     return pl.pallas_call(
         kernel,
-        out_shape=out_shape,
-        in_specs=[vmem] * len(pieces) + [pl.BlockSpec(memory_space=pltpu.SMEM)] * len(tables) + [vmem] * len(small),
-        out_specs=(vmem,) * len(outs),
-        scratch_shapes=[pltpu.VMEM((slots, order, order), jnp.bfloat16)] * 2,
+        out_shape=tuple(
+            out if placed else jax.ShapeDtypeStruct(out.shape, out.dtype) for out in outs
+        ),
+        in_specs=[vmem] * len(pieces)
+        + [pl.BlockSpec(memory_space=pl.ANY)] * len(far)
+        + [pl.BlockSpec(memory_space=pltpu.SMEM)] * len(tables)
+        + [vmem] * len(small),
+        out_specs=tuple(vmem if out.dtype == jnp.float32 else pl.BlockSpec(memory_space=pl.ANY) for out in outs),
+        scratch_shapes=list(scratch),
         cost_estimate=pl.CostEstimate(
-            flops=steps * 6 * 64 * order * order, transcendentals=0, bytes_accessed=steps * MATRIX_BYTES
+            flops=steps * 6 * 64 * 1024 * 1024, transcendentals=0, bytes_accessed=steps * MATRIX_BYTES
         ),
-        compiler_params=pltpu.CompilerParams(vmem_limit_bytes=(slots + 3) * MATRIX_BYTES),
-    )(*here[: len(pieces)], *tables, *here[len(pieces) :])
+        compiler_params=pltpu.CompilerParams(vmem_limit_bytes=used + room * 1024 * 1024),
+    )(*here[: len(pieces)], *far, *tables, *here[len(pieces) :])
+
+
+def matrices(slots, order, space=pltpu.VMEM):
+    return (space((slots, order, order), jnp.bfloat16),) * 2
 
 
 def panel_of(x, y, core):
@@ -178,14 +213,6 @@
         along_y = panel_of(x - outer + SIDE, y - inner + SIDE, 1)
         found.append(jnp.where(owner == 0, along_x, along_y).reshape(-1))
     return jnp.concatenate(found)
-
-
-def gather_two_and_one(rows):
-    line = line_of(rows)
-    mine = spread(jnp.stack([block[:2] for block in line]))
-    rest = jnp.stack([block[2:] for block in line])
-    rest, *_ = lax.optimization_barrier((rest, *mine[1:]))
-    return flipped(mine), spread(rest)
 
 
 def after(pieces, value):
@@ -204,32 +231,47 @@
     inner_flag = inner.astype(jnp.int32)[None]
     facts = jnp.stack([panel * panel_rows, material[0]])
     own = lax.dynamic_index_in_dim(reflections, material[0], 0, keepdims=False)
-    refl, trans = call(
-        layer_kernel, 2 * TERMS, (rows, rows), flipped(spread(jnp.stack(line_of(own[None])))),
-        (places, facts, thickness), (own, wave_decay),
+    block = pltpu.VMEM(rows, jnp.float32)
+    refl, trans, decays, *halved = call(
+        layer_kernel, 10, 2 * TERMS, (block, block, pltpu.VMEM((1, order), jnp.float32), *matrices(1, order, pltpu.HBM)),
+        flipped(spread(jnp.stack(line_of(own[None])))), (places, facts, thickness), (), far=(wave_decay,),
+        scratch=(
+            *matrices(1, order), pltpu.VMEM((1, order), jnp.float32),
+            pltpu.SemaphoreType.DMA(()), pltpu.SemaphoreType.DMA((2,)),
+        ),
     )
     pairs = [(0, 1), (1, 0), (2, 3), (3, 2)]
-    oth_refl = lax.ppermute(refl, "layer", pairs)
+    line = jnp.stack(line_of(refl[None]))
+    oth_line = lax.ppermute(line, "layer", pairs)
     oth_trans = lax.ppermute(trans, "layer", pairs)
-    pieces, closing = gather_two_and_one(jnp.stack([refl, oth_refl, trans]))
-    (summed,) = call(pair_chain, 2 * TERMS, ((2 * panel_rows, order),), pieces, (places,), (trans, oth_trans))
-    closing, summed = after(closing, summed)
+    mine = spread(line)
+    oth_line, oth_trans, mine[3] = lax.optimization_barrier((oth_line, oth_trans, mine[3]))
     refl, trans, away = call(
-        pair_close, 2, (rows, rows, rows), closing, (places, inner_flag), (summed, refl)
-    )
+        pair_kernel, 16, 4 * TERMS, (block, block, block), flipped(mine) + flipped(spread(oth_line)),
+        (places, inner_flag), (refl, trans, oth_trans, decays), far=halved,
+        scratch=matrices(1, order) * 3 + (pltpu.SemaphoreType.DMA((2,)),),
+    )
+    far = lax.ppermute(away, "layer", [(0, 2), (2, 0), (1, 3), (3, 1)])
     near = lax.ppermute(refl, "layer", [(1, 0), (2, 3)])
     cross = lax.ppermute(refl, "layer", [(1, 2), (2, 1)])
-    far = lax.ppermute(away, "layer", [(0, 2), (2, 0), (1, 3), (3, 1)])
+    blocks = jnp.stack(
+        [jnp.where(inner, cross, near), jnp.where(inner, refl, far), jnp.where(inner, far, trans)]
+    )
+    trans, blocks = lax.optimization_barrier((trans, blocks))
     near_trans = lax.ppermute(trans, "layer", [(1, 0), (2, 3)])
-    pieces, closing = gather_two_and_one(
-        jnp.stack(
-            [jnp.where(inner, cross, near), jnp.where(inner, refl, far), jnp.where(inner, far, trans)]
-        )
-    )
+    line = line_of(blocks)
+    mine = spread(jnp.stack([part[:2] for part in line]))
+    rest = jnp.stack([part[2:] for part in line])
+    rest, *_ = lax.optimization_barrier((rest, *mine[1:]))
+    rest = spread(rest)
     start = jnp.where(inner, trans, near_trans)
-    (summed,) = call(last_chain, 2 * TERMS, (rows,), pieces, (places, inner_flag), (start,))
-    closing, summed = after(closing, summed)
-    (out,) = call(last_close, 2, (rows,), closing, (places, inner_flag), (summed, refl), placed=False)
+    (summed,) = call(
+        last_chain, 12, 2 * TERMS, (block,), flipped(mine), (places, inner_flag), (start,), scratch=matrices(2, order)
+    )
+    closing, summed = after(rest, summed)
+    (out,) = call(
+        last_close, 10, 2, (block,), closing, (places, inner_flag), (summed, refl), scratch=matrices(1, order), placed=False
+    )
     return out[None]
 
 

time: 203 us -> 186 us (0.916)
  waiting for transfers between devices: 92.1 us -> 65.3 us
  Pallas kernels: 36.1 us -> 44.3 us
    ppermute x24, waiting for transfers between devices: 71.7 us -> 51.8 us  [moved(): return lax.ppermute(block, 'panel', route)]
    pallas_call x5 -> x4, Pallas kernels: 36.1 us -> 44.3 us  [call(): pl.pallas_call(kernel, out_shape=tuple((out if placed else jax.ShapeDtype...]
    ppermute x1, waiting for transfers between devices: 3.57 us -> 0.01 us  [local(): oth_trans = lax.ppermute(trans, 'layer', pairs)]
    unnamed x2 -> x8, local copies, waits for them, and re-layouts: 0.9 us -> 3.67 us
    ppermute x1, waiting for transfers between devices: 0.8 us -> 3.07 us  [local(): near = lax.ppermute(refl, 'layer', [(1, 0), (2, 3)])]
    ppermute x1, waiting for transfers between devices: 3.83 us -> 1.6 us  [local(): far = lax.ppermute(away, 'layer', [(0, 2), (2, 0), (1, 3), (3, 1)])]
  transfers between devices with their start and end apart: 50 -> 50, of which waited for: 28 -> 26; matrix products, arithmetic and copies ran while one was open for 2% -> 1% of each run, Pallas kernels for 10% -> 6%
where the time goes in v3:
time: 186 us; the launch traced here: 185 us
  starting transfers between devices  66.5 us (36%)
  waiting for transfers between devices  65.3 us (35%)
  Pallas kernels  44.3 us (24%)
  local copies, waits for them, and re-layouts  5.78 us (3%)
    ppermute x24, waiting for transfers between devices, moved(): return lax.ppermute(block, 'panel', route)  51.8 us
    pallas_call x4, Pallas kernels, call(): pl.pallas_call(kernel, out_shape=tuple((out if placed else jax.ShapeDtype...  44.3 us
    ppermute x24, starting transfers between devices, moved(): return lax.ppermute(block, 'panel', route)  28.9 us
    ppermute x20, starting transfers between devices, flipped(): return pieces + [lax.ppermute(piece, 'panel', flip) for piece in pieces]  27.6 us
    ppermute x20, waiting for transfers between devices, flipped(): return pieces + [lax.ppermute(piece, 'panel', flip) for piece in pieces]  5.85 us
  transfers between devices with their start and end apart: 50, of which 26 were waited for; matrix products, arithmetic and copies ran while one was open for 1% of the time, Pallas kernels for 6%

profile of v3, /device:TPU:1, one launch (start us, length us, event | category | flops | bytes accessed | tf_op | source)
XLA Modules:
  0.0 184.6 jit_solution(8013363340613419593)
XLA Ops:
  0.7 0.9 constant_dynamic-slice_fusion
  1.6 3.6 %collective-permute-start.1 = (f32[1,32,1024]{2,1,0:T(8,128)S(1)}, f32[1,32,1024]{2,1,0:T(8,128)S(1)}, u32[]{:S(2)}, u32[]{:S(2)}) collective-permute-start(f32[1,32,1024]{2,1,0:T(8,128)S(1)} %constant_dynamic-slice_fusion), channel_id=1, source_target_pairs={{0,24},{1,7},{2,26},{3,1},{4,28},{5,3},{6,30},{7,5},{8,0},{9,15},{... | collective-permute-start | bytes 393224 | tf_op jit(solution)/shard_map/ppermute | solution.py:190
  5.2 1.6 collective-permute-start.2
  6.9 0.9 fusion.5
  7.8 4.2 %collective-permute-done = f32[1,32,1024]{2,1,0:T(8,128)S(1)} collective-permute-done((f32[1,32,1024]{2,1,0:T(8,128)S(1)}, f32[1,32,1024]{2,1,0:T(8,128)S(1)}, u32[]{:S(2)}, u32[]{:S(2)}) %collective-permute-start) | collective-permute-done | bytes 131104 | tf_op jit(solution)/shard_map/ppermute | solution.py:190
  12.0 2.5 %collective-permute-start.5 = (f32[4,1,32,1024]{3,2,1,0:T(8,128)S(1)}, f32[4,1,32,1024]{3,2,1,0:T(8,128)S(1)}, u32[]{:S(2)}, u32[]{:S(2)}) collective-permute-start(f32[4,1,32,1024]{3,2,1,0:T(8,128)S(1)} %pad_maximum_fusion.1.refs_0_), channel_id=1, source_target_pairs={{0,4},{1,17},{2,6},{3,19},{4,0},{5,21},{6,2},{7,23},{8,12},{9,25},... | collective-permute-start | bytes 1572872 | tf_op jit(solution)/shard_map/ppermute | solution.py:190
  14.5 0.9 collective-permute-start.4
  16.0 2.9 %collective-permute-start.6 = (f32[4,1,32,1024]{3,2,1,0:T(8,128)S(1)}, f32[4,1,32,1024]{3,2,1,0:T(8,128)S(1)}, u32[]{:S(2)}, u32[]{:S(2)}) collective-permute-start(f32[4,1,32,1024]{3,2,1,0:T(8,128)S(1)} %pad_maximum_fusion.1.refs_0_), channel_id=1, source_target_pairs={{0,1},{1,0},{2,3},{3,2},{4,5},{5,4},{6,7},{7,6},{8,9},{9,8},{10,11... | collective-permute-start | bytes 1572872 | tf_op jit(solution)/shard_map/ppermute | solution.py:203
  18.8 3.1 %collective-permute-done.5.refs_3_ = f32[4,1,32,1024]{3,2,1,0:T(8,128)S(1)} collective-permute-done((f32[4,1,32,1024]{3,2,1,0:T(8,128)S(1)}, f32[4,1,32,1024]{3,2,1,0:T(8,128)S(1)}, u32[]{:S(2)}, u32[]{:S(2)}) %collective-permute-start.5) | collective-permute-done | bytes 524320 | tf_op jit(solution)/shard_map/ppermute | solution.py:190
  21.9 2.5 %collective-permute-start.9 = (f32[4,1,32,1024]{3,2,1,0:T(8,128)S(1)}, f32[4,1,32,1024]{3,2,1,0:T(8,128)S(1)}, u32[]{:S(2)}, u32[]{:S(2)}) collective-permute-start(f32[4,1,32,1024]{3,2,1,0:T(8,128)S(1)} %collective-permute-done.5.refs_3_), channel_id=1, source_target_pairs={{0,1},{1,0},{2,3},{3,2},{4,5},{5,4},{6,7},{7,6},{8,9},{9,8},{10,11... | collective-permute-start | bytes 1572872 | tf_op jit(solution)/shard_map/ppermute | solution.py:203
  24.4 3.2 %collective-permute-done.4.refs_2_ = f32[4,1,32,1024]{3,2,1,0:T(8,128)S(1)} collective-permute-done((f32[4,1,32,1024]{3,2,1,0:T(8,128)S(1)}, f32[4,1,32,1024]{3,2,1,0:T(8,128)S(1)}, u32[]{:S(2)}, u32[]{:S(2)}) %collective-permute-start.4) | collective-permute-done | bytes 524320 | tf_op jit(solution)/shard_map/ppermute | solution.py:190
  27.6 2.7 %collective-permute-start.8 = (f32[4,1,32,1024]{3,2,1,0:T(8,128)S(1)}, f32[4,1,32,1024]{3,2,1,0:T(8,128)}, u32[]{:S(2)}, u32[]{:S(2)}) collective-permute-start(f32[4,1,32,1024]{3,2,1,0:T(8,128)S(1)} %collective-permute-done.4.refs_2_), channel_id=1, source_target_pairs={{0,1},{1,0},{2,3},{3,2},{4,5},{5,4},{6,7},{7,6},{8,9},{9,8},{10,11... | collective-permute-start | bytes 1572872 | tf_op jit(solution)/shard_map/ppermute | solution.py:203
  32.7 10.6 %shard_map.55 = (f32[32,1024]{1,0:T(8,128)S(1)}, f32[32,1024]{1,0:T(8,128)S(1)}, f32[1,1024]{1,0:T(1,128)S(1)}, bf16[1,1024,1024]{2,1,0:T(8,128)(2,1)}, bf16[1,1024,1024]{2,1,0:T(8,128)(2,1)}) custom-call(f32[4,1,32,1024]{3,2,1,0:T(8,128)S(1)} %pad_maximum_fusion.1.refs_0_, f32[4,1,32,1024]{3,2,1,0:T(8,128)S(1)} %collective-permute-done.3.refs_1_, ...), custom_call_target="tpu_custom_call" | custom-call | flops 4831838208 | bytes 50331648 | tf_op jit(solution)/shard_map/pallas_call | solution.py:156
  43.3 1.9 %collective-permute-start.12 = (f32[1,32,1024]{2,1,0:T(8,128)S(1)}, f32[1,32,1024]{2,1,0:T(8,128)S(1)}, u32[]{:S(2)}, u32[]{:S(2)}) collective-permute-start(f32[1,32,1024]{2,1,0:T(8,128)S(1)} %bitcast.39), channel_id=1, source_target_pairs={{0,16},{1,5},{2,18},{3,7},{4,20},{5,1},{6,22},{7,3},{8,24},{9,13},... | collective-permute-start | bytes 393224 | tf_op jit(solution)/shard_map/ppermute | solution.py:190
  45.3 1.4 collective-permute-start.11
  46.7 1.6 collective-permute-start.16
  49.0 1.4 collective-permute-done.11
  50.4 1.5 collective-permute-done.10
  51.9 0.8 collective-permute-start.17
  52.8 1.6 collective-permute-start.15
  54.4 2.0 %collective-permute-start.18 = (f32[4,1,32,1024]{3,2,1,0:T(8,128)S(1)}, f32[4,1,32,1024]{3,2,1,0:T(8,128)S(1)}, u32[]{:S(2)}, u32[]{:S(2)}) collective-permute-start(f32[4,1,32,1024]{3,2,1,0:T(8,128)S(1)} %pad_maximum_fusion.2.refs_0_), channel_id=1, source_target_pairs={{0,1},{1,0},{2,3},{3,2},{4,5},{5,4},{6,7},{7,6},{8,9},{9,8},{10,11... | collective-permute-start | bytes 1572872 | tf_op jit(solution)/shard_map/ppermute | solution.py:203
  56.4 1.1 collective-permute-start.14
  57.9 4.0 %collective-permute-done.17.refs_3_ = f32[4,1,32,1024]{3,2,1,0:T(8,128)S(1)} collective-permute-done((f32[4,1,32,1024]{3,2,1,0:T(8,128)S(1)}, f32[4,1,32,1024]{3,2,1,0:T(8,128)S(1)}, u32[]{:S(2)}, u32[]{:S(2)}) %collective-permute-start.17) | collective-permute-done | bytes 524320 | tf_op jit(solution)/shard_map/ppermute | solution.py:190
  61.9 3.0 %collective-permute-done.15.refs_8_ = f32[4,1,32,1024]{3,2,1,0:T(8,128)S(1)} collective-permute-done((f32[4,1,32,1024]{3,2,1,0:T(8,128)S(1)}, f32[4,1,32,1024]{3,2,1,0:T(8,128)S(1)}, u32[]{:S(2)}, u32[]{:S(2)}) %collective-permute-start.15) | collective-permute-done | bytes 524320 | tf_op jit(solution)/shard_map/ppermute | solution.py:245
  64.8 2.5 %collective-permute-start.21 = (f32[4,1,32,1024]{3,2,1,0:T(8,128)S(1)}, f32[4,1,32,1024]{3,2,1,0:T(8,128)S(1)}, u32[]{:S(2)}, u32[]{:S(2)}) collective-permute-start(f32[4,1,32,1024]{3,2,1,0:T(8,128)S(1)} %collective-permute-done.17.refs_3_), channel_id=1, source_target_pairs={{0,1},{1,0},{2,3},{3,2},{4,5},{5,4},{6,7},{7,6},{8,9},{9,8},{10,11... | collective-permute-start | bytes 1572872 | tf_op jit(solution)/shard_map/ppermute | solution.py:203
  67.3 2.2 %collective-permute-start.24 = (f32[4,1,32,1024]{3,2,1,0:T(8,128)S(1)}, f32[4,1,32,1024]{3,2,1,0:T(8,128)}, u32[]{:S(2)}, u32[]{:S(2)}) collective-permute-start(f32[4,1,32,1024]{3,2,1,0:T(8,128)S(1)} %collective-permute-done.15.refs_8_), channel_id=1, source_target_pairs={{0,4},{1,17},{2,6},{3,19},{4,0},{5,21},{6,2},{7,23},{8,12},{9,25},... | collective-permute-start | bytes 1572872 | tf_op jit(solution)/shard_map/ppermute | solution.py:190
  69.5 1.5 collective-permute-start.23
  71.1 0.8 copy-done
  72.2 0.8 copy-done.2
  73.2 4.1 %collective-permute-done.24.refs_11_ = f32[4,1,32,1024]{3,2,1,0:T(8,128)} collective-permute-done((f32[4,1,32,1024]{3,2,1,0:T(8,128)S(1)}, f32[4,1,32,1024]{3,2,1,0:T(8,128)}, u32[]{:S(2)}, u32[]{:S(2)}) %collective-permute-start.24) | collective-permute-done | bytes 524320 | tf_op jit(solution)/shard_map/ppermute | solution.py:190
  77.3 1.4 collective-permute-start.28
  78.7 2.9 %collective-permute-done.23.refs_10_ = f32[4,1,32,1024]{3,2,1,0:T(8,128)} collective-permute-done((f32[4,1,32,1024]{3,2,1,0:T(8,128)S(1)}, f32[4,1,32,1024]{3,2,1,0:T(8,128)}, u32[]{:S(2)}, u32[]{:S(2)}) %collective-permute-start.23) | collective-permute-done | bytes 524320 | tf_op jit(solution)/shard_map/ppermute | solution.py:190
  81.5 1.1 collective-permute-start.27
  82.8 1.4 collective-permute-start.26
  84.5 1.6 collective-permute-done.26.refs_13_
  86.1 1.0 copy-done.1
  87.1 1.0 copy-done.3
  88.2 20.6 %shard_map.56 = (f32[32,1024]{1,0:T(8,128)S(1)}, f32[32,1024]{1,0:T(8,128)S(1)}, f32[32,1024]{1,0:T(8,128)S(1)}) custom-call(f32[4,1,32,1024]{3,2,1,0:T(8,128)S(1)} %pad_maximum_fusion.2.refs_0_, f32[4,1,32,1024]{3,2,1,0:T(8,128)S(1)} %collective-permute-done.13.refs_1_, f32[4,1,32,1024]{3,2,1,0:T(8,128)S(1)} %collective-permute-done.14.refs_2_, ...), custom_call_target="tpu_custom_call" | custom-call | flops 9663676416 | bytes 100663296 | tf_op jit(solution)/shard_map/pallas_call | solution.py:156
  108.8 3.5 %collective-permute-start.31 = (f32[32,1024]{1,0:T(8,128)S(1)}, f32[32,1024]{1,0:T(8,128)S(1)}, u32[]{:S(2)}, u32[]{:S(2)}) collective-permute-start(f32[32,1024]{1,0:T(8,128)S(1)} %get-tuple-element.34), channel_id=1, source_target_pairs={{0,64},{64,0},{32,96},{96,32},{1,65},{65,1},{33,97},{97,33},{2,66}... | collective-permute-start | bytes 393224 | tf_op jit(solution)/shard_map/ppermute | solution.py:254
  112.3 1.3 collective-permute-start.30
  114.3 1.6 collective-permute-done.31
  115.9 3.1 %collective-permute-done.30 = f32[32,1024]{1,0:T(8,128)S(1)} collective-permute-done((f32[32,1024]{1,0:T(8,128)S(1)}, f32[32,1024]{1,0:T(8,128)S(1)}, u32[]{:S(2)}, u32[]{:S(2)}) %collective-permute-start.30) | collective-permute-done | bytes 131104 | tf_op jit(solution)/shard_map/ppermute | solution.py:255
  119.0 1.1 collective-permute-start.34
  120.1 1.7 collective-permute-start.33
  121.8 5.7 %collective-permute-done.34 = f32[3,32,1024]{2,1,0:T(8,128)S(1)} collective-permute-done((f32[3,32,1024]{2,1,0:T(8,128)S(1)}, f32[3,32,1024]{2,1,0:T(8,128)S(1)}, u32[]{:S(2)}, u32[]{:S(2)}) %collective-permute-start.34) | collective-permute-done | bytes 393248 | tf_op jit(solution)/shard_map/ppermute | solution.py:190
  127.6 3.2 %collective-permute-done.33 = f32[3,32,1024]{2,1,0:T(8,128)S(1)} collective-permute-done((f32[3,32,1024]{2,1,0:T(8,128)S(1)}, f32[3,32,1024]{2,1,0:T(8,128)S(1)}, u32[]{:S(2)}, u32[]{:S(2)}) %collective-permute-start.33) | collective-permute-done | bytes 393248 | tf_op jit(solution)/shard_map/ppermute | solution.py:190
  130.9 0.9 collective-permute-done.32
  131.9 2.0 %collective-permute-start.37 = (f32[4,2,32,1024]{3,2,1,0:T(8,128)S(1)}, f32[4,2,32,1024]{3,2,1,0:T(8,128)S(1)}, u32[]{:S(2)}, u32[]{:S(2)}) collective-permute-start(f32[4,2,32,1024]{3,2,1,0:T(8,128)S(1)} %pad_maximum_fusion.refs_0_), channel_id=1, source_target_pairs={{0,4},{1,17},{2,6},{3,19},{4,0},{5,21},{6,2},{7,23},{8,12},{9,25},... | collective-permute-start | bytes 3145736 | tf_op jit(solution)/shard_map/ppermute | solution.py:190
  133.9 1.7 collective-permute-start.36
  135.6 1.3 collective-permute-start.45
  136.9 1.9 %collective-permute-start.41 = (f32[4,2,32,1024]{3,2,1,0:T(8,128)S(1)}, f32[4,2,32,1024]{3,2,1,0:T(8,128)S(1)}, u32[]{:S(2)}, u32[]{:S(2)}) collective-permute-start(f32[4,2,32,1024]{3,2,1,0:T(8,128)S(1)} %pad_maximum_fusion.refs_0_), channel_id=1, source_target_pairs={{0,1},{1,0},{2,3},{3,2},{4,5},{5,4},{6,7},{7,6},{8,9},{9,8},{10,11... | collective-permute-start | bytes 3145736 | tf_op jit(solution)/shard_map/ppermute | solution.py:203
  138.8 8.6 %collective-permute-done.37.refs_3_ = f32[4,2,32,1024]{3,2,1,0:T(8,128)S(1)} collective-permute-done((f32[4,2,32,1024]{3,2,1,0:T(8,128)S(1)}, f32[4,2,32,1024]{3,2,1,0:T(8,128)S(1)}, u32[]{:S(2)}, u32[]{:S(2)}) %collective-permute-start.37) | collective-permute-done | bytes 1048608 | tf_op jit(solution)/shard_map/ppermute | solution.py:190
  147.5 3.1 %collective-permute-start.44 = (f32[4,2,32,1024]{3,2,1,0:T(8,128)S(1)}, f32[4,2,32,1024]{3,2,1,0:T(8,128)S(1)}, u32[]{:S(2)}, u32[]{:S(2)}) collective-permute-start(f32[4,2,32,1024]{3,2,1,0:T(8,128)S(1)} %collective-permute-done.37.refs_3_), channel_id=1, source_target_pairs={{0,1},{1,0},{2,3},{3,2},{4,5},{5,4},{6,7},{7,6},{8,9},{9,8},{10,11... | collective-permute-start | bytes 3145736 | tf_op jit(solution)/shard_map/ppermute | solution.py:203
  150.6 6.8 %collective-permute-done.36.refs_2_ = f32[4,2,32,1024]{3,2,1,0:T(8,128)S(1)} collective-permute-done((f32[4,2,32,1024]{3,2,1,0:T(8,128)S(1)}, f32[4,2,32,1024]{3,2,1,0:T(8,128)S(1)}, u32[]{:S(2)}, u32[]{:S(2)}) %collective-permute-start.36) | collective-permute-done | bytes 1048608 | tf_op jit(solution)/shard_map/ppermute | solution.py:190
  157.3 3.8 %collective-permute-start.43 = (f32[4,2,32,1024]{3,2,1,0:T(8,128)S(1)}, f32[4,2,32,1024]{3,2,1,0:T(8,128)S(1)}, u32[]{:S(2)}, u32[]{:S(2)}) collective-permute-start(f32[4,2,32,1024]{3,2,1,0:T(8,128)S(1)} %collective-permute-done.36.refs_2_), channel_id=1, source_target_pairs={{0,1},{1,0},{2,3},{3,2},{4,5},{5,4},{6,7},{7,6},{8,9},{9,8},{10,11... | collective-permute-start | bytes 3145736 | tf_op jit(solution)/shard_map/ppermute | solution.py:203
  161.8 2.3 %collective-permute-start.40 = (f32[4,1,32,1024]{3,2,1,0:T(8,128)S(1)}, f32[4,1,32,1024]{3,2,1,0:T(8,128)S(1)}, u32[]{:S(2)}, u32[]{:S(2)}) collective-permute-start(f32[4,1,32,1024]{3,2,1,0:T(8,128)S(1)} %pad_maximum_fusion.3.refs_0_), channel_id=1, source_target_pairs={{0,4},{1,17},{2,6},{3,19},{4,0},{5,21},{6,2},{7,23},{8,12},{9,25},... | collective-permute-start | bytes 1572872 | tf_op jit(solution)/shard_map/ppermute | solution.py:190
  164.1 0.9 collective-permute-start.39
  165.6 10.4 %shard_map.57.refs_10_ = f32[32,1024]{1,0:T(8,128)S(1)} custom-call(f32[4,2,32,1024]{3,2,1,0:T(8,128)S(1)} %pad_maximum_fusion.refs_0_, f32[4,2,32,1024]{3,2,1,0:T(8,128)S(1)} %collective-permute-done.35.refs_1_, f32[4,2,32,1024]{3,2,1,0:T(8,128)S(1)} %collective-permute-done.36.refs_2_, f32[4,2,32,1024]{3,2,1,0:T(8,128)S(1)} %collective-permute-done.37.refs_3_, ...), custom_call_target="tpu_custom_call" | custom-call | flops 4831838208 | bytes 50331648 | tf_op jit(solution)/shard_map/pallas_call | solution.py:156
  176.0 1.3 collective-permute-done.38.refs_1_
  177.3 0.9 collective-permute-start.46
  178.7 1.0 collective-permute-done.46.refs_4_
  179.7 0.7 collective-permute-done.47.refs_5_
  180.5 0.7 collective-permute-done.48.refs_6_
  182.0 2.7 %shard_map.58 = f32[32,1024]{1,0:T(8,128)} custom-call(f32[4,1,32,1024]{3,2,1,0:T(8,128)S(1)} %pad_maximum_fusion.3.refs_0_, f32[4,1,32,1024]{3,2,1,0:T(8,128)S(1)} %collective-permute-done.38.refs_1_, f32[4,1,32,1024]{3,2,1,0:T(8,128)S(1)} %collective-permute-done.39.refs_2_, f32[4,1,32,1024]{3,2,1,0:T(8,128)S(1)} %collective-permute-done.40.refs_3_, ...), custom_call_target="tpu_custom_call" | custom-call | flops 805306368 | bytes 8388608 | tf_op jit(solution)/shard_map/pallas_call | solution.py:156
  (72 shorter events, 8.0 us)
Async XLA Ops:
  1.6 6.2 %collective-permute-start.1 = (f32[1,32,1024]{2,1,0:T(8,128)S(1)}, f32[1,32,1024]{2,1,0:T(8,128)S(1)}, u32[]{:S(2)}, u32[]{:S(2)}) collective-permute-start(f32[1,32,1024]{2,1,0:T(8,128)S(1)} %constant_dynamic-slice_fusion), channel_id=1, source_target_pairs={{0,24},{1,7},{2,26},{3,1},{4,28},{5,3},{6,30},{7,5},{8,0},{9,15},{... | collective-permute-start | bytes 393224 | tf_op jit(solution)/shard_map/ppermute | solution.py:190
  5.2 6.7 %collective-permute-start = (f32[1,32,1024]{2,1,0:T(8,128)S(1)}, f32[1,32,1024]{2,1,0:T(8,128)S(1)}, u32[]{:S(2)}, u32[]{:S(2)}) collective-permute-start(f32[1,32,1024]{2,1,0:T(8,128)S(1)} %constant_dynamic-slice_fusion), channel_id=1, source_target_pairs={{0,8},{1,3},{2,10},{3,5},{4,12},{5,7},{6,14},{7,1},{8,16},{9,11},{... | collective-permute-start | bytes 393224 | tf_op jit(solution)/shard_map/ppermute | solution.py:190
  5.2 6.7 %collective-permute-start.2 = (f32[1,32,1024]{2,1,0:T(8,128)S(1)}, f32[1,32,1024]{2,1,0:T(8,128)S(1)}, u32[]{:S(2)}, u32[]{:S(2)}) collective-permute-start(f32[1,32,1024]{2,1,0:T(8,128)S(1)} %constant_dynamic-slice_fusion), channel_id=1, source_target_pairs={{0,16},{1,5},{2,18},{3,7},{4,20},{5,1},{6,22},{7,3},{8,24},{9,13},... | collective-permute-start | bytes 393224 | tf_op jit(solution)/shard_map/ppermute | solution.py:190
  12.0 10.0 %collective-permute-start.5 = (f32[4,1,32,1024]{3,2,1,0:T(8,128)S(1)}, f32[4,1,32,1024]{3,2,1,0:T(8,128)S(1)}, u32[]{:S(2)}, u32[]{:S(2)}) collective-permute-start(f32[4,1,32,1024]{3,2,1,0:T(8,128)S(1)} %pad_maximum_fusion.1.refs_0_), channel_id=1, source_target_pairs={{0,4},{1,17},{2,6},{3,19},{4,0},{5,21},{6,2},{7,23},{8,12},{9,25},... | collective-permute-start | bytes 1572872 | tf_op jit(solution)/shard_map/ppermute | solution.py:190
  14.5 13.1 %collective-permute-start.4 = (f32[4,1,32,1024]{3,2,1,0:T(8,128)S(1)}, f32[4,1,32,1024]{3,2,1,0:T(8,128)S(1)}, u32[]{:S(2)}, u32[]{:S(2)}) collective-permute-start(f32[4,1,32,1024]{3,2,1,0:T(8,128)S(1)} %pad_maximum_fusion.1.refs_0_), channel_id=1, source_target_pairs={{0,6},{1,25},{2,0},{3,27},{4,2},{5,29},{6,4},{7,31},{8,14},{9,1},{... | collective-permute-start | bytes 1572872 | tf_op jit(solution)/shard_map/ppermute | solution.py:190
  15.4 14.9 %collective-permute-start.3 = (f32[4,1,32,1024]{3,2,1,0:T(8,128)S(1)}, f32[4,1,32,1024]{3,2,1,0:T(8,128)S(1)}, u32[]{:S(2)}, u32[]{:S(2)}) collective-permute-start(f32[4,1,32,1024]{3,2,1,0:T(8,128)S(1)} %pad_maximum_fusion.1.refs_0_), channel_id=1, source_target_pairs={{0,2},{1,9},{2,4},{3,11},{4,6},{5,13},{6,0},{7,15},{8,10},{9,17},{... | collective-permute-start | bytes 1572872 | tf_op jit(solution)/shard_map/ppermute | solution.py:190
  16.0 16.1 %collective-permute-start.6 = (f32[4,1,32,1024]{3,2,1,0:T(8,128)S(1)}, f32[4,1,32,1024]{3,2,1,0:T(8,128)S(1)}, u32[]{:S(2)}, u32[]{:S(2)}) collective-permute-start(f32[4,1,32,1024]{3,2,1,0:T(8,128)S(1)} %pad_maximum_fusion.1.refs_0_), channel_id=1, source_target_pairs={{0,1},{1,0},{2,3},{3,2},{4,5},{5,4},{6,7},{7,6},{8,9},{9,8},{10,11... | collective-permute-start | bytes 1572872 | tf_op jit(solution)/shard_map/ppermute | solution.py:203
  21.9 10.1 %collective-permute-start.9 = (f32[4,1,32,1024]{3,2,1,0:T(8,128)S(1)}, f32[4,1,32,1024]{3,2,1,0:T(8,128)S(1)}, u32[]{:S(2)}, u32[]{:S(2)}) collective-permute-start(f32[4,1,32,1024]{3,2,1,0:T(8,128)S(1)} %collective-permute-done.5.refs_3_), channel_id=1, source_target_pairs={{0,1},{1,0},{2,3},{3,2},{4,5},{5,4},{6,7},{7,6},{8,9},{9,8},{10,11... | collective-permute-start | bytes 1572872 | tf_op jit(solution)/shard_map/ppermute | solution.py:203
  27.6 4.4 %collective-permute-start.8 = (f32[4,1,32,1024]{3,2,1,0:T(8,128)S(1)}, f32[4,1,32,1024]{3,2,1,0:T(8,128)}, u32[]{:S(2)}, u32[]{:S(2)}) collective-permute-start(f32[4,1,32,1024]{3,2,1,0:T(8,128)S(1)} %collective-permute-done.4.refs_2_), channel_id=1, source_target_pairs={{0,1},{1,0},{2,3},{3,2},{4,5},{5,4},{6,7},{7,6},{8,9},{9,8},{10,11... | collective-permute-start | bytes 1572872 | tf_op jit(solution)/shard_map/ppermute | solution.py:203
  30.3 2.4 %collective-permute-start.7 = (f32[4,1,32,1024]{3,2,1,0:T(8,128)S(1)}, f32[4,1,32,1024]{3,2,1,0:T(8,128)}, u32[]{:S(2)}, u32[]{:S(2)}) collective-permute-start(f32[4,1,32,1024]{3,2,1,0:T(8,128)S(1)} %collective-permute-done.3.refs_1_), channel_id=1, source_target_pairs={{0,1},{1,0},{2,3},{3,2},{4,5},{5,4},{6,7},{7,6},{8,9},{9,8},{10,11... | collective-permute-start | bytes 1572872 | tf_op jit(solution)/shard_map/ppermute | solution.py:203
  43.3 5.7 %collective-permute-start.12 = (f32[1,32,1024]{2,1,0:T(8,128)S(1)}, f32[1,32,1024]{2,1,0:T(8,128)S(1)}, u32[]{:S(2)}, u32[]{:S(2)}) collective-permute-start(f32[1,32,1024]{2,1,0:T(8,128)S(1)} %bitcast.39), channel_id=1, source_target_pairs={{0,16},{1,5},{2,18},{3,7},{4,20},{5,1},{6,22},{7,3},{8,24},{9,13},... | collective-permute-start | bytes 393224 | tf_op jit(solution)/shard_map/ppermute | solution.py:190
  45.3 5.1 %collective-permute-start.11 = (f32[1,32,1024]{2,1,0:T(8,128)S(1)}, f32[1,32,1024]{2,1,0:T(8,128)S(1)}, u32[]{:S(2)}, u32[]{:S(2)}) collective-permute-start(f32[1,32,1024]{2,1,0:T(8,128)S(1)} %bitcast.40), channel_id=1, source_target_pairs={{0,24},{1,7},{2,26},{3,1},{4,28},{5,3},{6,30},{7,5},{8,0},{9,15},{... | collective-permute-start | bytes 393224 | tf_op jit(solution)/shard_map/ppermute | solution.py:190
  46.7 5.2 %collective-permute-start.10 = (f32[1,32,1024]{2,1,0:T(8,128)S(1)}, f32[1,32,1024]{2,1,0:T(8,128)S(1)}, u32[]{:S(2)}, u32[]{:S(2)}) collective-permute-start(f32[1,32,1024]{2,1,0:T(8,128)S(1)} %bitcast.41), channel_id=1, source_target_pairs={{0,8},{1,3},{2,10},{3,5},{4,12},{5,7},{6,14},{7,1},{8,16},{9,11},{... | collective-permute-start | bytes 393224 | tf_op jit(solution)/shard_map/ppermute | solution.py:190
  46.7 10.8 %collective-permute-start.16 = (f32[32,1024]{1,0:T(8,128)S(1)}, f32[32,1024]{1,0:T(8,128)S(1)}, u32[]{:S(2)}, u32[]{:S(2)}) collective-permute-start(f32[32,1024]{1,0:T(8,128)S(1)} %get-tuple-element.25.refs_21_), channel_id=1, source_target_pairs={{0,32},{32,0},{64,96},{96,64},{1,33},{33,1},{65,97},{97,65},{2,34}... | collective-permute-start | bytes 393224 | tf_op jit(solution)/shard_map/ppermute | solution.py:246
  51.9 9.9 %collective-permute-start.17 = (f32[4,1,32,1024]{3,2,1,0:T(8,128)S(1)}, f32[4,1,32,1024]{3,2,1,0:T(8,128)S(1)}, u32[]{:S(2)}, u32[]{:S(2)}) collective-permute-start(f32[4,1,32,1024]{3,2,1,0:T(8,128)S(1)} %pad_maximum_fusion.2.refs_0_), channel_id=1, source_target_pairs={{0,4},{1,17},{2,6},{3,19},{4,0},{5,21},{6,2},{7,23},{8,12},{9,25},... | collective-permute-start | bytes 1572872 | tf_op jit(solution)/shard_map/ppermute | solution.py:190
  52.8 12.1 %collective-permute-start.15 = (f32[4,1,32,1024]{3,2,1,0:T(8,128)S(1)}, f32[4,1,32,1024]{3,2,1,0:T(8,128)S(1)}, u32[]{:S(2)}, u32[]{:S(2)}) collective-permute-start(f32[4,1,32,1024]{3,2,1,0:T(8,128)S(1)} %pad_maximum_fusion.2.refs_0_), channel_id=1, source_target_pairs={{0,32},{32,0},{64,96},{96,64},{1,33},{33,1},{65,97},{97,65},{2,34}... | collective-permute-start | bytes 1572872 | tf_op jit(solution)/shard_map/ppermute | solution.py:245
  54.4 12.9 %collective-permute-start.18 = (f32[4,1,32,1024]{3,2,1,0:T(8,128)S(1)}, f32[4,1,32,1024]{3,2,1,0:T(8,128)S(1)}, u32[]{:S(2)}, u32[]{:S(2)}) collective-permute-start(f32[4,1,32,1024]{3,2,1,0:T(8,128)S(1)} %pad_maximum_fusion.2.refs_0_), channel_id=1, source_target_pairs={{0,1},{1,0},{2,3},{3,2},{4,5},{5,4},{6,7},{7,6},{8,9},{9,8},{10,11... | collective-permute-start | bytes 1572872 | tf_op jit(solution)/shard_map/ppermute | solution.py:203
  56.4 13.1 %collective-permute-start.14 = (f32[4,1,32,1024]{3,2,1,0:T(8,128)S(1)}, f32[4,1,32,1024]{3,2,1,0:T(8,128)S(1)}, u32[]{:S(2)}, u32[]{:S(2)}) collective-permute-start(f32[4,1,32,1024]{3,2,1,0:T(8,128)S(1)} %pad_maximum_fusion.2.refs_0_), channel_id=1, source_target_pairs={{0,6},{1,25},{2,0},{3,27},{4,2},{5,29},{6,4},{7,31},{8,14},{9,1},{... | collective-permute-start | bytes 1572872 | tf_op jit(solution)/shard_map/ppermute | solution.py:190
  57.5 13.5 %collective-permute-start.13 = (f32[4,1,32,1024]{3,2,1,0:T(8,128)S(1)}, f32[4,1,32,1024]{3,2,1,0:T(8,128)S(1)}, u32[]{:S(2)}, u32[]{:S(2)}) collective-permute-start(f32[4,1,32,1024]{3,2,1,0:T(8,128)S(1)} %pad_maximum_fusion.2.refs_0_), channel_id=1, source_target_pairs={{0,2},{1,9},{2,4},{3,11},{4,6},{5,13},{6,0},{7,15},{8,10},{9,17},{... | collective-permute-start | bytes 1572872 | tf_op jit(solution)/shard_map/ppermute | solution.py:190
  64.8 6.2 %collective-permute-start.21 = (f32[4,1,32,1024]{3,2,1,0:T(8,128)S(1)}, f32[4,1,32,1024]{3,2,1,0:T(8,128)S(1)}, u32[]{:S(2)}, u32[]{:S(2)}) collective-permute-start(f32[4,1,32,1024]{3,2,1,0:T(8,128)S(1)} %collective-permute-done.17.refs_3_), channel_id=1, source_target_pairs={{0,1},{1,0},{2,3},{3,2},{4,5},{5,4},{6,7},{7,6},{8,9},{9,8},{10,11... | collective-permute-start | bytes 1572872 | tf_op jit(solution)/shard_map/ppermute | solution.py:203
  67.3 4.9 %collective-permute-start.25 = (f32[4,1,32,1024]{3,2,1,0:T(8,128)S(1)}, f32[4,1,32,1024]{3,2,1,0:T(8,128)S(1)}, u32[]{:S(2)}, u32[]{:S(2)}) collective-permute-start(f32[4,1,32,1024]{3,2,1,0:T(8,128)S(1)} %collective-permute-done.15.refs_8_), channel_id=1, source_target_pairs={{0,1},{1,0},{2,3},{3,2},{4,5},{5,4},{6,7},{7,6},{8,9},{9,8},{10,11... | collective-permute-start | bytes 1572872 | tf_op jit(solution)/shard_map/ppermute | solution.py:203
  67.3 10.0 %collective-permute-start.24 = (f32[4,1,32,1024]{3,2,1,0:T(8,128)S(1)}, f32[4,1,32,1024]{3,2,1,0:T(8,128)}, u32[]{:S(2)}, u32[]{:S(2)}) collective-permute-start(f32[4,1,32,1024]{3,2,1,0:T(8,128)S(1)} %collective-permute-done.15.refs_8_), channel_id=1, source_target_pairs={{0,4},{1,17},{2,6},{3,19},{4,0},{5,21},{6,2},{7,23},{8,12},{9,25},... | collective-permute-start | bytes 1572872 | tf_op jit(solution)/shard_map/ppermute | solution.py:190
  69.5 12.0 %collective-permute-start.23 = (f32[4,1,32,1024]{3,2,1,0:T(8,128)S(1)}, f32[4,1,32,1024]{3,2,1,0:T(8,128)}, u32[]{:S(2)}, u32[]{:S(2)}) collective-permute-start(f32[4,1,32,1024]{3,2,1,0:T(8,128)S(1)} %collective-permute-done.15.refs_8_), channel_id=1, source_target_pairs={{0,6},{1,25},{2,0},{3,27},{4,2},{5,29},{6,4},{7,31},{8,14},{9,1},{... | collective-permute-start | bytes 1572872 | tf_op jit(solution)/shard_map/ppermute | solution.py:190
  71.0 11.8 %collective-permute-start.22 = (f32[4,1,32,1024]{3,2,1,0:T(8,128)S(1)}, f32[4,1,32,1024]{3,2,1,0:T(8,128)}, u32[]{:S(2)}, u32[]{:S(2)}) collective-permute-start(f32[4,1,32,1024]{3,2,1,0:T(8,128)S(1)} %collective-permute-done.15.refs_8_), channel_id=1, source_target_pairs={{0,2},{1,9},{2,4},{3,11},{4,6},{5,13},{6,0},{7,15},{8,10},{9,17},{... | collective-permute-start | bytes 1572872 | tf_op jit(solution)/shard_map/ppermute | solution.py:190
  71.0 0.8 copy-start
  71.8 12.4 %collective-permute-start.20 = (f32[4,1,32,1024]{3,2,1,0:T(8,128)S(1)}, f32[4,1,32,1024]{3,2,1,0:T(8,128)}, u32[]{:S(2)}, u32[]{:S(2)}) collective-permute-start(f32[4,1,32,1024]{3,2,1,0:T(8,128)S(1)} %collective-permute-done.14.refs_2_), channel_id=1, source_target_pairs={{0,1},{1,0},{2,3},{3,2},{4,5},{5,4},{6,7},{7,6},{8,9},{9,8},{10,11... | collective-permute-start | bytes 1572872 | tf_op jit(solution)/shard_map/ppermute | solution.py:203
  72.2 0.8 copy-start.2
  73.0 11.3 %collective-permute-start.19 = (f32[4,1,32,1024]{3,2,1,0:T(8,128)S(1)}, f32[4,1,32,1024]{3,2,1,0:T(8,128)}, u32[]{:S(2)}, u32[]{:S(2)}) collective-permute-start(f32[4,1,32,1024]{3,2,1,0:T(8,128)S(1)} %collective-permute-done.13.refs_1_), channel_id=1, source_target_pairs={{0,1},{1,0},{2,3},{3,2},{4,5},{5,4},{6,7},{7,6},{8,9},{9,8},{10,11... | collective-permute-start | bytes 1572872 | tf_op jit(solution)/shard_map/ppermute | solution.py:203
  77.3 6.9 %collective-permute-start.28 = (f32[4,1,32,1024]{3,2,1,0:T(8,128)}, f32[4,1,32,1024]{3,2,1,0:T(8,128)}, u32[]{:S(2)}, u32[]{:S(2)}) collective-permute-start(f32[4,1,32,1024]{3,2,1,0:T(8,128)} %collective-permute-done.24.refs_11_), channel_id=1, source_target_pairs={{0,1},{1,0},{2,3},{3,2},{4,5},{5,4},{6,7},{7,6},{8,9},{9,8},{10,11... | collective-permute-start | bytes 1572872 | tf_op jit(solution)/shard_map/ppermute | solution.py:203
  81.5 2.9 %collective-permute-start.27 = (f32[4,1,32,1024]{3,2,1,0:T(8,128)}, f32[4,1,32,1024]{3,2,1,0:T(8,128)}, u32[]{:S(2)}, u32[]{:S(2)}) collective-permute-start(f32[4,1,32,1024]{3,2,1,0:T(8,128)} %collective-permute-done.23.refs_10_), channel_id=1, source_target_pairs={{0,1},{1,0},{2,3},{3,2},{4,5},{5,4},{6,7},{7,6},{8,9},{9,8},{10,11... | collective-permute-start | bytes 1572872 | tf_op jit(solution)/shard_map/ppermute | solution.py:203
  82.8 3.2 %collective-permute-start.26 = (f32[4,1,32,1024]{3,2,1,0:T(8,128)}, f32[4,1,32,1024]{3,2,1,0:T(8,128)}, u32[]{:S(2)}, u32[]{:S(2)}) collective-permute-start(f32[4,1,32,1024]{3,2,1,0:T(8,128)} %collective-permute-done.22.refs_9_), channel_id=1, source_target_pairs={{0,1},{1,0},{2,3},{3,2},{4,5},{5,4},{6,7},{7,6},{8,9},{9,8},{10,11... | collective-permute-start | bytes 1572872 | tf_op jit(solution)/shard_map/ppermute | solution.py:203
  86.1 1.0 copy-start.1
  87.1 1.0 copy-start.3
  108.8 7.1 %collective-permute-start.31 = (f32[32,1024]{1,0:T(8,128)S(1)}, f32[32,1024]{1,0:T(8,128)S(1)}, u32[]{:S(2)}, u32[]{:S(2)}) collective-permute-start(f32[32,1024]{1,0:T(8,128)S(1)} %get-tuple-element.34), channel_id=1, source_target_pairs={{0,64},{64,0},{32,96},{96,32},{1,65},{65,1},{33,97},{97,33},{2,66}... | collective-permute-start | bytes 393224 | tf_op jit(solution)/shard_map/ppermute | solution.py:254
  112.3 6.7 %collective-permute-start.30 = (f32[32,1024]{1,0:T(8,128)S(1)}, f32[32,1024]{1,0:T(8,128)S(1)}, u32[]{:S(2)}, u32[]{:S(2)}) collective-permute-start(f32[32,1024]{1,0:T(8,128)S(1)} %get-tuple-element.33.refs_11_), channel_id=1, source_target_pairs={{32,0},{64,96},{33,1},{65,97},{34,2},{66,98},{35,3},{67,99},{36,4}... | collective-permute-start | bytes 393224 | tf_op jit(solution)/shard_map/ppermute | solution.py:255
  113.6 5.4 %collective-permute-start.29 = (f32[32,1024]{1,0:T(8,128)S(1)}, f32[32,1024]{1,0:T(8,128)S(1)}, u32[]{:S(2)}, u32[]{:S(2)}) collective-permute-start(f32[32,1024]{1,0:T(8,128)S(1)} %get-tuple-element.33.refs_11_), channel_id=1, source_target_pairs={{32,64},{64,32},{33,65},{65,33},{34,66},{66,34},{35,67},{67,35},{3... | collective-permute-start | bytes 393224 | tf_op jit(solution)/shard_map/ppermute | solution.py:256
  119.0 8.5 %collective-permute-start.34 = (f32[3,32,1024]{2,1,0:T(8,128)S(1)}, f32[3,32,1024]{2,1,0:T(8,128)S(1)}, u32[]{:S(2)}, u32[]{:S(2)}) collective-permute-start(f32[3,32,1024]{2,1,0:T(8,128)S(1)} %pad_maximum_fusion.4), channel_id=1, source_target_pairs={{0,16},{1,5},{2,18},{3,7},{4,20},{5,1},{6,22},{7,3},{8,24},{9,13},... | collective-permute-start | bytes 1179656 | tf_op jit(solution)/shard_map/ppermute | solution.py:190
  120.1 10.8 %collective-permute-start.33 = (f32[3,32,1024]{2,1,0:T(8,128)S(1)}, f32[3,32,1024]{2,1,0:T(8,128)S(1)}, u32[]{:S(2)}, u32[]{:S(2)}) collective-permute-start(f32[3,32,1024]{2,1,0:T(8,128)S(1)} %pad_maximum_fusion.4), channel_id=1, source_target_pairs={{0,24},{1,7},{2,26},{3,1},{4,28},{5,3},{6,30},{7,5},{8,0},{9,15},{... | collective-permute-start | bytes 1179656 | tf_op jit(solution)/shard_map/ppermute | solution.py:190
  121.8 9.9 %collective-permute-start.32 = (f32[3,32,1024]{2,1,0:T(8,128)S(1)}, f32[3,32,1024]{2,1,0:T(8,128)S(1)}, u32[]{:S(2)}, u32[]{:S(2)}) collective-permute-start(f32[3,32,1024]{2,1,0:T(8,128)S(1)} %pad_maximum_fusion.4), channel_id=1, source_target_pairs={{0,8},{1,3},{2,10},{3,5},{4,12},{5,7},{6,14},{7,1},{8,16},{9,11},{... | collective-permute-start | bytes 1179656 | tf_op jit(solution)/shard_map/ppermute | solution.py:190
  131.9 15.6 %collective-permute-start.37 = (f32[4,2,32,1024]{3,2,1,0:T(8,128)S(1)}, f32[4,2,32,1024]{3,2,1,0:T(8,128)S(1)}, u32[]{:S(2)}, u32[]{:S(2)}) collective-permute-start(f32[4,2,32,1024]{3,2,1,0:T(8,128)S(1)} %pad_maximum_fusion.refs_0_), channel_id=1, source_target_pairs={{0,4},{1,17},{2,6},{3,19},{4,0},{5,21},{6,2},{7,23},{8,12},{9,25},... | collective-permute-start | bytes 3145736 | tf_op jit(solution)/shard_map/ppermute | solution.py:190
  133.9 23.5 %collective-permute-start.36 = (f32[4,2,32,1024]{3,2,1,0:T(8,128)S(1)}, f32[4,2,32,1024]{3,2,1,0:T(8,128)S(1)}, u32[]{:S(2)}, u32[]{:S(2)}) collective-permute-start(f32[4,2,32,1024]{3,2,1,0:T(8,128)S(1)} %pad_maximum_fusion.refs_0_), channel_id=1, source_target_pairs={{0,6},{1,25},{2,0},{3,27},{4,2},{5,29},{6,4},{7,31},{8,14},{9,1},{... | collective-permute-start | bytes 3145736 | tf_op jit(solution)/shard_map/ppermute | solution.py:190
  135.6 25.5 %collective-permute-start.35 = (f32[4,2,32,1024]{3,2,1,0:T(8,128)S(1)}, f32[4,2,32,1024]{3,2,1,0:T(8,128)S(1)}, u32[]{:S(2)}, u32[]{:S(2)}) collective-permute-start(f32[4,2,32,1024]{3,2,1,0:T(8,128)S(1)} %pad_maximum_fusion.refs_0_), channel_id=1, source_target_pairs={{0,2},{1,9},{2,4},{3,11},{4,6},{5,13},{6,0},{7,15},{8,10},{9,17},{... | collective-permute-start | bytes 3145736 | tf_op jit(solution)/shard_map/ppermute | solution.py:190
  135.6 26.2 %collective-permute-start.45 = (f32[32,1024]{1,0:T(8,128)S(1)}, f32[32,1024]{1,0:T(8,128)S(1)}, u32[]{:S(2)}, u32[]{:S(2)}) collective-permute-start(f32[32,1024]{1,0:T(8,128)S(1)} %get-tuple-element.37), channel_id=1, source_target_pairs={{32,0},{64,96},{33,1},{65,97},{34,2},{66,98},{35,3},{67,99},{36,4}... | collective-permute-start | bytes 393224 | tf_op jit(solution)/shard_map/ppermute | solution.py:261
  136.9 27.2 %collective-permute-start.41 = (f32[4,2,32,1024]{3,2,1,0:T(8,128)S(1)}, f32[4,2,32,1024]{3,2,1,0:T(8,128)S(1)}, u32[]{:S(2)}, u32[]{:S(2)}) collective-permute-start(f32[4,2,32,1024]{3,2,1,0:T(8,128)S(1)} %pad_maximum_fusion.refs_0_), channel_id=1, source_target_pairs={{0,1},{1,0},{2,3},{3,2},{4,5},{5,4},{6,7},{7,6},{8,9},{9,8},{10,11... | collective-permute-start | bytes 3145736 | tf_op jit(solution)/shard_map/ppermute | solution.py:203
  147.5 17.6 %collective-permute-start.44 = (f32[4,2,32,1024]{3,2,1,0:T(8,128)S(1)}, f32[4,2,32,1024]{3,2,1,0:T(8,128)S(1)}, u32[]{:S(2)}, u32[]{:S(2)}) collective-permute-start(f32[4,2,32,1024]{3,2,1,0:T(8,128)S(1)} %collective-permute-done.37.refs_3_), channel_id=1, source_target_pairs={{0,1},{1,0},{2,3},{3,2},{4,5},{5,4},{6,7},{7,6},{8,9},{9,8},{10,11... | collective-permute-start | bytes 3145736 | tf_op jit(solution)/shard_map/ppermute | solution.py:203
  157.3 8.3 %collective-permute-start.43 = (f32[4,2,32,1024]{3,2,1,0:T(8,128)S(1)}, f32[4,2,32,1024]{3,2,1,0:T(8,128)S(1)}, u32[]{:S(2)}, u32[]{:S(2)}) collective-permute-start(f32[4,2,32,1024]{3,2,1,0:T(8,128)S(1)} %collective-permute-done.36.refs_2_), channel_id=1, source_target_pairs={{0,1},{1,0},{2,3},{3,2},{4,5},{5,4},{6,7},{7,6},{8,9},{9,8},{10,11... | collective-permute-start | bytes 3145736 | tf_op jit(solution)/shard_map/ppermute | solution.py:203
  161.1 4.5 %collective-permute-start.42 = (f32[4,2,32,1024]{3,2,1,0:T(8,128)S(1)}, f32[4,2,32,1024]{3,2,1,0:T(8,128)S(1)}, u32[]{:S(2)}, u32[]{:S(2)}) collective-permute-start(f32[4,2,32,1024]{3,2,1,0:T(8,128)S(1)} %collective-permute-done.35.refs_1_), channel_id=1, source_target_pairs={{0,1},{1,0},{2,3},{3,2},{4,5},{5,4},{6,7},{7,6},{8,9},{9,8},{10,11... | collective-permute-start | bytes 3145736 | tf_op jit(solution)/shard_map/ppermute | solution.py:203
  161.8 14.2 %collective-permute-start.40 = (f32[4,1,32,1024]{3,2,1,0:T(8,128)S(1)}, f32[4,1,32,1024]{3,2,1,0:T(8,128)S(1)}, u32[]{:S(2)}, u32[]{:S(2)}) collective-permute-start(f32[4,1,32,1024]{3,2,1,0:T(8,128)S(1)} %pad_maximum_fusion.3.refs_0_), channel_id=1, source_target_pairs={{0,4},{1,17},{2,6},{3,19},{4,0},{5,21},{6,2},{7,23},{8,12},{9,25},... | collective-permute-start | bytes 1572872 | tf_op jit(solution)/shard_map/ppermute | solution.py:190
  164.1 12.0 %collective-permute-start.39 = (f32[4,1,32,1024]{3,2,1,0:T(8,128)S(1)}, f32[4,1,32,1024]{3,2,1,0:T(8,128)S(1)}, u32[]{:S(2)}, u32[]{:S(2)}) collective-permute-start(f32[4,1,32,1024]{3,2,1,0:T(8,128)S(1)} %pad_maximum_fusion.3.refs_0_), channel_id=1, source_target_pairs={{0,6},{1,25},{2,0},{3,27},{4,2},{5,29},{6,4},{7,31},{8,14},{9,1},{... | collective-permute-start | bytes 1572872 | tf_op jit(solution)/shard_map/ppermute | solution.py:190
  165.0 12.3 %collective-permute-start.38 = (f32[4,1,32,1024]{3,2,1,0:T(8,128)S(1)}, f32[4,1,32,1024]{3,2,1,0:T(8,128)S(1)}, u32[]{:S(2)}, u32[]{:S(2)}) collective-permute-start(f32[4,1,32,1024]{3,2,1,0:T(8,128)S(1)} %pad_maximum_fusion.3.refs_0_), channel_id=1, source_target_pairs={{0,2},{1,9},{2,4},{3,11},{4,6},{5,13},{6,0},{7,15},{8,10},{9,17},{... | collective-permute-start | bytes 1572872 | tf_op jit(solution)/shard_map/ppermute | solution.py:190
  177.3 2.4 %collective-permute-start.46 = (f32[4,1,32,1024]{3,2,1,0:T(8,128)S(1)}, f32[4,1,32,1024]{3,2,1,0:T(8,128)S(1)}, u32[]{:S(2)}, u32[]{:S(2)}) collective-permute-start(f32[4,1,32,1024]{3,2,1,0:T(8,128)S(1)} %pad_maximum_fusion.3.refs_0_), channel_id=1, source_target_pairs={{0,1},{1,0},{2,3},{3,2},{4,5},{5,4},{6,7},{7,6},{8,9},{9,8},{10,11... | collective-permute-start | bytes 1572872 | tf_op jit(solution)/shard_map/ppermute | solution.py:203
  178.2 2.3 %collective-permute-start.47 = (f32[4,1,32,1024]{3,2,1,0:T(8,128)S(1)}, f32[4,1,32,1024]{3,2,1,0:T(8,128)S(1)}, u32[]{:S(2)}, u32[]{:S(2)}) collective-permute-start(f32[4,1,32,1024]{3,2,1,0:T(8,128)S(1)} %collective-permute-done.38.refs_1_), channel_id=1, source_target_pairs={{0,1},{1,0},{2,3},{3,2},{4,5},{5,4},{6,7},{7,6},{8,9},{9,8},{10,11... | collective-permute-start | bytes 1572872 | tf_op jit(solution)/shard_map/ppermute | solution.py:203
  178.2 3.0 %collective-permute-start.48 = (f32[4,1,32,1024]{3,2,1,0:T(8,128)S(1)}, f32[4,1,32,1024]{3,2,1,0:T(8,128)S(1)}, u32[]{:S(2)}, u32[]{:S(2)}) collective-permute-start(f32[4,1,32,1024]{3,2,1,0:T(8,128)S(1)} %collective-permute-done.39.refs_2_), channel_id=1, source_target_pairs={{0,1},{1,0},{2,3},{3,2},{4,5},{5,4},{6,7},{7,6},{8,9},{9,8},{10,11... | collective-permute-start | bytes 1572872 | tf_op jit(solution)/shard_map/ppermute | solution.py:203
  178.7 3.3 %collective-permute-start.49 = (f32[4,1,32,1024]{3,2,1,0:T(8,128)S(1)}, f32[4,1,32,1024]{3,2,1,0:T(8,128)S(1)}, u32[]{:S(2)}, u32[]{:S(2)}) collective-permute-start(f32[4,1,32,1024]{3,2,1,0:T(8,128)S(1)} %collective-permute-done.40.refs_3_), channel_id=1, source_target_pairs={{0,1},{1,0},{2,3},{3,2},{4,5},{5,4},{6,7},{7,6},{8,9},{9,8},{10,11... | collective-permute-start | bytes 1572872 | tf_op jit(solution)/shard_map/ppermute | solution.py:203

commit v4 on v3

--- a/solution.py
+++ b/solution.py
@@ -11,6 +11,7 @@
 SIDE = 4
 STEPS = (1, 3, 2)
 PIECES = 2 * SIDE
+FEW_ROWS = 32
 MATRIX_BYTES = 4 * 1024 * 1024
 
 
@@ -25,16 +26,20 @@
     high, low = halves(rows)
     both = jnp.concatenate([high, low], axis=0)
     by_high = jnp.dot(both, high_ref[...], preferred_element_type=jnp.float32)
-    by_low = jnp.dot(high, low_ref[...], preferred_element_type=jnp.float32)
+    by_low = jnp.dot(both if count > FEW_ROWS else high, low_ref[...], preferred_element_type=jnp.float32)
+    if count > FEW_ROWS:
+        done = by_high + by_low
+        return done[:count] + done[count:]
     return by_high[:count] + (by_high[count:] + by_low)
 
 
 def split(pieces, places, high_ref, low_ref):
-    lines, slots, panel_rows, _ = pieces[0].shape
-    for i, piece in enumerate(pieces):
-
-        def body(j, carry, i=i, piece=piece):
-            rows = pl.ds(pl.multiple_of(places[i * lines + j] * panel_rows, panel_rows), panel_rows)
+    before = 0
+    for piece in pieces:
+        lines, slots, panel_rows, _ = piece.shape
+
+        def body(j, carry, before=before, piece=piece):
+            rows = pl.ds(pl.multiple_of(places[before + j] * panel_rows, panel_rows), panel_rows)
             for slot in range(slots):
                 high, low = halves(piece[j, slot])
                 high_ref[slot, rows, :] = high
@@ -42,6 +47,7 @@
             return carry
 
         lax.fori_loop(0, lines, body, 0)
+        before += lines
 
 
 def layer_kernel(*refs):
@@ -124,10 +130,10 @@
 
 def last_chain(*refs):
     pieces, refs = refs[:PIECES], refs[PIECES:]
-    places, inner, start, out, high, low = refs
+    places, inner, own_trans, near_trans, out, high, low = refs
     split(pieces, places, high, low)
     first, second = 1 - inner[0], inner[0]
-    term = start[...]
+    term = jnp.where(inner[0] == 1, own_trans[...], near_trans[...])
     half = product(term, high.at[first], low.at[first])
 
     def body(k, carry):
@@ -141,11 +147,23 @@
 
 
 def last_close(*refs):
-    pieces, refs = refs[:PIECES], refs[PIECES:]
-    places, inner, summed, own_refl, out, high, low = refs
+    pieces, refs = refs[:SIDE], refs[SIDE:]
+    places, summed, oth_summed, own_out, oth_out, high, low = refs
     split(pieces, places, high, low)
-    base = jnp.where(inner[0] == 1, 0.0, own_refl[...])
-    out[...] = base + product(summed[...], high.at[0], low.at[0])
+    rows, order = summed.shape
+    empty = jnp.zeros((rows, order), jnp.bfloat16)
+
+    def clear(j, carry):
+        part = pl.ds(pl.multiple_of(places[SIDE * SIDE + j] * rows, rows), rows)
+        high[0, part, :] = empty
+        low[0, part, :] = empty
+        return carry
+
+    lax.fori_loop(0, SIDE * SIDE, clear, 0)
+    both = jnp.concatenate([summed[...], oth_summed[...]], axis=0)
+    done = product(both, high.at[0], low.at[0])
+    own_out[...] = done[:rows]
+    oth_out[...] = done[rows:]
 
 
 def call(kernel, room, steps, outs, pieces, tables, small, far=(), scratch=(), placed=True):
@@ -198,9 +216,12 @@
     return [line] + [moved(line, 1, step) for step in STEPS]
 
 
+def other_core(block):
+    return lax.ppermute(block, "panel", [(i, i ^ 1) for i in range(2 * SIDE * SIDE)])
+
+
 def flipped(pieces):
-    flip = [(i, i ^ 1) for i in range(2 * SIDE * SIDE)]
-    return pieces + [lax.ppermute(piece, "panel", flip) for piece in pieces]
+    return pieces + [other_core(piece) for piece in pieces]
 
 
 def places_of(panel):
@@ -213,11 +234,6 @@
         along_y = panel_of(x - outer + SIDE, y - inner + SIDE, 1)
         found.append(jnp.where(owner == 0, along_x, along_y).reshape(-1))
     return jnp.concatenate(found)
-
-
-def after(pieces, value):
-    *pieces, value = lax.optimization_barrier((*pieces, value))
-    return flipped(pieces), value
 
 
 def local(reflections, wave_decay, thickness, material):
@@ -264,14 +280,14 @@
     rest = jnp.stack([part[2:] for part in line])
     rest, *_ = lax.optimization_barrier((rest, *mine[1:]))
     rest = spread(rest)
-    start = jnp.where(inner, trans, near_trans)
     (summed,) = call(
-        last_chain, 12, 2 * TERMS, (block,), flipped(mine), (places, inner_flag), (start,), scratch=matrices(2, order)
-    )
-    closing, summed = after(rest, summed)
-    (out,) = call(
-        last_close, 10, 2, (block,), closing, (places, inner_flag), (summed, refl), scratch=matrices(1, order), placed=False
-    )
+        last_chain, 12, 2 * TERMS, (block,), flipped(mine), (places, inner_flag), (trans, near_trans), scratch=matrices(2, order)
+    )
+    *rest, summed = lax.optimization_barrier((*rest, summed))
+    own_part, oth_part = call(
+        last_close, 10, 2, (block, block), rest, (places,), (summed, other_core(summed)), scratch=matrices(1, order)
+    )
+    out = jnp.where(inner, 0.0, refl) + (own_part + other_core(oth_part))
     return out[None]
 
 

time: 186 us -> 183 us (0.984)
  Pallas kernels: 44.3 us -> 42.3 us
    pallas_call x4, Pallas kernels: 44.3 us -> 42.3 us  [call(): pl.pallas_call(kernel, out_shape=tuple((out if placed else jax.ShapeDtype...]
    ppermute x20 -> x18, waiting for transfers between devices: 5.85 us -> 4.55 us  [other_core(): lax.ppermute(block, 'panel', [(i, i ^ 1) for i in range(2 * SIDE * SIDE)])]
    ppermute x20 -> x18, starting transfers between devices: 27.6 us -> 27.5 us  [other_core(): lax.ppermute(block, 'panel', [(i, i ^ 1) for i in range(2 * SIDE * SIDE)])]
  transfers between devices with their start and end apart: 50 -> 48, of which waited for: 26 -> 25; matrix products, arithmetic and copies ran while one was open for 1% -> 1% of each run, Pallas kernels for 6% -> 6%
where the time goes in v4:
time: 183 us; the launch traced here: 182 us
  starting transfers between devices  66.5 us (36%)
  waiting for transfers between devices  64 us (35%)
  Pallas kernels  42.3 us (23%)
  local copies, waits for them, and re-layouts  5.78 us (3%)
  other arithmetic  1.84 us (1%)
    ppermute x24, waiting for transfers between devices, moved(): return lax.ppermute(block, 'panel', route)  51.8 us
    pallas_call x4, Pallas kernels, call(): pl.pallas_call(kernel, out_shape=tuple((out if placed else jax.ShapeDtype...  42.3 us
    ppermute x24, starting transfers between devices, moved(): return lax.ppermute(block, 'panel', route)  29 us
    ppermute x18, starting transfers between devices, other_core(): lax.ppermute(block, 'panel', [(i, i ^ 1) for i in range(2 * SIDE * SIDE)])  27.5 us
    ppermute x18, waiting for transfers between devices, other_core(): lax.ppermute(block, 'panel', [(i, i ^ 1) for i in range(2 * SIDE * SIDE)])  4.55 us
    unnamed x8, local copies, waits for them, and re-layouts  3.67 us
  transfers between devices with their start and end apart: 48, of which 25 were waited for; matrix products, arithmetic and copies ran while one was open for 1% of the time, Pallas kernels for 6%

profile of v4, /device:TPU:1, one launch (start us, length us, event | category | flops | bytes accessed | tf_op | source)
XLA Modules:
  0.0 182.0 jit_solution(1151586929014543386)
XLA Ops:
  0.7 0.9 constant_dynamic-slice_fusion
  1.6 3.6 %collective-permute-start.1 = (f32[1,32,1024]{2,1,0:T(8,128)S(1)}, f32[1,32,1024]{2,1,0:T(8,128)S(1)}, u32[]{:S(2)}, u32[]{:S(2)}) collective-permute-start(f32[1,32,1024]{2,1,0:T(8,128)S(1)} %constant_dynamic-slice_fusion), channel_id=1, source_target_pairs={{0,24},{1,7},{2,26},{3,1},{4,28},{5,3},{6,30},{7,5},{8,0},{9,15},{... | collective-permute-start | bytes 393224 | tf_op jit(solution)/shard_map/ppermute | solution.py:208
  5.2 1.6 collective-permute-start.2
  6.9 0.9 fusion.5
  7.8 4.2 %collective-permute-done = f32[1,32,1024]{2,1,0:T(8,128)S(1)} collective-permute-done((f32[1,32,1024]{2,1,0:T(8,128)S(1)}, f32[1,32,1024]{2,1,0:T(8,128)S(1)}, u32[]{:S(2)}, u32[]{:S(2)}) %collective-permute-start) | collective-permute-done | bytes 131104 | tf_op jit(solution)/shard_map/ppermute | solution.py:208
  12.0 2.5 %collective-permute-start.5 = (f32[4,1,32,1024]{3,2,1,0:T(8,128)S(1)}, f32[4,1,32,1024]{3,2,1,0:T(8,128)S(1)}, u32[]{:S(2)}, u32[]{:S(2)}) collective-permute-start(f32[4,1,32,1024]{3,2,1,0:T(8,128)S(1)} %pad_maximum_fusion.1.refs_0_), channel_id=1, source_target_pairs={{0,4},{1,17},{2,6},{3,19},{4,0},{5,21},{6,2},{7,23},{8,12},{9,25},... | collective-permute-start | bytes 1572872 | tf_op jit(solution)/shard_map/ppermute | solution.py:208
  14.5 0.9 collective-permute-start.4
  16.0 2.9 %collective-permute-start.6 = (f32[4,1,32,1024]{3,2,1,0:T(8,128)S(1)}, f32[4,1,32,1024]{3,2,1,0:T(8,128)S(1)}, u32[]{:S(2)}, u32[]{:S(2)}) collective-permute-start(f32[4,1,32,1024]{3,2,1,0:T(8,128)S(1)} %pad_maximum_fusion.1.refs_0_), channel_id=1, source_target_pairs={{0,1},{1,0},{2,3},{3,2},{4,5},{5,4},{6,7},{7,6},{8,9},{9,8},{10,11... | collective-permute-start | bytes 1572872 | tf_op jit(solution)/shard_map/ppermute | solution.py:220
  18.8 3.1 %collective-permute-done.5.refs_3_ = f32[4,1,32,1024]{3,2,1,0:T(8,128)S(1)} collective-permute-done((f32[4,1,32,1024]{3,2,1,0:T(8,128)S(1)}, f32[4,1,32,1024]{3,2,1,0:T(8,128)S(1)}, u32[]{:S(2)}, u32[]{:S(2)}) %collective-permute-start.5) | collective-permute-done | bytes 524320 | tf_op jit(solution)/shard_map/ppermute | solution.py:208
  21.9 2.5 %collective-permute-start.9 = (f32[4,1,32,1024]{3,2,1,0:T(8,128)S(1)}, f32[4,1,32,1024]{3,2,1,0:T(8,128)S(1)}, u32[]{:S(2)}, u32[]{:S(2)}) collective-permute-start(f32[4,1,32,1024]{3,2,1,0:T(8,128)S(1)} %collective-permute-done.5.refs_3_), channel_id=1, source_target_pairs={{0,1},{1,0},{2,3},{3,2},{4,5},{5,4},{6,7},{7,6},{8,9},{9,8},{10,11... | collective-permute-start | bytes 1572872 | tf_op jit(solution)/shard_map/ppermute | solution.py:220
  24.4 3.2 %collective-permute-done.4.refs_2_ = f32[4,1,32,1024]{3,2,1,0:T(8,128)S(1)} collective-permute-done((f32[4,1,32,1024]{3,2,1,0:T(8,128)S(1)}, f32[4,1,32,1024]{3,2,1,0:T(8,128)S(1)}, u32[]{:S(2)}, u32[]{:S(2)}) %collective-permute-start.4) | collective-permute-done | bytes 524320 | tf_op jit(solution)/shard_map/ppermute | solution.py:208
  27.6 2.7 %collective-permute-start.8 = (f32[4,1,32,1024]{3,2,1,0:T(8,128)S(1)}, f32[4,1,32,1024]{3,2,1,0:T(8,128)}, u32[]{:S(2)}, u32[]{:S(2)}) collective-permute-start(f32[4,1,32,1024]{3,2,1,0:T(8,128)S(1)} %collective-permute-done.4.refs_2_), channel_id=1, source_target_pairs={{0,1},{1,0},{2,3},{3,2},{4,5},{5,4},{6,7},{7,6},{8,9},{9,8},{10,11... | collective-permute-start | bytes 1572872 | tf_op jit(solution)/shard_map/ppermute | solution.py:220
  32.7 10.5 %shard_map.55 = (f32[32,1024]{1,0:T(8,128)S(1)}, f32[32,1024]{1,0:T(8,128)S(1)}, f32[1,1024]{1,0:T(1,128)S(1)}, bf16[1,1024,1024]{2,1,0:T(8,128)(2,1)}, bf16[1,1024,1024]{2,1,0:T(8,128)(2,1)}) custom-call(f32[4,1,32,1024]{3,2,1,0:T(8,128)S(1)} %pad_maximum_fusion.1.refs_0_, f32[4,1,32,1024]{3,2,1,0:T(8,128)S(1)} %collective-permute-done.3.refs_1_, ...), custom_call_target="tpu_custom_call" | custom-call | flops 4831838208 | bytes 50331648 | tf_op jit(solution)/shard_map/pallas_call | solution.py:174
  43.3 1.9 %collective-permute-start.12 = (f32[1,32,1024]{2,1,0:T(8,128)S(1)}, f32[1,32,1024]{2,1,0:T(8,128)S(1)}, u32[]{:S(2)}, u32[]{:S(2)}) collective-permute-start(f32[1,32,1024]{2,1,0:T(8,128)S(1)} %bitcast.40), channel_id=1, source_target_pairs={{0,16},{1,5},{2,18},{3,7},{4,20},{5,1},{6,22},{7,3},{8,24},{9,13},... | collective-permute-start | bytes 393224 | tf_op jit(solution)/shard_map/ppermute | solution.py:208
  45.2 1.4 collective-permute-start.11
  46.7 1.6 collective-permute-start.16
  49.0 1.4 collective-permute-done.11
  50.3 1.5 collective-permute-done.10
  51.9 0.8 collective-permute-start.17
  52.7 1.6 collective-permute-start.15
  54.3 2.0 %collective-permute-start.18 = (f32[4,1,32,1024]{3,2,1,0:T(8,128)S(1)}, f32[4,1,32,1024]{3,2,1,0:T(8,128)S(1)}, u32[]{:S(2)}, u32[]{:S(2)}) collective-permute-start(f32[4,1,32,1024]{3,2,1,0:T(8,128)S(1)} %pad_maximum_fusion.2.refs_0_), channel_id=1, source_target_pairs={{0,1},{1,0},{2,3},{3,2},{4,5},{5,4},{6,7},{7,6},{8,9},{9,8},{10,11... | collective-permute-start | bytes 1572872 | tf_op jit(solution)/shard_map/ppermute | solution.py:220
  56.3 1.1 collective-permute-start.14
  57.8 4.0 %collective-permute-done.17.refs_3_ = f32[4,1,32,1024]{3,2,1,0:T(8,128)S(1)} collective-permute-done((f32[4,1,32,1024]{3,2,1,0:T(8,128)S(1)}, f32[4,1,32,1024]{3,2,1,0:T(8,128)S(1)}, u32[]{:S(2)}, u32[]{:S(2)}) %collective-permute-start.17) | collective-permute-done | bytes 524320 | tf_op jit(solution)/shard_map/ppermute | solution.py:208
  61.8 3.0 %collective-permute-done.15.refs_8_ = f32[4,1,32,1024]{3,2,1,0:T(8,128)S(1)} collective-permute-done((f32[4,1,32,1024]{3,2,1,0:T(8,128)S(1)}, f32[4,1,32,1024]{3,2,1,0:T(8,128)S(1)}, u32[]{:S(2)}, u32[]{:S(2)}) %collective-permute-start.15) | collective-permute-done | bytes 524320 | tf_op jit(solution)/shard_map/ppermute | solution.py:261
  64.8 2.5 %collective-permute-start.21 = (f32[4,1,32,1024]{3,2,1,0:T(8,128)S(1)}, f32[4,1,32,1024]{3,2,1,0:T(8,128)S(1)}, u32[]{:S(2)}, u32[]{:S(2)}) collective-permute-start(f32[4,1,32,1024]{3,2,1,0:T(8,128)S(1)} %collective-permute-done.17.refs_3_), channel_id=1, source_target_pairs={{0,1},{1,0},{2,3},{3,2},{4,5},{5,4},{6,7},{7,6},{8,9},{9,8},{10,11... | collective-permute-start | bytes 1572872 | tf_op jit(solution)/shard_map/ppermute | solution.py:220
  67.2 2.2 %collective-permute-start.24 = (f32[4,1,32,1024]{3,2,1,0:T(8,128)S(1)}, f32[4,1,32,1024]{3,2,1,0:T(8,128)}, u32[]{:S(2)}, u32[]{:S(2)}) collective-permute-start(f32[4,1,32,1024]{3,2,1,0:T(8,128)S(1)} %collective-permute-done.15.refs_8_), channel_id=1, source_target_pairs={{0,4},{1,17},{2,6},{3,19},{4,0},{5,21},{6,2},{7,23},{8,12},{9,25},... | collective-permute-start | bytes 1572872 | tf_op jit(solution)/shard_map/ppermute | solution.py:208
  69.4 1.5 collective-permute-start.23
  71.0 0.8 copy-done
  72.1 0.8 copy-done.2
  73.1 4.1 %collective-permute-done.24.refs_11_ = f32[4,1,32,1024]{3,2,1,0:T(8,128)} collective-permute-done((f32[4,1,32,1024]{3,2,1,0:T(8,128)S(1)}, f32[4,1,32,1024]{3,2,1,0:T(8,128)}, u32[]{:S(2)}, u32[]{:S(2)}) %collective-permute-start.24) | collective-permute-done | bytes 524320 | tf_op jit(solution)/shard_map/ppermute | solution.py:208
  77.2 1.4 collective-permute-start.28
  78.6 2.9 %collective-permute-done.23.refs_10_ = f32[4,1,32,1024]{3,2,1,0:T(8,128)} collective-permute-done((f32[4,1,32,1024]{3,2,1,0:T(8,128)S(1)}, f32[4,1,32,1024]{3,2,1,0:T(8,128)}, u32[]{:S(2)}, u32[]{:S(2)}) %collective-permute-start.23) | collective-permute-done | bytes 524320 | tf_op jit(solution)/shard_map/ppermute | solution.py:208
  81.5 1.1 collective-permute-start.27
  82.8 1.4 collective-permute-start.26
  84.4 1.6 collective-permute-done.26.refs_13_
  86.0 1.0 copy-done.1
  87.1 1.0 copy-done.3
  88.1 19.6 %shard_map.56 = (f32[32,1024]{1,0:T(8,128)S(1)}, f32[32,1024]{1,0:T(8,128)S(1)}, f32[32,1024]{1,0:T(8,128)S(1)}) custom-call(f32[4,1,32,1024]{3,2,1,0:T(8,128)S(1)} %pad_maximum_fusion.2.refs_0_, f32[4,1,32,1024]{3,2,1,0:T(8,128)S(1)} %collective-permute-done.13.refs_1_, f32[4,1,32,1024]{3,2,1,0:T(8,128)S(1)} %collective-permute-done.14.refs_2_, ...), custom_call_target="tpu_custom_call" | custom-call | flops 9663676416 | bytes 100663296 | tf_op jit(solution)/shard_map/pallas_call | solution.py:174
  107.7 3.5 %collective-permute-start.31 = (f32[32,1024]{1,0:T(8,128)S(1)}, f32[32,1024]{1,0:T(8,128)S(1)}, u32[]{:S(2)}, u32[]{:S(2)}) collective-permute-start(f32[32,1024]{1,0:T(8,128)S(1)} %get-tuple-element.36), channel_id=1, source_target_pairs={{0,64},{64,0},{32,96},{96,32},{1,65},{65,1},{33,97},{97,33},{2,66}... | collective-permute-start | bytes 393224 | tf_op jit(solution)/shard_map/ppermute | solution.py:270
  111.2 1.3 collective-permute-start.30
  113.2 1.6 collective-permute-done.31
  114.8 3.1 %collective-permute-done.30 = f32[32,1024]{1,0:T(8,128)S(1)} collective-permute-done((f32[32,1024]{1,0:T(8,128)S(1)}, f32[32,1024]{1,0:T(8,128)S(1)}, u32[]{:S(2)}, u32[]{:S(2)}) %collective-permute-start.30) | collective-permute-done | bytes 131104 | tf_op jit(solution)/shard_map/ppermute | solution.py:271
  117.9 1.1 collective-permute-start.34
  119.0 1.8 collective-permute-start.33
  120.8 5.7 %collective-permute-done.34 = f32[3,32,1024]{2,1,0:T(8,128)S(1)} collective-permute-done((f32[3,32,1024]{2,1,0:T(8,128)S(1)}, f32[3,32,1024]{2,1,0:T(8,128)S(1)}, u32[]{:S(2)}, u32[]{:S(2)}) %collective-permute-start.34) | collective-permute-done | bytes 393248 | tf_op jit(solution)/shard_map/ppermute | solution.py:208
  126.5 3.3 %collective-permute-done.33 = f32[3,32,1024]{2,1,0:T(8,128)S(1)} collective-permute-done((f32[3,32,1024]{2,1,0:T(8,128)S(1)}, f32[3,32,1024]{2,1,0:T(8,128)S(1)}, u32[]{:S(2)}, u32[]{:S(2)}) %collective-permute-start.33) | collective-permute-done | bytes 393248 | tf_op jit(solution)/shard_map/ppermute | solution.py:208
  129.8 0.8 collective-permute-done.32
  130.7 2.0 %collective-permute-start.37 = (f32[4,2,32,1024]{3,2,1,0:T(8,128)S(1)}, f32[4,2,32,1024]{3,2,1,0:T(8,128)S(1)}, u32[]{:S(2)}, u32[]{:S(2)}) collective-permute-start(f32[4,2,32,1024]{3,2,1,0:T(8,128)S(1)} %pad_maximum_fusion.refs_0_), channel_id=1, source_target_pairs={{0,4},{1,17},{2,6},{3,19},{4,0},{5,21},{6,2},{7,23},{8,12},{9,25},... | collective-permute-start | bytes 3145736 | tf_op jit(solution)/shard_map/ppermute | solution.py:208
  132.7 1.7 collective-permute-start.36
  134.5 1.3 collective-permute-start.45
  135.7 1.9 %collective-permute-start.41 = (f32[4,2,32,1024]{3,2,1,0:T(8,128)S(1)}, f32[4,2,32,1024]{3,2,1,0:T(8,128)S(1)}, u32[]{:S(2)}, u32[]{:S(2)}) collective-permute-start(f32[4,2,32,1024]{3,2,1,0:T(8,128)S(1)} %pad_maximum_fusion.refs_0_), channel_id=1, source_target_pairs={{0,1},{1,0},{2,3},{3,2},{4,5},{5,4},{6,7},{7,6},{8,9},{9,8},{10,11... | collective-permute-start | bytes 3145736 | tf_op jit(solution)/shard_map/ppermute | solution.py:220
  137.7 8.6 %collective-permute-done.37.refs_3_ = f32[4,2,32,1024]{3,2,1,0:T(8,128)S(1)} collective-permute-done((f32[4,2,32,1024]{3,2,1,0:T(8,128)S(1)}, f32[4,2,32,1024]{3,2,1,0:T(8,128)S(1)}, u32[]{:S(2)}, u32[]{:S(2)}) %collective-permute-start.37) | collective-permute-done | bytes 1048608 | tf_op jit(solution)/shard_map/ppermute | solution.py:208
  146.3 3.1 %collective-permute-start.44 = (f32[4,2,32,1024]{3,2,1,0:T(8,128)S(1)}, f32[4,2,32,1024]{3,2,1,0:T(8,128)S(1)}, u32[]{:S(2)}, u32[]{:S(2)}) collective-permute-start(f32[4,2,32,1024]{3,2,1,0:T(8,128)S(1)} %collective-permute-done.37.refs_3_), channel_id=1, source_target_pairs={{0,1},{1,0},{2,3},{3,2},{4,5},{5,4},{6,7},{7,6},{8,9},{9,8},{10,11... | collective-permute-start | bytes 3145736 | tf_op jit(solution)/shard_map/ppermute | solution.py:220
  149.4 6.8 %collective-permute-done.36.refs_2_ = f32[4,2,32,1024]{3,2,1,0:T(8,128)S(1)} collective-permute-done((f32[4,2,32,1024]{3,2,1,0:T(8,128)S(1)}, f32[4,2,32,1024]{3,2,1,0:T(8,128)S(1)}, u32[]{:S(2)}, u32[]{:S(2)}) %collective-permute-start.36) | collective-permute-done | bytes 1048608 | tf_op jit(solution)/shard_map/ppermute | solution.py:208
  156.2 3.8 %collective-permute-start.43 = (f32[4,2,32,1024]{3,2,1,0:T(8,128)S(1)}, f32[4,2,32,1024]{3,2,1,0:T(8,128)S(1)}, u32[]{:S(2)}, u32[]{:S(2)}) collective-permute-start(f32[4,2,32,1024]{3,2,1,0:T(8,128)S(1)} %collective-permute-done.36.refs_2_), channel_id=1, source_target_pairs={{0,1},{1,0},{2,3},{3,2},{4,5},{5,4},{6,7},{7,6},{8,9},{9,8},{10,11... | collective-permute-start | bytes 3145736 | tf_op jit(solution)/shard_map/ppermute | solution.py:220
  160.7 2.3 %collective-permute-start.40 = (f32[4,1,32,1024]{3,2,1,0:T(8,128)S(1)}, f32[4,1,32,1024]{3,2,1,0:T(8,128)S(1)}, u32[]{:S(2)}, u32[]{:S(2)}) collective-permute-start(f32[4,1,32,1024]{3,2,1,0:T(8,128)S(1)} %pad_maximum_fusion.3.refs_0_), channel_id=1, source_target_pairs={{0,4},{1,17},{2,6},{3,19},{4,0},{5,21},{6,2},{7,23},{8,12},{9,25},... | collective-permute-start | bytes 1572872 | tf_op jit(solution)/shard_map/ppermute | solution.py:208
  163.0 0.9 collective-permute-start.39
  164.4 10.4 %shard_map.57.refs_5_ = f32[32,1024]{1,0:T(8,128)S(1)} custom-call(f32[4,2,32,1024]{3,2,1,0:T(8,128)S(1)} %pad_maximum_fusion.refs_0_, f32[4,2,32,1024]{3,2,1,0:T(8,128)S(1)} %collective-permute-done.35.refs_1_, f32[4,2,32,1024]{3,2,1,0:T(8,128)S(1)} %collective-permute-done.36.refs_2_, f32[4,2,32,1024]{3,2,1,0:T(8,128)S(1)} %collective-permute-done.37.refs_3_, ...), custom_call_target="tpu_custom_call" | custom-call | flops 4831838208 | bytes 50331648 | tf_op jit(solution)/shard_map/pallas_call | solution.py:174
  174.9 1.3 collective-permute-done.38.refs_1_
  176.2 0.9 collective-permute-start.46
  177.1 1.0 collective-permute-done.46.refs_6_
  178.0 1.8 %shard_map.58 = (f32[32,1024]{1,0:T(8,128)S(1)}, f32[32,1024]{1,0:T(8,128)S(1)}) custom-call(f32[4,1,32,1024]{3,2,1,0:T(8,128)S(1)} %pad_maximum_fusion.3.refs_0_, f32[4,1,32,1024]{3,2,1,0:T(8,128)S(1)} %collective-permute-done.38.refs_1_, f32[4,1,32,1024]{3,2,1,0:T(8,128)S(1)} %collective-permute-done.39.refs_2_, ...), custom_call_target="tpu_custom_call" | custom-call | flops 805306368 | bytes 8388608 | tf_op jit(solution)/shard_map/pallas_call | solution.py:174
  180.3 1.0 collective-permute-done.47
  181.3 0.7 add_bitcast_fusion
  (68 shorter events, 7.1 us)
Async XLA Ops:
  1.6 6.2 %collective-permute-start.1 = (f32[1,32,1024]{2,1,0:T(8,128)S(1)}, f32[1,32,1024]{2,1,0:T(8,128)S(1)}, u32[]{:S(2)}, u32[]{:S(2)}) collective-permute-start(f32[1,32,1024]{2,1,0:T(8,128)S(1)} %constant_dynamic-slice_fusion), channel_id=1, source_target_pairs={{0,24},{1,7},{2,26},{3,1},{4,28},{5,3},{6,30},{7,5},{8,0},{9,15},{... | collective-permute-start | bytes 393224 | tf_op jit(solution)/shard_map/ppermute | solution.py:208
  5.2 6.7 %collective-permute-start = (f32[1,32,1024]{2,1,0:T(8,128)S(1)}, f32[1,32,1024]{2,1,0:T(8,128)S(1)}, u32[]{:S(2)}, u32[]{:S(2)}) collective-permute-start(f32[1,32,1024]{2,1,0:T(8,128)S(1)} %constant_dynamic-slice_fusion), channel_id=1, source_target_pairs={{0,8},{1,3},{2,10},{3,5},{4,12},{5,7},{6,14},{7,1},{8,16},{9,11},{... | collective-permute-start | bytes 393224 | tf_op jit(solution)/shard_map/ppermute | solution.py:208
  5.2 6.7 %collective-permute-start.2 = (f32[1,32,1024]{2,1,0:T(8,128)S(1)}, f32[1,32,1024]{2,1,0:T(8,128)S(1)}, u32[]{:S(2)}, u32[]{:S(2)}) collective-permute-start(f32[1,32,1024]{2,1,0:T(8,128)S(1)} %constant_dynamic-slice_fusion), channel_id=1, source_target_pairs={{0,16},{1,5},{2,18},{3,7},{4,20},{5,1},{6,22},{7,3},{8,24},{9,13},... | collective-permute-start | bytes 393224 | tf_op jit(solution)/shard_map/ppermute | solution.py:208
  12.0 10.0 %collective-permute-start.5 = (f32[4,1,32,1024]{3,2,1,0:T(8,128)S(1)}, f32[4,1,32,1024]{3,2,1,0:T(8,128)S(1)}, u32[]{:S(2)}, u32[]{:S(2)}) collective-permute-start(f32[4,1,32,1024]{3,2,1,0:T(8,128)S(1)} %pad_maximum_fusion.1.refs_0_), channel_id=1, source_target_pairs={{0,4},{1,17},{2,6},{3,19},{4,0},{5,21},{6,2},{7,23},{8,12},{9,25},... | collective-permute-start | bytes 1572872 | tf_op jit(solution)/shard_map/ppermute | solution.py:208
  14.5 13.1 %collective-permute-start.4 = (f32[4,1,32,1024]{3,2,1,0:T(8,128)S(1)}, f32[4,1,32,1024]{3,2,1,0:T(8,128)S(1)}, u32[]{:S(2)}, u32[]{:S(2)}) collective-permute-start(f32[4,1,32,1024]{3,2,1,0:T(8,128)S(1)} %pad_maximum_fusion.1.refs_0_), channel_id=1, source_target_pairs={{0,6},{1,25},{2,0},{3,27},{4,2},{5,29},{6,4},{7,31},{8,14},{9,1},{... | collective-permute-start | bytes 1572872 | tf_op jit(solution)/shard_map/ppermute | solution.py:208
  15.4 14.9 %collective-permute-start.3 = (f32[4,1,32,1024]{3,2,1,0:T(8,128)S(1)}, f32[4,1,32,1024]{3,2,1,0:T(8,128)S(1)}, u32[]{:S(2)}, u32[]{:S(2)}) collective-permute-start(f32[4,1,32,1024]{3,2,1,0:T(8,128)S(1)} %pad_maximum_fusion.1.refs_0_), channel_id=1, source_target_pairs={{0,2},{1,9},{2,4},{3,11},{4,6},{5,13},{6,0},{7,15},{8,10},{9,17},{... | collective-permute-start | bytes 1572872 | tf_op jit(solution)/shard_map/ppermute | solution.py:208
  16.0 16.1 %collective-permute-start.6 = (f32[4,1,32,1024]{3,2,1,0:T(8,128)S(1)}, f32[4,1,32,1024]{3,2,1,0:T(8,128)S(1)}, u32[]{:S(2)}, u32[]{:S(2)}) collective-permute-start(f32[4,1,32,1024]{3,2,1,0:T(8,128)S(1)} %pad_maximum_fusion.1.refs_0_), channel_id=1, source_target_pairs={{0,1},{1,0},{2,3},{3,2},{4,5},{5,4},{6,7},{7,6},{8,9},{9,8},{10,11... | collective-permute-start | bytes 1572872 | tf_op jit(solution)/shard_map/ppermute | solution.py:220
  21.9 10.1 %collective-permute-start.9 = (f32[4,1,32,1024]{3,2,1,0:T(8,128)S(1)}, f32[4,1,32,1024]{3,2,1,0:T(8,128)S(1)}, u32[]{:S(2)}, u32[]{:S(2)}) collective-permute-start(f32[4,1,32,1024]{3,2,1,0:T(8,128)S(1)} %collective-permute-done.5.refs_3_), channel_id=1, source_target_pairs={{0,1},{1,0},{2,3},{3,2},{4,5},{5,4},{6,7},{7,6},{8,9},{9,8},{10,11... | collective-permute-start | bytes 1572872 | tf_op jit(solution)/shard_map/ppermute | solution.py:220
  27.6 4.4 %collective-permute-start.8 = (f32[4,1,32,1024]{3,2,1,0:T(8,128)S(1)}, f32[4,1,32,1024]{3,2,1,0:T(8,128)}, u32[]{:S(2)}, u32[]{:S(2)}) collective-permute-start(f32[4,1,32,1024]{3,2,1,0:T(8,128)S(1)} %collective-permute-done.4.refs_2_), channel_id=1, source_target_pairs={{0,1},{1,0},{2,3},{3,2},{4,5},{5,4},{6,7},{7,6},{8,9},{9,8},{10,11... | collective-permute-start | bytes 1572872 | tf_op jit(solution)/shard_map/ppermute | solution.py:220
  30.3 2.4 %collective-permute-start.7 = (f32[4,1,32,1024]{3,2,1,0:T(8,128)S(1)}, f32[4,1,32,1024]{3,2,1,0:T(8,128)}, u32[]{:S(2)}, u32[]{:S(2)}) collective-permute-start(f32[4,1,32,1024]{3,2,1,0:T(8,128)S(1)} %collective-permute-done.3.refs_1_), channel_id=1, source_target_pairs={{0,1},{1,0},{2,3},{3,2},{4,5},{5,4},{6,7},{7,6},{8,9},{9,8},{10,11... | collective-permute-start | bytes 1572872 | tf_op jit(solution)/shard_map/ppermute | solution.py:220
  43.3 5.7 %collective-permute-start.12 = (f32[1,32,1024]{2,1,0:T(8,128)S(1)}, f32[1,32,1024]{2,1,0:T(8,128)S(1)}, u32[]{:S(2)}, u32[]{:S(2)}) collective-permute-start(f32[1,32,1024]{2,1,0:T(8,128)S(1)} %bitcast.40), channel_id=1, source_target_pairs={{0,16},{1,5},{2,18},{3,7},{4,20},{5,1},{6,22},{7,3},{8,24},{9,13},... | collective-permute-start | bytes 393224 | tf_op jit(solution)/shard_map/ppermute | solution.py:208
  45.2 5.1 %collective-permute-start.11 = (f32[1,32,1024]{2,1,0:T(8,128)S(1)}, f32[1,32,1024]{2,1,0:T(8,128)S(1)}, u32[]{:S(2)}, u32[]{:S(2)}) collective-permute-start(f32[1,32,1024]{2,1,0:T(8,128)S(1)} %bitcast.41), channel_id=1, source_target_pairs={{0,24},{1,7},{2,26},{3,1},{4,28},{5,3},{6,30},{7,5},{8,0},{9,15},{... | collective-permute-start | bytes 393224 | tf_op jit(solution)/shard_map/ppermute | solution.py:208
  46.7 5.2 %collective-permute-start.10 = (f32[1,32,1024]{2,1,0:T(8,128)S(1)}, f32[1,32,1024]{2,1,0:T(8,128)S(1)}, u32[]{:S(2)}, u32[]{:S(2)}) collective-permute-start(f32[1,32,1024]{2,1,0:T(8,128)S(1)} %bitcast.42), channel_id=1, source_target_pairs={{0,8},{1,3},{2,10},{3,5},{4,12},{5,7},{6,14},{7,1},{8,16},{9,11},{... | collective-permute-start | bytes 393224 | tf_op jit(solution)/shard_map/ppermute | solution.py:208
  46.7 10.8 %collective-permute-start.16 = (f32[32,1024]{1,0:T(8,128)S(1)}, f32[32,1024]{1,0:T(8,128)S(1)}, u32[]{:S(2)}, u32[]{:S(2)}) collective-permute-start(f32[32,1024]{1,0:T(8,128)S(1)} %get-tuple-element.27.refs_21_), channel_id=1, source_target_pairs={{0,32},{32,0},{64,96},{96,64},{1,33},{33,1},{65,97},{97,65},{2,34}... | collective-permute-start | bytes 393224 | tf_op jit(solution)/shard_map/ppermute | solution.py:262
  51.9 9.9 %collective-permute-start.17 = (f32[4,1,32,1024]{3,2,1,0:T(8,128)S(1)}, f32[4,1,32,1024]{3,2,1,0:T(8,128)S(1)}, u32[]{:S(2)}, u32[]{:S(2)}) collective-permute-start(f32[4,1,32,1024]{3,2,1,0:T(8,128)S(1)} %pad_maximum_fusion.2.refs_0_), channel_id=1, source_target_pairs={{0,4},{1,17},{2,6},{3,19},{4,0},{5,21},{6,2},{7,23},{8,12},{9,25},... | collective-permute-start | bytes 1572872 | tf_op jit(solution)/shard_map/ppermute | solution.py:208
  52.7 12.1 %collective-permute-start.15 = (f32[4,1,32,1024]{3,2,1,0:T(8,128)S(1)}, f32[4,1,32,1024]{3,2,1,0:T(8,128)S(1)}, u32[]{:S(2)}, u32[]{:S(2)}) collective-permute-start(f32[4,1,32,1024]{3,2,1,0:T(8,128)S(1)} %pad_maximum_fusion.2.refs_0_), channel_id=1, source_target_pairs={{0,32},{32,0},{64,96},{96,64},{1,33},{33,1},{65,97},{97,65},{2,34}... | collective-permute-start | bytes 1572872 | tf_op jit(solution)/shard_map/ppermute | solution.py:261
  54.3 12.9 %collective-permute-start.18 = (f32[4,1,32,1024]{3,2,1,0:T(8,128)S(1)}, f32[4,1,32,1024]{3,2,1,0:T(8,128)S(1)}, u32[]{:S(2)}, u32[]{:S(2)}) collective-permute-start(f32[4,1,32,1024]{3,2,1,0:T(8,128)S(1)} %pad_maximum_fusion.2.refs_0_), channel_id=1, source_target_pairs={{0,1},{1,0},{2,3},{3,2},{4,5},{5,4},{6,7},{7,6},{8,9},{9,8},{10,11... | collective-permute-start | bytes 1572872 | tf_op jit(solution)/shard_map/ppermute | solution.py:220
  56.3 13.1 %collective-permute-start.14 = (f32[4,1,32,1024]{3,2,1,0:T(8,128)S(1)}, f32[4,1,32,1024]{3,2,1,0:T(8,128)S(1)}, u32[]{:S(2)}, u32[]{:S(2)}) collective-permute-start(f32[4,1,32,1024]{3,2,1,0:T(8,128)S(1)} %pad_maximum_fusion.2.refs_0_), channel_id=1, source_target_pairs={{0,6},{1,25},{2,0},{3,27},{4,2},{5,29},{6,4},{7,31},{8,14},{9,1},{... | collective-permute-start | bytes 1572872 | tf_op jit(solution)/shard_map/ppermute | solution.py:208
  57.5 13.5 %collective-permute-start.13 = (f32[4,1,32,1024]{3,2,1,0:T(8,128)S(1)}, f32[4,1,32,1024]{3,2,1,0:T(8,128)S(1)}, u32[]{:S(2)}, u32[]{:S(2)}) collective-permute-start(f32[4,1,32,1024]{3,2,1,0:T(8,128)S(1)} %pad_maximum_fusion.2.refs_0_), channel_id=1, source_target_pairs={{0,2},{1,9},{2,4},{3,11},{4,6},{5,13},{6,0},{7,15},{8,10},{9,17},{... | collective-permute-start | bytes 1572872 | tf_op jit(solution)/shard_map/ppermute | solution.py:208
  64.8 6.2 %collective-permute-start.21 = (f32[4,1,32,1024]{3,2,1,0:T(8,128)S(1)}, f32[4,1,32,1024]{3,2,1,0:T(8,128)S(1)}, u32[]{:S(2)}, u32[]{:S(2)}) collective-permute-start(f32[4,1,32,1024]{3,2,1,0:T(8,128)S(1)} %collective-permute-done.17.refs_3_), channel_id=1, source_target_pairs={{0,1},{1,0},{2,3},{3,2},{4,5},{5,4},{6,7},{7,6},{8,9},{9,8},{10,11... | collective-permute-start | bytes 1572872 | tf_op jit(solution)/shard_map/ppermute | solution.py:220
  67.2 4.9 %collective-permute-start.25 = (f32[4,1,32,1024]{3,2,1,0:T(8,128)S(1)}, f32[4,1,32,1024]{3,2,1,0:T(8,128)S(1)}, u32[]{:S(2)}, u32[]{:S(2)}) collective-permute-start(f32[4,1,32,1024]{3,2,1,0:T(8,128)S(1)} %collective-permute-done.15.refs_8_), channel_id=1, source_target_pairs={{0,1},{1,0},{2,3},{3,2},{4,5},{5,4},{6,7},{7,6},{8,9},{9,8},{10,11... | collective-permute-start | bytes 1572872 | tf_op jit(solution)/shard_map/ppermute | solution.py:220
  67.2 10.0 %collective-permute-start.24 = (f32[4,1,32,1024]{3,2,1,0:T(8,128)S(1)}, f32[4,1,32,1024]{3,2,1,0:T(8,128)}, u32[]{:S(2)}, u32[]{:S(2)}) collective-permute-start(f32[4,1,32,1024]{3,2,1,0:T(8,128)S(1)} %collective-permute-done.15.refs_8_), channel_id=1, source_target_pairs={{0,4},{1,17},{2,6},{3,19},{4,0},{5,21},{6,2},{7,23},{8,12},{9,25},... | collective-permute-start | bytes 1572872 | tf_op jit(solution)/shard_map/ppermute | solution.py:208
  69.4 12.0 %collective-permute-start.23 = (f32[4,1,32,1024]{3,2,1,0:T(8,128)S(1)}, f32[4,1,32,1024]{3,2,1,0:T(8,128)}, u32[]{:S(2)}, u32[]{:S(2)}) collective-permute-start(f32[4,1,32,1024]{3,2,1,0:T(8,128)S(1)} %collective-permute-done.15.refs_8_), channel_id=1, source_target_pairs={{0,6},{1,25},{2,0},{3,27},{4,2},{5,29},{6,4},{7,31},{8,14},{9,1},{... | collective-permute-start | bytes 1572872 | tf_op jit(solution)/shard_map/ppermute | solution.py:208
  71.0 11.8 %collective-permute-start.22 = (f32[4,1,32,1024]{3,2,1,0:T(8,128)S(1)}, f32[4,1,32,1024]{3,2,1,0:T(8,128)}, u32[]{:S(2)}, u32[]{:S(2)}) collective-permute-start(f32[4,1,32,1024]{3,2,1,0:T(8,128)S(1)} %collective-permute-done.15.refs_8_), channel_id=1, source_target_pairs={{0,2},{1,9},{2,4},{3,11},{4,6},{5,13},{6,0},{7,15},{8,10},{9,17},{... | collective-permute-start | bytes 1572872 | tf_op jit(solution)/shard_map/ppermute | solution.py:208
  71.0 0.8 copy-start
  71.8 12.4 %collective-permute-start.20 = (f32[4,1,32,1024]{3,2,1,0:T(8,128)S(1)}, f32[4,1,32,1024]{3,2,1,0:T(8,128)}, u32[]{:S(2)}, u32[]{:S(2)}) collective-permute-start(f32[4,1,32,1024]{3,2,1,0:T(8,128)S(1)} %collective-permute-done.14.refs_2_), channel_id=1, source_target_pairs={{0,1},{1,0},{2,3},{3,2},{4,5},{5,4},{6,7},{7,6},{8,9},{9,8},{10,11... | collective-permute-start | bytes 1572872 | tf_op jit(solution)/shard_map/ppermute | solution.py:220
  72.1 0.8 copy-start.2
  72.9 11.3 %collective-permute-start.19 = (f32[4,1,32,1024]{3,2,1,0:T(8,128)S(1)}, f32[4,1,32,1024]{3,2,1,0:T(8,128)}, u32[]{:S(2)}, u32[]{:S(2)}) collective-permute-start(f32[4,1,32,1024]{3,2,1,0:T(8,128)S(1)} %collective-permute-done.13.refs_1_), channel_id=1, source_target_pairs={{0,1},{1,0},{2,3},{3,2},{4,5},{5,4},{6,7},{7,6},{8,9},{9,8},{10,11... | collective-permute-start | bytes 1572872 | tf_op jit(solution)/shard_map/ppermute | solution.py:220
  77.2 6.9 %collective-permute-start.28 = (f32[4,1,32,1024]{3,2,1,0:T(8,128)}, f32[4,1,32,1024]{3,2,1,0:T(8,128)}, u32[]{:S(2)}, u32[]{:S(2)}) collective-permute-start(f32[4,1,32,1024]{3,2,1,0:T(8,128)} %collective-permute-done.24.refs_11_), channel_id=1, source_target_pairs={{0,1},{1,0},{2,3},{3,2},{4,5},{5,4},{6,7},{7,6},{8,9},{9,8},{10,11... | collective-permute-start | bytes 1572872 | tf_op jit(solution)/shard_map/ppermute | solution.py:220
  81.5 2.9 %collective-permute-start.27 = (f32[4,1,32,1024]{3,2,1,0:T(8,128)}, f32[4,1,32,1024]{3,2,1,0:T(8,128)}, u32[]{:S(2)}, u32[]{:S(2)}) collective-permute-start(f32[4,1,32,1024]{3,2,1,0:T(8,128)} %collective-permute-done.23.refs_10_), channel_id=1, source_target_pairs={{0,1},{1,0},{2,3},{3,2},{4,5},{5,4},{6,7},{7,6},{8,9},{9,8},{10,11... | collective-permute-start | bytes 1572872 | tf_op jit(solution)/shard_map/ppermute | solution.py:220
  82.8 3.2 %collective-permute-start.26 = (f32[4,1,32,1024]{3,2,1,0:T(8,128)}, f32[4,1,32,1024]{3,2,1,0:T(8,128)}, u32[]{:S(2)}, u32[]{:S(2)}) collective-permute-start(f32[4,1,32,1024]{3,2,1,0:T(8,128)} %collective-permute-done.22.refs_9_), channel_id=1, source_target_pairs={{0,1},{1,0},{2,3},{3,2},{4,5},{5,4},{6,7},{7,6},{8,9},{9,8},{10,11... | collective-permute-start | bytes 1572872 | tf_op jit(solution)/shard_map/ppermute | solution.py:220
  86.0 1.0 copy-start.1
  87.1 1.0 copy-start.3
  107.7 7.1 %collective-permute-start.31 = (f32[32,1024]{1,0:T(8,128)S(1)}, f32[32,1024]{1,0:T(8,128)S(1)}, u32[]{:S(2)}, u32[]{:S(2)}) collective-permute-start(f32[32,1024]{1,0:T(8,128)S(1)} %get-tuple-element.36), channel_id=1, source_target_pairs={{0,64},{64,0},{32,96},{96,32},{1,65},{65,1},{33,97},{97,33},{2,66}... | collective-permute-start | bytes 393224 | tf_op jit(solution)/shard_map/ppermute | solution.py:270
  111.2 6.7 %collective-permute-start.30 = (f32[32,1024]{1,0:T(8,128)S(1)}, f32[32,1024]{1,0:T(8,128)S(1)}, u32[]{:S(2)}, u32[]{:S(2)}) collective-permute-start(f32[32,1024]{1,0:T(8,128)S(1)} %get-tuple-element.34), channel_id=1, source_target_pairs={{32,0},{64,96},{33,1},{65,97},{34,2},{66,98},{35,3},{67,99},{36,4}... | collective-permute-start | bytes 393224 | tf_op jit(solution)/shard_map/ppermute | solution.py:271
  112.5 5.4 %collective-permute-start.29 = (f32[32,1024]{1,0:T(8,128)S(1)}, f32[32,1024]{1,0:T(8,128)S(1)}, u32[]{:S(2)}, u32[]{:S(2)}) collective-permute-start(f32[32,1024]{1,0:T(8,128)S(1)} %get-tuple-element.34), channel_id=1, source_target_pairs={{32,64},{64,32},{33,65},{65,33},{34,66},{66,34},{35,67},{67,35},{3... | collective-permute-start | bytes 393224 | tf_op jit(solution)/shard_map/ppermute | solution.py:272
  117.9 8.5 %collective-permute-start.34 = (f32[3,32,1024]{2,1,0:T(8,128)S(1)}, f32[3,32,1024]{2,1,0:T(8,128)S(1)}, u32[]{:S(2)}, u32[]{:S(2)}) collective-permute-start(f32[3,32,1024]{2,1,0:T(8,128)S(1)} %pad_maximum_fusion.4), channel_id=1, source_target_pairs={{0,16},{1,5},{2,18},{3,7},{4,20},{5,1},{6,22},{7,3},{8,24},{9,13},... | collective-permute-start | bytes 1179656 | tf_op jit(solution)/shard_map/ppermute | solution.py:208
  119.0 10.8 %collective-permute-start.33 = (f32[3,32,1024]{2,1,0:T(8,128)S(1)}, f32[3,32,1024]{2,1,0:T(8,128)S(1)}, u32[]{:S(2)}, u32[]{:S(2)}) collective-permute-start(f32[3,32,1024]{2,1,0:T(8,128)S(1)} %pad_maximum_fusion.4), channel_id=1, source_target_pairs={{0,24},{1,7},{2,26},{3,1},{4,28},{5,3},{6,30},{7,5},{8,0},{9,15},{... | collective-permute-start | bytes 1179656 | tf_op jit(solution)/shard_map/ppermute | solution.py:208
  120.7 9.9 %collective-permute-start.32 = (f32[3,32,1024]{2,1,0:T(8,128)S(1)}, f32[3,32,1024]{2,1,0:T(8,128)S(1)}, u32[]{:S(2)}, u32[]{:S(2)}) collective-permute-start(f32[3,32,1024]{2,1,0:T(8,128)S(1)} %pad_maximum_fusion.4), channel_id=1, source_target_pairs={{0,8},{1,3},{2,10},{3,5},{4,12},{5,7},{6,14},{7,1},{8,16},{9,11},{... | collective-permute-start | bytes 1179656 | tf_op jit(solution)/shard_map/ppermute | solution.py:208
  130.7 15.6 %collective-permute-start.37 = (f32[4,2,32,1024]{3,2,1,0:T(8,128)S(1)}, f32[4,2,32,1024]{3,2,1,0:T(8,128)S(1)}, u32[]{:S(2)}, u32[]{:S(2)}) collective-permute-start(f32[4,2,32,1024]{3,2,1,0:T(8,128)S(1)} %pad_maximum_fusion.refs_0_), channel_id=1, source_target_pairs={{0,4},{1,17},{2,6},{3,19},{4,0},{5,21},{6,2},{7,23},{8,12},{9,25},... | collective-permute-start | bytes 3145736 | tf_op jit(solution)/shard_map/ppermute | solution.py:208
  132.7 23.5 %collective-permute-start.36 = (f32[4,2,32,1024]{3,2,1,0:T(8,128)S(1)}, f32[4,2,32,1024]{3,2,1,0:T(8,128)S(1)}, u32[]{:S(2)}, u32[]{:S(2)}) collective-permute-start(f32[4,2,32,1024]{3,2,1,0:T(8,128)S(1)} %pad_maximum_fusion.refs_0_), channel_id=1, source_target_pairs={{0,6},{1,25},{2,0},{3,27},{4,2},{5,29},{6,4},{7,31},{8,14},{9,1},{... | collective-permute-start | bytes 3145736 | tf_op jit(solution)/shard_map/ppermute | solution.py:208
  134.5 25.5 %collective-permute-start.35 = (f32[4,2,32,1024]{3,2,1,0:T(8,128)S(1)}, f32[4,2,32,1024]{3,2,1,0:T(8,128)S(1)}, u32[]{:S(2)}, u32[]{:S(2)}) collective-permute-start(f32[4,2,32,1024]{3,2,1,0:T(8,128)S(1)} %pad_maximum_fusion.refs_0_), channel_id=1, source_target_pairs={{0,2},{1,9},{2,4},{3,11},{4,6},{5,13},{6,0},{7,15},{8,10},{9,17},{... | collective-permute-start | bytes 3145736 | tf_op jit(solution)/shard_map/ppermute | solution.py:208
  134.5 26.2 %collective-permute-start.45 = (f32[32,1024]{1,0:T(8,128)S(1)}, f32[32,1024]{1,0:T(8,128)S(1)}, u32[]{:S(2)}, u32[]{:S(2)}) collective-permute-start(f32[32,1024]{1,0:T(8,128)S(1)} %get-tuple-element.39.refs_10_), channel_id=1, source_target_pairs={{32,0},{64,96},{33,1},{65,97},{34,2},{66,98},{35,3},{67,99},{36,4}... | collective-permute-start | bytes 393224 | tf_op jit(solution)/shard_map/ppermute | solution.py:277
  135.7 27.2 %collective-permute-start.41 = (f32[4,2,32,1024]{3,2,1,0:T(8,128)S(1)}, f32[4,2,32,1024]{3,2,1,0:T(8,128)S(1)}, u32[]{:S(2)}, u32[]{:S(2)}) collective-permute-start(f32[4,2,32,1024]{3,2,1,0:T(8,128)S(1)} %pad_maximum_fusion.refs_0_), channel_id=1, source_target_pairs={{0,1},{1,0},{2,3},{3,2},{4,5},{5,4},{6,7},{7,6},{8,9},{9,8},{10,11... | collective-permute-start | bytes 3145736 | tf_op jit(solution)/shard_map/ppermute | solution.py:220
  146.3 17.6 %collective-permute-start.44 = (f32[4,2,32,1024]{3,2,1,0:T(8,128)S(1)}, f32[4,2,32,1024]{3,2,1,0:T(8,128)S(1)}, u32[]{:S(2)}, u32[]{:S(2)}) collective-permute-start(f32[4,2,32,1024]{3,2,1,0:T(8,128)S(1)} %collective-permute-done.37.refs_3_), channel_id=1, source_target_pairs={{0,1},{1,0},{2,3},{3,2},{4,5},{5,4},{6,7},{7,6},{8,9},{9,8},{10,11... | collective-permute-start | bytes 3145736 | tf_op jit(solution)/shard_map/ppermute | solution.py:220
  156.2 8.3 %collective-permute-start.43 = (f32[4,2,32,1024]{3,2,1,0:T(8,128)S(1)}, f32[4,2,32,1024]{3,2,1,0:T(8,128)S(1)}, u32[]{:S(2)}, u32[]{:S(2)}) collective-permute-start(f32[4,2,32,1024]{3,2,1,0:T(8,128)S(1)} %collective-permute-done.36.refs_2_), channel_id=1, source_target_pairs={{0,1},{1,0},{2,3},{3,2},{4,5},{5,4},{6,7},{7,6},{8,9},{9,8},{10,11... | collective-permute-start | bytes 3145736 | tf_op jit(solution)/shard_map/ppermute | solution.py:220
  160.0 4.5 %collective-permute-start.42 = (f32[4,2,32,1024]{3,2,1,0:T(8,128)S(1)}, f32[4,2,32,1024]{3,2,1,0:T(8,128)S(1)}, u32[]{:S(2)}, u32[]{:S(2)}) collective-permute-start(f32[4,2,32,1024]{3,2,1,0:T(8,128)S(1)} %collective-permute-done.35.refs_1_), channel_id=1, source_target_pairs={{0,1},{1,0},{2,3},{3,2},{4,5},{5,4},{6,7},{7,6},{8,9},{9,8},{10,11... | collective-permute-start | bytes 3145736 | tf_op jit(solution)/shard_map/ppermute | solution.py:220
  160.7 14.2 %collective-permute-start.40 = (f32[4,1,32,1024]{3,2,1,0:T(8,128)S(1)}, f32[4,1,32,1024]{3,2,1,0:T(8,128)S(1)}, u32[]{:S(2)}, u32[]{:S(2)}) collective-permute-start(f32[4,1,32,1024]{3,2,1,0:T(8,128)S(1)} %pad_maximum_fusion.3.refs_0_), channel_id=1, source_target_pairs={{0,4},{1,17},{2,6},{3,19},{4,0},{5,21},{6,2},{7,23},{8,12},{9,25},... | collective-permute-start | bytes 1572872 | tf_op jit(solution)/shard_map/ppermute | solution.py:208
  163.0 11.9 %collective-permute-start.39 = (f32[4,1,32,1024]{3,2,1,0:T(8,128)S(1)}, f32[4,1,32,1024]{3,2,1,0:T(8,128)S(1)}, u32[]{:S(2)}, u32[]{:S(2)}) collective-permute-start(f32[4,1,32,1024]{3,2,1,0:T(8,128)S(1)} %pad_maximum_fusion.3.refs_0_), channel_id=1, source_target_pairs={{0,6},{1,25},{2,0},{3,27},{4,2},{5,29},{6,4},{7,31},{8,14},{9,1},{... | collective-permute-start | bytes 1572872 | tf_op jit(solution)/shard_map/ppermute | solution.py:208
  163.9 12.3 %collective-permute-start.38 = (f32[4,1,32,1024]{3,2,1,0:T(8,128)S(1)}, f32[4,1,32,1024]{3,2,1,0:T(8,128)S(1)}, u32[]{:S(2)}, u32[]{:S(2)}) collective-permute-start(f32[4,1,32,1024]{3,2,1,0:T(8,128)S(1)} %pad_maximum_fusion.3.refs_0_), channel_id=1, source_target_pairs={{0,2},{1,9},{2,4},{3,11},{4,6},{5,13},{6,0},{7,15},{8,10},{9,17},{... | collective-permute-start | bytes 1572872 | tf_op jit(solution)/shard_map/ppermute | solution.py:208
  176.2 1.8 %collective-permute-start.46 = (f32[32,1024]{1,0:T(8,128)S(1)}, f32[32,1024]{1,0:T(8,128)S(1)}, u32[]{:S(2)}, u32[]{:S(2)}) collective-permute-start(f32[32,1024]{1,0:T(8,128)S(1)} %shard_map.57.refs_5_), channel_id=1, source_target_pairs={{0,1},{1,0},{2,3},{3,2},{4,5},{5,4},{6,7},{7,6},{8,9},{9,8},{10,11... | collective-permute-start | bytes 393224 | tf_op jit(solution)/shard_map/ppermute | solution.py:220
  179.9 1.4 collective-permute-start.47

commit v5 on v4

--- a/solution.py
+++ b/solution.py
@@ -33,8 +33,7 @@
     return by_high[:count] + (by_high[count:] + by_low)
 
 
-def split(pieces, places, high_ref, low_ref):
-    before = 0
+def split(pieces, places, high_ref, low_ref, before=0):
     for piece in pieces:
         lines, slots, panel_rows, _ = piece.shape
 
@@ -85,9 +84,15 @@
 
 
 def pair_kernel(*refs):
-    own_pieces, oth_pieces, refs = refs[:PIECES], refs[PIECES : 2 * PIECES], refs[2 * PIECES :]
-    high_in, low_in, places, inner, own_refl, own_trans, oth_trans, decay_row = refs[:8]
-    refl_out, trans_out, far_out, own_high, own_low, oth_high, oth_low, layer_high, layer_low, sems = refs[8:]
+    own_pieces, oth_pieces, refs = refs[: PIECES - 1], refs[PIECES - 1 : 2 * PIECES - 2], refs[2 * PIECES - 2 :]
+    high_in, low_in, own_far, oth_far, places, inner, own_refl, own_trans, oth_trans, decay_row = refs[:10]
+    refl_out, trans_out, far_out, own_high, own_low, oth_high, oth_low, layer_high, layer_low, stage, sems = refs[10:]
+    brought = [
+        pltpu.make_async_copy(own_far, stage.at[0], sems.at[2]),
+        pltpu.make_async_copy(oth_far, stage.at[1], sems.at[3]),
+    ]
+    for load in brought:
+        load.start()
     loads = [
         pltpu.make_async_copy(high_in, layer_high, sems.at[0]),
         pltpu.make_async_copy(low_in, layer_low, sems.at[1]),
@@ -95,7 +100,12 @@
     for load in loads:
         load.start()
     split(own_pieces, places, own_high, own_low)
-    split(oth_pieces, places, oth_high, oth_low)
+    split(oth_pieces[:SIDE], places, oth_high, oth_low)
+    split(oth_pieces[SIDE:], places, oth_high, oth_low, before=(SIDE + 1) * SIDE)
+    for load in brought:
+        load.wait()
+    split([stage.at[0]], places, own_high, own_low, before=(PIECES - 1) * SIDE)
+    split([stage.at[1]], places, oth_high, oth_low, before=SIDE * SIDE)
     first = product(own_trans[...], oth_high.at[0], oth_low.at[0])
     both = jnp.concatenate([first, oth_trans[...]], axis=0)
 
@@ -262,10 +272,13 @@
     oth_trans = lax.ppermute(trans, "layer", pairs)
     mine = spread(line)
     oth_line, oth_trans, mine[3] = lax.optimization_barrier((oth_line, oth_trans, mine[3]))
+    own_pieces, oth_pieces = flipped(mine), flipped(spread(oth_line))
     refl, trans, away = call(
-        pair_kernel, 16, 4 * TERMS, (block, block, block), flipped(mine) + flipped(spread(oth_line)),
-        (places, inner_flag), (refl, trans, oth_trans, decays), far=halved,
-        scratch=matrices(1, order) * 3 + (pltpu.SemaphoreType.DMA((2,)),),
+        pair_kernel, 16, 4 * TERMS, (block, block, block),
+        own_pieces[: PIECES - 1] + oth_pieces[:SIDE] + oth_pieces[SIDE + 1 :], (places, inner_flag),
+        (refl, trans, oth_trans, decays), far=(*halved, own_pieces[PIECES - 1], oth_pieces[SIDE]),
+        scratch=matrices(1, order) * 3
+        + (pltpu.VMEM((2, SIDE, 1, *rows), jnp.float32), pltpu.SemaphoreType.DMA((4,))),
     )
     far = lax.ppermute(away, "layer", [(0, 2), (2, 0), (1, 3), (3, 1)])
     near = lax.ppermute(refl, "layer", [(1, 0), (2, 3)])

time: 183 us -> 181 us (0.989)
  local copies, waits for them, and re-layouts: 5.78 us -> 2.12 us
    unnamed x8 -> x4, local copies, waits for them, and re-layouts: 3.67 us -> 0.01 us
where the time goes in v5:
time: 181 us; the launch traced here: 180 us
  starting transfers between devices  66.6 us (37%)
  waiting for transfers between devices  65.4 us (36%)
  Pallas kernels  42.4 us (23%)
  local copies, waits for them, and re-layouts  2.12 us (1%)
  other arithmetic  1.87 us (1%)
    ppermute x24, waiting for transfers between devices, moved(): return lax.ppermute(block, 'panel', route)  53.2 us
    pallas_call x4, Pallas kernels, call(): pl.pallas_call(kernel, out_shape=tuple((out if placed else jax.ShapeDtype...  42.4 us
    ppermute x24, starting transfers between devices, moved(): return lax.ppermute(block, 'panel', route)  29 us
    ppermute x18, starting transfers between devices, other_core(): lax.ppermute(block, 'panel', [(i, i ^ 1) for i in range(2 * SIDE * SIDE)])  27.6 us
    ppermute x18, waiting for transfers between devices, other_core(): lax.ppermute(block, 'panel', [(i, i ^ 1) for i in range(2 * SIDE * SIDE)])  4.55 us
  transfers between devices with their start and end apart: 48, of which 25 were waited for; matrix products, arithmetic and copies ran while one was open for 1% of the time, Pallas kernels for 6%

profile of v5, /device:TPU:1, one launch (start us, length us, event | category | flops | bytes accessed | tf_op | source)
XLA Modules:
  0.0 179.9 jit_solution(13283880466028388000)
XLA Ops:
  0.7 0.9 constant_dynamic-slice_fusion
  1.6 3.6 %collective-permute-start.1 = (f32[1,32,1024]{2,1,0:T(8,128)S(1)}, f32[1,32,1024]{2,1,0:T(8,128)S(1)}, u32[]{:S(2)}, u32[]{:S(2)}) collective-permute-start(f32[1,32,1024]{2,1,0:T(8,128)S(1)} %constant_dynamic-slice_fusion), channel_id=1, source_target_pairs={{0,24},{1,7},{2,26},{3,1},{4,28},{5,3},{6,30},{7,5},{8,0},{9,15},{... | collective-permute-start | bytes 393224 | tf_op jit(solution)/shard_map/ppermute | solution.py:218
  5.2 1.6 collective-permute-start.2
  6.9 0.9 fusion.5
  7.8 4.2 %collective-permute-done = f32[1,32,1024]{2,1,0:T(8,128)S(1)} collective-permute-done((f32[1,32,1024]{2,1,0:T(8,128)S(1)}, f32[1,32,1024]{2,1,0:T(8,128)S(1)}, u32[]{:S(2)}, u32[]{:S(2)}) %collective-permute-start) | collective-permute-done | bytes 131104 | tf_op jit(solution)/shard_map/ppermute | solution.py:218
  12.0 2.5 %collective-permute-start.5 = (f32[4,1,32,1024]{3,2,1,0:T(8,128)S(1)}, f32[4,1,32,1024]{3,2,1,0:T(8,128)S(1)}, u32[]{:S(2)}, u32[]{:S(2)}) collective-permute-start(f32[4,1,32,1024]{3,2,1,0:T(8,128)S(1)} %pad_maximum_fusion.1.refs_0_), channel_id=1, source_target_pairs={{0,4},{1,17},{2,6},{3,19},{4,0},{5,21},{6,2},{7,23},{8,12},{9,25},... | collective-permute-start | bytes 1572872 | tf_op jit(solution)/shard_map/ppermute | solution.py:218
  14.5 0.9 collective-permute-start.4
  16.0 2.9 %collective-permute-start.6 = (f32[4,1,32,1024]{3,2,1,0:T(8,128)S(1)}, f32[4,1,32,1024]{3,2,1,0:T(8,128)S(1)}, u32[]{:S(2)}, u32[]{:S(2)}) collective-permute-start(f32[4,1,32,1024]{3,2,1,0:T(8,128)S(1)} %pad_maximum_fusion.1.refs_0_), channel_id=1, source_target_pairs={{0,1},{1,0},{2,3},{3,2},{4,5},{5,4},{6,7},{7,6},{8,9},{9,8},{10,11... | collective-permute-start | bytes 1572872 | tf_op jit(solution)/shard_map/ppermute | solution.py:230
  18.8 3.1 %collective-permute-done.5.refs_3_ = f32[4,1,32,1024]{3,2,1,0:T(8,128)S(1)} collective-permute-done((f32[4,1,32,1024]{3,2,1,0:T(8,128)S(1)}, f32[4,1,32,1024]{3,2,1,0:T(8,128)S(1)}, u32[]{:S(2)}, u32[]{:S(2)}) %collective-permute-start.5) | collective-permute-done | bytes 524320 | tf_op jit(solution)/shard_map/ppermute | solution.py:218
  21.9 2.5 %collective-permute-start.9 = (f32[4,1,32,1024]{3,2,1,0:T(8,128)S(1)}, f32[4,1,32,1024]{3,2,1,0:T(8,128)S(1)}, u32[]{:S(2)}, u32[]{:S(2)}) collective-permute-start(f32[4,1,32,1024]{3,2,1,0:T(8,128)S(1)} %collective-permute-done.5.refs_3_), channel_id=1, source_target_pairs={{0,1},{1,0},{2,3},{3,2},{4,5},{5,4},{6,7},{7,6},{8,9},{9,8},{10,11... | collective-permute-start | bytes 1572872 | tf_op jit(solution)/shard_map/ppermute | solution.py:230
  24.4 3.2 %collective-permute-done.4.refs_2_ = f32[4,1,32,1024]{3,2,1,0:T(8,128)S(1)} collective-permute-done((f32[4,1,32,1024]{3,2,1,0:T(8,128)S(1)}, f32[4,1,32,1024]{3,2,1,0:T(8,128)S(1)}, u32[]{:S(2)}, u32[]{:S(2)}) %collective-permute-start.4) | collective-permute-done | bytes 524320 | tf_op jit(solution)/shard_map/ppermute | solution.py:218
  27.6 2.7 %collective-permute-start.8 = (f32[4,1,32,1024]{3,2,1,0:T(8,128)S(1)}, f32[4,1,32,1024]{3,2,1,0:T(8,128)}, u32[]{:S(2)}, u32[]{:S(2)}) collective-permute-start(f32[4,1,32,1024]{3,2,1,0:T(8,128)S(1)} %collective-permute-done.4.refs_2_), channel_id=1, source_target_pairs={{0,1},{1,0},{2,3},{3,2},{4,5},{5,4},{6,7},{7,6},{8,9},{9,8},{10,11... | collective-permute-start | bytes 1572872 | tf_op jit(solution)/shard_map/ppermute | solution.py:230
  30.3 0.7 fusion.2
  32.0 0.7 collective-permute-done.7.refs_5_
  32.7 10.5 %shard_map.55 = (f32[32,1024]{1,0:T(8,128)S(1)}, f32[32,1024]{1,0:T(8,128)S(1)}, f32[1,1024]{1,0:T(1,128)S(1)}, bf16[1,1024,1024]{2,1,0:T(8,128)(2,1)}, bf16[1,1024,1024]{2,1,0:T(8,128)(2,1)}) custom-call(f32[4,1,32,1024]{3,2,1,0:T(8,128)S(1)} %pad_maximum_fusion.1.refs_0_, f32[4,1,32,1024]{3,2,1,0:T(8,128)S(1)} %collective-permute-done.3.refs_1_, ...), custom_call_target="tpu_custom_call" | custom-call | flops 4831838208 | bytes 50331648 | tf_op jit(solution)/shard_map/pallas_call | solution.py:184
  43.3 1.9 %collective-permute-start.12 = (f32[1,32,1024]{2,1,0:T(8,128)S(1)}, f32[1,32,1024]{2,1,0:T(8,128)S(1)}, u32[]{:S(2)}, u32[]{:S(2)}) collective-permute-start(f32[1,32,1024]{2,1,0:T(8,128)S(1)} %bitcast.40), channel_id=1, source_target_pairs={{0,16},{1,5},{2,18},{3,7},{4,20},{5,1},{6,22},{7,3},{8,24},{9,13},... | collective-permute-start | bytes 393224 | tf_op jit(solution)/shard_map/ppermute | solution.py:218
  45.2 1.4 collective-permute-start.11
  46.7 1.6 collective-permute-start.16
  48.3 0.7 collective-permute-done.12
  49.0 1.4 collective-permute-done.11
  50.3 1.5 collective-permute-done.10
  51.9 0.8 collective-permute-start.17
  52.7 1.6 collective-permute-start.15
  54.3 2.0 %collective-permute-start.18 = (f32[4,1,32,1024]{3,2,1,0:T(8,128)S(1)}, f32[4,1,32,1024]{3,2,1,0:T(8,128)S(1)}, u32[]{:S(2)}, u32[]{:S(2)}) collective-permute-start(f32[4,1,32,1024]{3,2,1,0:T(8,128)S(1)} %pad_maximum_fusion.2.refs_0_), channel_id=1, source_target_pairs={{0,1},{1,0},{2,3},{3,2},{4,5},{5,4},{6,7},{7,6},{8,9},{9,8},{10,11... | collective-permute-start | bytes 1572872 | tf_op jit(solution)/shard_map/ppermute | solution.py:230
  56.3 1.1 collective-permute-start.14
  57.8 4.0 %collective-permute-done.17.refs_3_ = f32[4,1,32,1024]{3,2,1,0:T(8,128)S(1)} collective-permute-done((f32[4,1,32,1024]{3,2,1,0:T(8,128)S(1)}, f32[4,1,32,1024]{3,2,1,0:T(8,128)S(1)}, u32[]{:S(2)}, u32[]{:S(2)}) %collective-permute-start.17) | collective-permute-done | bytes 524320 | tf_op jit(solution)/shard_map/ppermute | solution.py:218
  61.8 3.0 %collective-permute-done.15.refs_7_ = f32[4,1,32,1024]{3,2,1,0:T(8,128)S(1)} collective-permute-done((f32[4,1,32,1024]{3,2,1,0:T(8,128)S(1)}, f32[4,1,32,1024]{3,2,1,0:T(8,128)S(1)}, u32[]{:S(2)}, u32[]{:S(2)}) %collective-permute-start.15) | collective-permute-done | bytes 524320 | tf_op jit(solution)/shard_map/ppermute | solution.py:271
  64.8 2.5 %collective-permute-start.27 = (f32[4,1,32,1024]{3,2,1,0:T(8,128)S(1)}, f32[4,1,32,1024]{3,2,1,0:T(8,128)S(1)}, u32[]{:S(2)}, u32[]{:S(2)}) collective-permute-start(f32[4,1,32,1024]{3,2,1,0:T(8,128)S(1)} %collective-permute-done.17.refs_3_), channel_id=1, source_target_pairs={{0,1},{1,0},{2,3},{3,2},{4,5},{5,4},{6,7},{7,6},{8,9},{9,8},{10,11... | collective-permute-start | bytes 1572872 | tf_op jit(solution)/shard_map/ppermute | solution.py:230
  67.2 2.2 %collective-permute-start.23 = (f32[4,1,32,1024]{3,2,1,0:T(8,128)S(1)}, f32[4,1,32,1024]{3,2,1,0:T(8,128)}, u32[]{:S(2)}, u32[]{:S(2)}) collective-permute-start(f32[4,1,32,1024]{3,2,1,0:T(8,128)S(1)} %collective-permute-done.15.refs_7_), channel_id=1, source_target_pairs={{0,4},{1,17},{2,6},{3,19},{4,0},{5,21},{6,2},{7,23},{8,12},{9,25},... | collective-permute-start | bytes 1572872 | tf_op jit(solution)/shard_map/ppermute | solution.py:218
  69.4 1.5 collective-permute-start.22
  71.6 5.6 %collective-permute-done.23.refs_10_ = f32[4,1,32,1024]{3,2,1,0:T(8,128)} collective-permute-done((f32[4,1,32,1024]{3,2,1,0:T(8,128)S(1)}, f32[4,1,32,1024]{3,2,1,0:T(8,128)}, u32[]{:S(2)}, u32[]{:S(2)}) %collective-permute-start.23) | collective-permute-done | bytes 524320 | tf_op jit(solution)/shard_map/ppermute | solution.py:218
  77.2 1.4 collective-permute-start.26
  78.6 2.9 %collective-permute-done.22.refs_9_ = f32[4,1,32,1024]{3,2,1,0:T(8,128)} collective-permute-done((f32[4,1,32,1024]{3,2,1,0:T(8,128)S(1)}, f32[4,1,32,1024]{3,2,1,0:T(8,128)}, u32[]{:S(2)}, u32[]{:S(2)}) %collective-permute-start.22) | collective-permute-done | bytes 524320 | tf_op jit(solution)/shard_map/ppermute | solution.py:218
  81.5 1.1 collective-permute-start.25
  82.8 1.4 collective-permute-start.24
  84.4 1.6 collective-permute-done.24.refs_11_
  86.0 19.6 %shard_map.56 = (f32[32,1024]{1,0:T(8,128)S(1)}, f32[32,1024]{1,0:T(8,128)S(1)}, f32[32,1024]{1,0:T(8,128)S(1)}) custom-call(f32[4,1,32,1024]{3,2,1,0:T(8,128)S(1)} %pad_maximum_fusion.2.refs_0_, f32[4,1,32,1024]{3,2,1,0:T(8,128)S(1)} %collective-permute-done.13.refs_1_, f32[4,1,32,1024]{3,2,1,0:T(8,128)S(1)} %collective-permute-done.14.refs_2_, ...), custom_call_target="tpu_custom_call" | custom-call | flops 9663676416 | bytes 100663296 | tf_op jit(solution)/shard_map/pallas_call | solution.py:184
  105.6 3.5 %collective-permute-start.31 = (f32[32,1024]{1,0:T(8,128)S(1)}, f32[32,1024]{1,0:T(8,128)S(1)}, u32[]{:S(2)}, u32[]{:S(2)}) collective-permute-start(f32[32,1024]{1,0:T(8,128)S(1)} %get-tuple-element.36), channel_id=1, source_target_pairs={{0,64},{64,0},{32,96},{96,32},{1,65},{65,1},{33,97},{97,33},{2,66}... | collective-permute-start | bytes 393224 | tf_op jit(solution)/shard_map/ppermute | solution.py:283
  109.1 1.3 collective-permute-start.30
  110.4 0.7 collective-permute-start.29
  111.1 1.6 collective-permute-done.31
  112.7 3.0 %collective-permute-done.30 = f32[32,1024]{1,0:T(8,128)S(1)} collective-permute-done((f32[32,1024]{1,0:T(8,128)S(1)}, f32[32,1024]{1,0:T(8,128)S(1)}, u32[]{:S(2)}, u32[]{:S(2)}) %collective-permute-start.30) | collective-permute-done | bytes 131104 | tf_op jit(solution)/shard_map/ppermute | solution.py:284
  115.8 1.1 collective-permute-start.34
  116.9 1.8 collective-permute-start.33
  118.7 5.7 %collective-permute-done.34 = f32[3,32,1024]{2,1,0:T(8,128)S(1)} collective-permute-done((f32[3,32,1024]{2,1,0:T(8,128)S(1)}, f32[3,32,1024]{2,1,0:T(8,128)S(1)}, u32[]{:S(2)}, u32[]{:S(2)}) %collective-permute-start.34) | collective-permute-done | bytes 393248 | tf_op jit(solution)/shard_map/ppermute | solution.py:218
  124.4 3.3 %collective-permute-done.33 = f32[3,32,1024]{2,1,0:T(8,128)S(1)} collective-permute-done((f32[3,32,1024]{2,1,0:T(8,128)S(1)}, f32[3,32,1024]{2,1,0:T(8,128)S(1)}, u32[]{:S(2)}, u32[]{:S(2)}) %collective-permute-start.33) | collective-permute-done | bytes 393248 | tf_op jit(solution)/shard_map/ppermute | solution.py:218
  127.7 0.8 collective-permute-done.32
  128.7 2.0 %collective-permute-start.37 = (f32[4,2,32,1024]{3,2,1,0:T(8,128)S(1)}, f32[4,2,32,1024]{3,2,1,0:T(8,128)S(1)}, u32[]{:S(2)}, u32[]{:S(2)}) collective-permute-start(f32[4,2,32,1024]{3,2,1,0:T(8,128)S(1)} %pad_maximum_fusion.refs_0_), channel_id=1, source_target_pairs={{0,4},{1,17},{2,6},{3,19},{4,0},{5,21},{6,2},{7,23},{8,12},{9,25},... | collective-permute-start | bytes 3145736 | tf_op jit(solution)/shard_map/ppermute | solution.py:218
  130.7 1.7 collective-permute-start.36
  132.4 1.3 collective-permute-start.45
  133.7 2.0 %collective-permute-start.41 = (f32[4,2,32,1024]{3,2,1,0:T(8,128)S(1)}, f32[4,2,32,1024]{3,2,1,0:T(8,128)S(1)}, u32[]{:S(2)}, u32[]{:S(2)}) collective-permute-start(f32[4,2,32,1024]{3,2,1,0:T(8,128)S(1)} %pad_maximum_fusion.refs_0_), channel_id=1, source_target_pairs={{0,1},{1,0},{2,3},{3,2},{4,5},{5,4},{6,7},{7,6},{8,9},{9,8},{10,11... | collective-permute-start | bytes 3145736 | tf_op jit(solution)/shard_map/ppermute | solution.py:230
  135.6 8.6 %collective-permute-done.37.refs_3_ = f32[4,2,32,1024]{3,2,1,0:T(8,128)S(1)} collective-permute-done((f32[4,2,32,1024]{3,2,1,0:T(8,128)S(1)}, f32[4,2,32,1024]{3,2,1,0:T(8,128)S(1)}, u32[]{:S(2)}, u32[]{:S(2)}) %collective-permute-start.37) | collective-permute-done | bytes 1048608 | tf_op jit(solution)/shard_map/ppermute | solution.py:218
  144.3 3.1 %collective-permute-start.44 = (f32[4,2,32,1024]{3,2,1,0:T(8,128)S(1)}, f32[4,2,32,1024]{3,2,1,0:T(8,128)S(1)}, u32[]{:S(2)}, u32[]{:S(2)}) collective-permute-start(f32[4,2,32,1024]{3,2,1,0:T(8,128)S(1)} %collective-permute-done.37.refs_3_), channel_id=1, source_target_pairs={{0,1},{1,0},{2,3},{3,2},{4,5},{5,4},{6,7},{7,6},{8,9},{9,8},{10,11... | collective-permute-start | bytes 3145736 | tf_op jit(solution)/shard_map/ppermute | solution.py:230
  147.4 6.8 %collective-permute-done.36.refs_2_ = f32[4,2,32,1024]{3,2,1,0:T(8,128)S(1)} collective-permute-done((f32[4,2,32,1024]{3,2,1,0:T(8,128)S(1)}, f32[4,2,32,1024]{3,2,1,0:T(8,128)S(1)}, u32[]{:S(2)}, u32[]{:S(2)}) %collective-permute-start.36) | collective-permute-done | bytes 1048608 | tf_op jit(solution)/shard_map/ppermute | solution.py:218
  154.1 3.8 %collective-permute-start.43 = (f32[4,2,32,1024]{3,2,1,0:T(8,128)S(1)}, f32[4,2,32,1024]{3,2,1,0:T(8,128)S(1)}, u32[]{:S(2)}, u32[]{:S(2)}) collective-permute-start(f32[4,2,32,1024]{3,2,1,0:T(8,128)S(1)} %collective-permute-done.36.refs_2_), channel_id=1, source_target_pairs={{0,1},{1,0},{2,3},{3,2},{4,5},{5,4},{6,7},{7,6},{8,9},{9,8},{10,11... | collective-permute-start | bytes 3145736 | tf_op jit(solution)/shard_map/ppermute | solution.py:230
  158.6 2.3 %collective-permute-start.40 = (f32[4,1,32,1024]{3,2,1,0:T(8,128)S(1)}, f32[4,1,32,1024]{3,2,1,0:T(8,128)S(1)}, u32[]{:S(2)}, u32[]{:S(2)}) collective-permute-start(f32[4,1,32,1024]{3,2,1,0:T(8,128)S(1)} %pad_maximum_fusion.3.refs_0_), channel_id=1, source_target_pairs={{0,4},{1,17},{2,6},{3,19},{4,0},{5,21},{6,2},{7,23},{8,12},{9,25},... | collective-permute-start | bytes 1572872 | tf_op jit(solution)/shard_map/ppermute | solution.py:218
  160.9 0.9 collective-permute-start.39
  162.4 10.4 %shard_map.57.refs_5_ = f32[32,1024]{1,0:T(8,128)S(1)} custom-call(f32[4,2,32,1024]{3,2,1,0:T(8,128)S(1)} %pad_maximum_fusion.refs_0_, f32[4,2,32,1024]{3,2,1,0:T(8,128)S(1)} %collective-permute-done.35.refs_1_, f32[4,2,32,1024]{3,2,1,0:T(8,128)S(1)} %collective-permute-done.36.refs_2_, f32[4,2,32,1024]{3,2,1,0:T(8,128)S(1)} %collective-permute-done.37.refs_3_, ...), custom_call_target="tpu_custom_call" | custom-call | flops 4831838208 | bytes 50331648 | tf_op jit(solution)/shard_map/pallas_call | solution.py:184
  172.9 1.3 collective-permute-done.38.refs_1_
  174.2 0.9 collective-permute-start.46
  175.0 1.0 collective-permute-done.46.refs_6_
  176.0 1.8 %shard_map.58 = (f32[32,1024]{1,0:T(8,128)S(1)}, f32[32,1024]{1,0:T(8,128)S(1)}) custom-call(f32[4,1,32,1024]{3,2,1,0:T(8,128)S(1)} %pad_maximum_fusion.3.refs_0_, f32[4,1,32,1024]{3,2,1,0:T(8,128)S(1)} %collective-permute-done.38.refs_1_, f32[4,1,32,1024]{3,2,1,0:T(8,128)S(1)} %collective-permute-done.39.refs_2_, ...), custom_call_target="tpu_custom_call" | custom-call | flops 805306368 | bytes 8388608 | tf_op jit(solution)/shard_map/pallas_call | solution.py:184
  178.3 1.0 collective-permute-done.47
  179.3 0.7 add_bitcast_fusion
  (64 shorter events, 4.5 us)
Async XLA Ops:
  1.6 6.2 %collective-permute-start.1 = (f32[1,32,1024]{2,1,0:T(8,128)S(1)}, f32[1,32,1024]{2,1,0:T(8,128)S(1)}, u32[]{:S(2)}, u32[]{:S(2)}) collective-permute-start(f32[1,32,1024]{2,1,0:T(8,128)S(1)} %constant_dynamic-slice_fusion), channel_id=1, source_target_pairs={{0,24},{1,7},{2,26},{3,1},{4,28},{5,3},{6,30},{7,5},{8,0},{9,15},{... | collective-permute-start | bytes 393224 | tf_op jit(solution)/shard_map/ppermute | solution.py:218
  5.2 6.7 %collective-permute-start = (f32[1,32,1024]{2,1,0:T(8,128)S(1)}, f32[1,32,1024]{2,1,0:T(8,128)S(1)}, u32[]{:S(2)}, u32[]{:S(2)}) collective-permute-start(f32[1,32,1024]{2,1,0:T(8,128)S(1)} %constant_dynamic-slice_fusion), channel_id=1, source_target_pairs={{0,8},{1,3},{2,10},{3,5},{4,12},{5,7},{6,14},{7,1},{8,16},{9,11},{... | collective-permute-start | bytes 393224 | tf_op jit(solution)/shard_map/ppermute | solution.py:218
  5.2 6.7 %collective-permute-start.2 = (f32[1,32,1024]{2,1,0:T(8,128)S(1)}, f32[1,32,1024]{2,1,0:T(8,128)S(1)}, u32[]{:S(2)}, u32[]{:S(2)}) collective-permute-start(f32[1,32,1024]{2,1,0:T(8,128)S(1)} %constant_dynamic-slice_fusion), channel_id=1, source_target_pairs={{0,16},{1,5},{2,18},{3,7},{4,20},{5,1},{6,22},{7,3},{8,24},{9,13},... | collective-permute-start | bytes 393224 | tf_op jit(solution)/shard_map/ppermute | solution.py:218
  12.0 10.0 %collective-permute-start.5 = (f32[4,1,32,1024]{3,2,1,0:T(8,128)S(1)}, f32[4,1,32,1024]{3,2,1,0:T(8,128)S(1)}, u32[]{:S(2)}, u32[]{:S(2)}) collective-permute-start(f32[4,1,32,1024]{3,2,1,0:T(8,128)S(1)} %pad_maximum_fusion.1.refs_0_), channel_id=1, source_target_pairs={{0,4},{1,17},{2,6},{3,19},{4,0},{5,21},{6,2},{7,23},{8,12},{9,25},... | collective-permute-start | bytes 1572872 | tf_op jit(solution)/shard_map/ppermute | solution.py:218
  14.5 13.1 %collective-permute-start.4 = (f32[4,1,32,1024]{3,2,1,0:T(8,128)S(1)}, f32[4,1,32,1024]{3,2,1,0:T(8,128)S(1)}, u32[]{:S(2)}, u32[]{:S(2)}) collective-permute-start(f32[4,1,32,1024]{3,2,1,0:T(8,128)S(1)} %pad_maximum_fusion.1.refs_0_), channel_id=1, source_target_pairs={{0,6},{1,25},{2,0},{3,27},{4,2},{5,29},{6,4},{7,31},{8,14},{9,1},{... | collective-permute-start | bytes 1572872 | tf_op jit(solution)/shard_map/ppermute | solution.py:218
  15.4 14.9 %collective-permute-start.3 = (f32[4,1,32,1024]{3,2,1,0:T(8,128)S(1)}, f32[4,1,32,1024]{3,2,1,0:T(8,128)S(1)}, u32[]{:S(2)}, u32[]{:S(2)}) collective-permute-start(f32[4,1,32,1024]{3,2,1,0:T(8,128)S(1)} %pad_maximum_fusion.1.refs_0_), channel_id=1, source_target_pairs={{0,2},{1,9},{2,4},{3,11},{4,6},{5,13},{6,0},{7,15},{8,10},{9,17},{... | collective-permute-start | bytes 1572872 | tf_op jit(solution)/shard_map/ppermute | solution.py:218
  16.0 16.1 %collective-permute-start.6 = (f32[4,1,32,1024]{3,2,1,0:T(8,128)S(1)}, f32[4,1,32,1024]{3,2,1,0:T(8,128)S(1)}, u32[]{:S(2)}, u32[]{:S(2)}) collective-permute-start(f32[4,1,32,1024]{3,2,1,0:T(8,128)S(1)} %pad_maximum_fusion.1.refs_0_), channel_id=1, source_target_pairs={{0,1},{1,0},{2,3},{3,2},{4,5},{5,4},{6,7},{7,6},{8,9},{9,8},{10,11... | collective-permute-start | bytes 1572872 | tf_op jit(solution)/shard_map/ppermute | solution.py:230
  21.9 10.1 %collective-permute-start.9 = (f32[4,1,32,1024]{3,2,1,0:T(8,128)S(1)}, f32[4,1,32,1024]{3,2,1,0:T(8,128)S(1)}, u32[]{:S(2)}, u32[]{:S(2)}) collective-permute-start(f32[4,1,32,1024]{3,2,1,0:T(8,128)S(1)} %collective-permute-done.5.refs_3_), channel_id=1, source_target_pairs={{0,1},{1,0},{2,3},{3,2},{4,5},{5,4},{6,7},{7,6},{8,9},{9,8},{10,11... | collective-permute-start | bytes 1572872 | tf_op jit(solution)/shard_map/ppermute | solution.py:230
  27.6 4.4 %collective-permute-start.8 = (f32[4,1,32,1024]{3,2,1,0:T(8,128)S(1)}, f32[4,1,32,1024]{3,2,1,0:T(8,128)}, u32[]{:S(2)}, u32[]{:S(2)}) collective-permute-start(f32[4,1,32,1024]{3,2,1,0:T(8,128)S(1)} %collective-permute-done.4.refs_2_), channel_id=1, source_target_pairs={{0,1},{1,0},{2,3},{3,2},{4,5},{5,4},{6,7},{7,6},{8,9},{9,8},{10,11... | collective-permute-start | bytes 1572872 | tf_op jit(solution)/shard_map/ppermute | solution.py:230
  30.3 2.4 %collective-permute-start.7 = (f32[4,1,32,1024]{3,2,1,0:T(8,128)S(1)}, f32[4,1,32,1024]{3,2,1,0:T(8,128)}, u32[]{:S(2)}, u32[]{:S(2)}) collective-permute-start(f32[4,1,32,1024]{3,2,1,0:T(8,128)S(1)} %collective-permute-done.3.refs_1_), channel_id=1, source_target_pairs={{0,1},{1,0},{2,3},{3,2},{4,5},{5,4},{6,7},{7,6},{8,9},{9,8},{10,11... | collective-permute-start | bytes 1572872 | tf_op jit(solution)/shard_map/ppermute | solution.py:230
  43.3 5.7 %collective-permute-start.12 = (f32[1,32,1024]{2,1,0:T(8,128)S(1)}, f32[1,32,1024]{2,1,0:T(8,128)S(1)}, u32[]{:S(2)}, u32[]{:S(2)}) collective-permute-start(f32[1,32,1024]{2,1,0:T(8,128)S(1)} %bitcast.40), channel_id=1, source_target_pairs={{0,16},{1,5},{2,18},{3,7},{4,20},{5,1},{6,22},{7,3},{8,24},{9,13},... | collective-permute-start | bytes 393224 | tf_op jit(solution)/shard_map/ppermute | solution.py:218
  45.2 5.1 %collective-permute-start.11 = (f32[1,32,1024]{2,1,0:T(8,128)S(1)}, f32[1,32,1024]{2,1,0:T(8,128)S(1)}, u32[]{:S(2)}, u32[]{:S(2)}) collective-permute-start(f32[1,32,1024]{2,1,0:T(8,128)S(1)} %bitcast.41), channel_id=1, source_target_pairs={{0,24},{1,7},{2,26},{3,1},{4,28},{5,3},{6,30},{7,5},{8,0},{9,15},{... | collective-permute-start | bytes 393224 | tf_op jit(solution)/shard_map/ppermute | solution.py:218
  46.7 5.2 %collective-permute-start.10 = (f32[1,32,1024]{2,1,0:T(8,128)S(1)}, f32[1,32,1024]{2,1,0:T(8,128)S(1)}, u32[]{:S(2)}, u32[]{:S(2)}) collective-permute-start(f32[1,32,1024]{2,1,0:T(8,128)S(1)} %bitcast.42), channel_id=1, source_target_pairs={{0,8},{1,3},{2,10},{3,5},{4,12},{5,7},{6,14},{7,1},{8,16},{9,11},{... | collective-permute-start | bytes 393224 | tf_op jit(solution)/shard_map/ppermute | solution.py:218
  46.7 10.8 %collective-permute-start.16 = (f32[32,1024]{1,0:T(8,128)S(1)}, f32[32,1024]{1,0:T(8,128)S(1)}, u32[]{:S(2)}, u32[]{:S(2)}) collective-permute-start(f32[32,1024]{1,0:T(8,128)S(1)} %get-tuple-element.27.refs_21_), channel_id=1, source_target_pairs={{0,32},{32,0},{64,96},{96,64},{1,33},{33,1},{65,97},{97,65},{2,34}... | collective-permute-start | bytes 393224 | tf_op jit(solution)/shard_map/ppermute | solution.py:272
  51.9 9.9 %collective-permute-start.17 = (f32[4,1,32,1024]{3,2,1,0:T(8,128)S(1)}, f32[4,1,32,1024]{3,2,1,0:T(8,128)S(1)}, u32[]{:S(2)}, u32[]{:S(2)}) collective-permute-start(f32[4,1,32,1024]{3,2,1,0:T(8,128)S(1)} %pad_maximum_fusion.2.refs_0_), channel_id=1, source_target_pairs={{0,4},{1,17},{2,6},{3,19},{4,0},{5,21},{6,2},{7,23},{8,12},{9,25},... | collective-permute-start | bytes 1572872 | tf_op jit(solution)/shard_map/ppermute | solution.py:218
  52.7 12.1 %collective-permute-start.15 = (f32[4,1,32,1024]{3,2,1,0:T(8,128)S(1)}, f32[4,1,32,1024]{3,2,1,0:T(8,128)S(1)}, u32[]{:S(2)}, u32[]{:S(2)}) collective-permute-start(f32[4,1,32,1024]{3,2,1,0:T(8,128)S(1)} %pad_maximum_fusion.2.refs_0_), channel_id=1, source_target_pairs={{0,32},{32,0},{64,96},{96,64},{1,33},{33,1},{65,97},{97,65},{2,34}... | collective-permute-start | bytes 1572872 | tf_op jit(solution)/shard_map/ppermute | solution.py:271
  54.3 12.9 %collective-permute-start.18 = (f32[4,1,32,1024]{3,2,1,0:T(8,128)S(1)}, f32[4,1,32,1024]{3,2,1,0:T(8,128)S(1)}, u32[]{:S(2)}, u32[]{:S(2)}) collective-permute-start(f32[4,1,32,1024]{3,2,1,0:T(8,128)S(1)} %pad_maximum_fusion.2.refs_0_), channel_id=1, source_target_pairs={{0,1},{1,0},{2,3},{3,2},{4,5},{5,4},{6,7},{7,6},{8,9},{9,8},{10,11... | collective-permute-start | bytes 1572872 | tf_op jit(solution)/shard_map/ppermute | solution.py:230
  56.3 13.1 %collective-permute-start.14 = (f32[4,1,32,1024]{3,2,1,0:T(8,128)S(1)}, f32[4,1,32,1024]{3,2,1,0:T(8,128)S(1)}, u32[]{:S(2)}, u32[]{:S(2)}) collective-permute-start(f32[4,1,32,1024]{3,2,1,0:T(8,128)S(1)} %pad_maximum_fusion.2.refs_0_), channel_id=1, source_target_pairs={{0,6},{1,25},{2,0},{3,27},{4,2},{5,29},{6,4},{7,31},{8,14},{9,1},{... | collective-permute-start | bytes 1572872 | tf_op jit(solution)/shard_map/ppermute | solution.py:218
  57.5 13.5 %collective-permute-start.13 = (f32[4,1,32,1024]{3,2,1,0:T(8,128)S(1)}, f32[4,1,32,1024]{3,2,1,0:T(8,128)S(1)}, u32[]{:S(2)}, u32[]{:S(2)}) collective-permute-start(f32[4,1,32,1024]{3,2,1,0:T(8,128)S(1)} %pad_maximum_fusion.2.refs_0_), channel_id=1, source_target_pairs={{0,2},{1,9},{2,4},{3,11},{4,6},{5,13},{6,0},{7,15},{8,10},{9,17},{... | collective-permute-start | bytes 1572872 | tf_op jit(solution)/shard_map/ppermute | solution.py:218
  64.8 6.2 %collective-permute-start.27 = (f32[4,1,32,1024]{3,2,1,0:T(8,128)S(1)}, f32[4,1,32,1024]{3,2,1,0:T(8,128)S(1)}, u32[]{:S(2)}, u32[]{:S(2)}) collective-permute-start(f32[4,1,32,1024]{3,2,1,0:T(8,128)S(1)} %collective-permute-done.17.refs_3_), channel_id=1, source_target_pairs={{0,1},{1,0},{2,3},{3,2},{4,5},{5,4},{6,7},{7,6},{8,9},{9,8},{10,11... | collective-permute-start | bytes 1572872 | tf_op jit(solution)/shard_map/ppermute | solution.py:230
  67.2 4.2 %collective-permute-start.28 = (f32[4,1,32,1024]{3,2,1,0:T(8,128)S(1)}, f32[4,1,32,1024]{3,2,1,0:T(8,128)S(1)}, u32[]{:S(2)}, u32[]{:S(2)}) collective-permute-start(f32[4,1,32,1024]{3,2,1,0:T(8,128)S(1)} %collective-permute-done.15.refs_7_), channel_id=1, source_target_pairs={{0,1},{1,0},{2,3},{3,2},{4,5},{5,4},{6,7},{7,6},{8,9},{9,8},{10,11... | collective-permute-start | bytes 1572872 | tf_op jit(solution)/shard_map/ppermute | solution.py:230
  67.2 10.0 %collective-permute-start.23 = (f32[4,1,32,1024]{3,2,1,0:T(8,128)S(1)}, f32[4,1,32,1024]{3,2,1,0:T(8,128)}, u32[]{:S(2)}, u32[]{:S(2)}) collective-permute-start(f32[4,1,32,1024]{3,2,1,0:T(8,128)S(1)} %collective-permute-done.15.refs_7_), channel_id=1, source_target_pairs={{0,4},{1,17},{2,6},{3,19},{4,0},{5,21},{6,2},{7,23},{8,12},{9,25},... | collective-permute-start | bytes 1572872 | tf_op jit(solution)/shard_map/ppermute | solution.py:218
  69.4 12.0 %collective-permute-start.22 = (f32[4,1,32,1024]{3,2,1,0:T(8,128)S(1)}, f32[4,1,32,1024]{3,2,1,0:T(8,128)}, u32[]{:S(2)}, u32[]{:S(2)}) collective-permute-start(f32[4,1,32,1024]{3,2,1,0:T(8,128)S(1)} %collective-permute-done.15.refs_7_), channel_id=1, source_target_pairs={{0,6},{1,25},{2,0},{3,27},{4,2},{5,29},{6,4},{7,31},{8,14},{9,1},{... | collective-permute-start | bytes 1572872 | tf_op jit(solution)/shard_map/ppermute | solution.py:218
  71.0 11.8 %collective-permute-start.21 = (f32[4,1,32,1024]{3,2,1,0:T(8,128)S(1)}, f32[4,1,32,1024]{3,2,1,0:T(8,128)}, u32[]{:S(2)}, u32[]{:S(2)}) collective-permute-start(f32[4,1,32,1024]{3,2,1,0:T(8,128)S(1)} %collective-permute-done.15.refs_7_), channel_id=1, source_target_pairs={{0,2},{1,9},{2,4},{3,11},{4,6},{5,13},{6,0},{7,15},{8,10},{9,17},{... | collective-permute-start | bytes 1572872 | tf_op jit(solution)/shard_map/ppermute | solution.py:218
  71.0 11.8 %copy-start = (f32[4,1,32,1024]{3,2,1,0:T(8,128)}, f32[4,1,32,1024]{3,2,1,0:T(8,128)S(1)}, u32[]{:S(2)}) copy-start(f32[4,1,32,1024]{3,2,1,0:T(8,128)S(1)} %collective-permute-done.27.refs_16_) | copy-start | bytes 1572868
  71.0 13.2 %collective-permute-start.20 = (f32[4,1,32,1024]{3,2,1,0:T(8,128)S(1)}, f32[4,1,32,1024]{3,2,1,0:T(8,128)}, u32[]{:S(2)}, u32[]{:S(2)}) collective-permute-start(f32[4,1,32,1024]{3,2,1,0:T(8,128)S(1)} %collective-permute-done.14.refs_2_), channel_id=1, source_target_pairs={{0,1},{1,0},{2,3},{3,2},{4,5},{5,4},{6,7},{7,6},{8,9},{9,8},{10,11... | collective-permute-start | bytes 1572872 | tf_op jit(solution)/shard_map/ppermute | solution.py:230
  71.4 11.4 %copy-start.1 = (f32[4,1,32,1024]{3,2,1,0:T(8,128)}, f32[4,1,32,1024]{3,2,1,0:T(8,128)S(1)}, u32[]{:S(2)}) copy-start(f32[4,1,32,1024]{3,2,1,0:T(8,128)S(1)} %collective-permute-done.28.refs_17_) | copy-start | bytes 1572868
  71.4 12.8 %collective-permute-start.19 = (f32[4,1,32,1024]{3,2,1,0:T(8,128)S(1)}, f32[4,1,32,1024]{3,2,1,0:T(8,128)}, u32[]{:S(2)}, u32[]{:S(2)}) collective-permute-start(f32[4,1,32,1024]{3,2,1,0:T(8,128)S(1)} %collective-permute-done.13.refs_1_), channel_id=1, source_target_pairs={{0,1},{1,0},{2,3},{3,2},{4,5},{5,4},{6,7},{7,6},{8,9},{9,8},{10,11... | collective-permute-start | bytes 1572872 | tf_op jit(solution)/shard_map/ppermute | solution.py:230
  77.2 7.0 %collective-permute-start.26 = (f32[4,1,32,1024]{3,2,1,0:T(8,128)}, f32[4,1,32,1024]{3,2,1,0:T(8,128)}, u32[]{:S(2)}, u32[]{:S(2)}) collective-permute-start(f32[4,1,32,1024]{3,2,1,0:T(8,128)} %collective-permute-done.23.refs_10_), channel_id=1, source_target_pairs={{0,1},{1,0},{2,3},{3,2},{4,5},{5,4},{6,7},{7,6},{8,9},{9,8},{10,11... | collective-permute-start | bytes 1572872 | tf_op jit(solution)/shard_map/ppermute | solution.py:230
  81.5 2.9 %collective-permute-start.25 = (f32[4,1,32,1024]{3,2,1,0:T(8,128)}, f32[4,1,32,1024]{3,2,1,0:T(8,128)}, u32[]{:S(2)}, u32[]{:S(2)}) collective-permute-start(f32[4,1,32,1024]{3,2,1,0:T(8,128)} %collective-permute-done.22.refs_9_), channel_id=1, source_target_pairs={{0,1},{1,0},{2,3},{3,2},{4,5},{5,4},{6,7},{7,6},{8,9},{9,8},{10,11... | collective-permute-start | bytes 1572872 | tf_op jit(solution)/shard_map/ppermute | solution.py:230
  82.8 3.2 %collective-permute-start.24 = (f32[4,1,32,1024]{3,2,1,0:T(8,128)}, f32[4,1,32,1024]{3,2,1,0:T(8,128)}, u32[]{:S(2)}, u32[]{:S(2)}) collective-permute-start(f32[4,1,32,1024]{3,2,1,0:T(8,128)} %collective-permute-done.21.refs_8_), channel_id=1, source_target_pairs={{0,1},{1,0},{2,3},{3,2},{4,5},{5,4},{6,7},{7,6},{8,9},{9,8},{10,11... | collective-permute-start | bytes 1572872 | tf_op jit(solution)/shard_map/ppermute | solution.py:230
  105.6 7.1 %collective-permute-start.31 = (f32[32,1024]{1,0:T(8,128)S(1)}, f32[32,1024]{1,0:T(8,128)S(1)}, u32[]{:S(2)}, u32[]{:S(2)}) collective-permute-start(f32[32,1024]{1,0:T(8,128)S(1)} %get-tuple-element.36), channel_id=1, source_target_pairs={{0,64},{64,0},{32,96},{96,32},{1,65},{65,1},{33,97},{97,33},{2,66}... | collective-permute-start | bytes 393224 | tf_op jit(solution)/shard_map/ppermute | solution.py:283
  109.1 6.6 %collective-permute-start.30 = (f32[32,1024]{1,0:T(8,128)S(1)}, f32[32,1024]{1,0:T(8,128)S(1)}, u32[]{:S(2)}, u32[]{:S(2)}) collective-permute-start(f32[32,1024]{1,0:T(8,128)S(1)} %get-tuple-element.34), channel_id=1, source_target_pairs={{32,0},{64,96},{33,1},{65,97},{34,2},{66,98},{35,3},{67,99},{36,4}... | collective-permute-start | bytes 393224 | tf_op jit(solution)/shard_map/ppermute | solution.py:284
  110.4 5.4 %collective-permute-start.29 = (f32[32,1024]{1,0:T(8,128)S(1)}, f32[32,1024]{1,0:T(8,128)S(1)}, u32[]{:S(2)}, u32[]{:S(2)}) collective-permute-start(f32[32,1024]{1,0:T(8,128)S(1)} %get-tuple-element.34), channel_id=1, source_target_pairs={{32,64},{64,32},{33,65},{65,33},{34,66},{66,34},{35,67},{67,35},{3... | collective-permute-start | bytes 393224 | tf_op jit(solution)/shard_map/ppermute | solution.py:285
  115.8 8.5 %collective-permute-start.34 = (f32[3,32,1024]{2,1,0:T(8,128)S(1)}, f32[3,32,1024]{2,1,0:T(8,128)S(1)}, u32[]{:S(2)}, u32[]{:S(2)}) collective-permute-start(f32[3,32,1024]{2,1,0:T(8,128)S(1)} %pad_maximum_fusion.4), channel_id=1, source_target_pairs={{0,16},{1,5},{2,18},{3,7},{4,20},{5,1},{6,22},{7,3},{8,24},{9,13},... | collective-permute-start | bytes 1179656 | tf_op jit(solution)/shard_map/ppermute | solution.py:218
  116.9 10.8 %collective-permute-start.33 = (f32[3,32,1024]{2,1,0:T(8,128)S(1)}, f32[3,32,1024]{2,1,0:T(8,128)S(1)}, u32[]{:S(2)}, u32[]{:S(2)}) collective-permute-start(f32[3,32,1024]{2,1,0:T(8,128)S(1)} %pad_maximum_fusion.4), channel_id=1, source_target_pairs={{0,24},{1,7},{2,26},{3,1},{4,28},{5,3},{6,30},{7,5},{8,0},{9,15},{... | collective-permute-start | bytes 1179656 | tf_op jit(solution)/shard_map/ppermute | solution.py:218
  118.7 9.9 %collective-permute-start.32 = (f32[3,32,1024]{2,1,0:T(8,128)S(1)}, f32[3,32,1024]{2,1,0:T(8,128)S(1)}, u32[]{:S(2)}, u32[]{:S(2)}) collective-permute-start(f32[3,32,1024]{2,1,0:T(8,128)S(1)} %pad_maximum_fusion.4), channel_id=1, source_target_pairs={{0,8},{1,3},{2,10},{3,5},{4,12},{5,7},{6,14},{7,1},{8,16},{9,11},{... | collective-permute-start | bytes 1179656 | tf_op jit(solution)/shard_map/ppermute | solution.py:218
  128.7 15.6 %collective-permute-start.37 = (f32[4,2,32,1024]{3,2,1,0:T(8,128)S(1)}, f32[4,2,32,1024]{3,2,1,0:T(8,128)S(1)}, u32[]{:S(2)}, u32[]{:S(2)}) collective-permute-start(f32[4,2,32,1024]{3,2,1,0:T(8,128)S(1)} %pad_maximum_fusion.refs_0_), channel_id=1, source_target_pairs={{0,4},{1,17},{2,6},{3,19},{4,0},{5,21},{6,2},{7,23},{8,12},{9,25},... | collective-permute-start | bytes 3145736 | tf_op jit(solution)/shard_map/ppermute | solution.py:218
  130.7 23.5 %collective-permute-start.36 = (f32[4,2,32,1024]{3,2,1,0:T(8,128)S(1)}, f32[4,2,32,1024]{3,2,1,0:T(8,128)S(1)}, u32[]{:S(2)}, u32[]{:S(2)}) collective-permute-start(f32[4,2,32,1024]{3,2,1,0:T(8,128)S(1)} %pad_maximum_fusion.refs_0_), channel_id=1, source_target_pairs={{0,6},{1,25},{2,0},{3,27},{4,2},{5,29},{6,4},{7,31},{8,14},{9,1},{... | collective-permute-start | bytes 3145736 | tf_op jit(solution)/shard_map/ppermute | solution.py:218
  132.4 25.5 %collective-permute-start.35 = (f32[4,2,32,1024]{3,2,1,0:T(8,128)S(1)}, f32[4,2,32,1024]{3,2,1,0:T(8,128)S(1)}, u32[]{:S(2)}, u32[]{:S(2)}) collective-permute-start(f32[4,2,32,1024]{3,2,1,0:T(8,128)S(1)} %pad_maximum_fusion.refs_0_), channel_id=1, source_target_pairs={{0,2},{1,9},{2,4},{3,11},{4,6},{5,13},{6,0},{7,15},{8,10},{9,17},{... | collective-permute-start | bytes 3145736 | tf_op jit(solution)/shard_map/ppermute | solution.py:218
  132.4 26.2 %collective-permute-start.45 = (f32[32,1024]{1,0:T(8,128)S(1)}, f32[32,1024]{1,0:T(8,128)S(1)}, u32[]{:S(2)}, u32[]{:S(2)}) collective-permute-start(f32[32,1024]{1,0:T(8,128)S(1)} %get-tuple-element.39.refs_10_), channel_id=1, source_target_pairs={{32,0},{64,96},{33,1},{65,97},{34,2},{66,98},{35,3},{67,99},{36,4}... | collective-permute-start | bytes 393224 | tf_op jit(solution)/shard_map/ppermute | solution.py:290
  133.7 27.2 %collective-permute-start.41 = (f32[4,2,32,1024]{3,2,1,0:T(8,128)S(1)}, f32[4,2,32,1024]{3,2,1,0:T(8,128)S(1)}, u32[]{:S(2)}, u32[]{:S(2)}) collective-permute-start(f32[4,2,32,1024]{3,2,1,0:T(8,128)S(1)} %pad_maximum_fusion.refs_0_), channel_id=1, source_target_pairs={{0,1},{1,0},{2,3},{3,2},{4,5},{5,4},{6,7},{7,6},{8,9},{9,8},{10,11... | collective-permute-start | bytes 3145736 | tf_op jit(solution)/shard_map/ppermute | solution.py:230
  144.3 17.6 %collective-permute-start.44 = (f32[4,2,32,1024]{3,2,1,0:T(8,128)S(1)}, f32[4,2,32,1024]{3,2,1,0:T(8,128)S(1)}, u32[]{:S(2)}, u32[]{:S(2)}) collective-permute-start(f32[4,2,32,1024]{3,2,1,0:T(8,128)S(1)} %collective-permute-done.37.refs_3_), channel_id=1, source_target_pairs={{0,1},{1,0},{2,3},{3,2},{4,5},{5,4},{6,7},{7,6},{8,9},{9,8},{10,11... | collective-permute-start | bytes 3145736 | tf_op jit(solution)/shard_map/ppermute | solution.py:230
  154.1 8.3 %collective-permute-start.43 = (f32[4,2,32,1024]{3,2,1,0:T(8,128)S(1)}, f32[4,2,32,1024]{3,2,1,0:T(8,128)S(1)}, u32[]{:S(2)}, u32[]{:S(2)}) collective-permute-start(f32[4,2,32,1024]{3,2,1,0:T(8,128)S(1)} %collective-permute-done.36.refs_2_), channel_id=1, source_target_pairs={{0,1},{1,0},{2,3},{3,2},{4,5},{5,4},{6,7},{7,6},{8,9},{9,8},{10,11... | collective-permute-start | bytes 3145736 | tf_op jit(solution)/shard_map/ppermute | solution.py:230
  157.9 4.5 %collective-permute-start.42 = (f32[4,2,32,1024]{3,2,1,0:T(8,128)S(1)}, f32[4,2,32,1024]{3,2,1,0:T(8,128)S(1)}, u32[]{:S(2)}, u32[]{:S(2)}) collective-permute-start(f32[4,2,32,1024]{3,2,1,0:T(8,128)S(1)} %collective-permute-done.35.refs_1_), channel_id=1, source_target_pairs={{0,1},{1,0},{2,3},{3,2},{4,5},{5,4},{6,7},{7,6},{8,9},{9,8},{10,11... | collective-permute-start | bytes 3145736 | tf_op jit(solution)/shard_map/ppermute | solution.py:230
  158.6 14.2 %collective-permute-start.40 = (f32[4,1,32,1024]{3,2,1,0:T(8,128)S(1)}, f32[4,1,32,1024]{3,2,1,0:T(8,128)S(1)}, u32[]{:S(2)}, u32[]{:S(2)}) collective-permute-start(f32[4,1,32,1024]{3,2,1,0:T(8,128)S(1)} %pad_maximum_fusion.3.refs_0_), channel_id=1, source_target_pairs={{0,4},{1,17},{2,6},{3,19},{4,0},{5,21},{6,2},{7,23},{8,12},{9,25},... | collective-permute-start | bytes 1572872 | tf_op jit(solution)/shard_map/ppermute | solution.py:218
  160.9 12.0 %collective-permute-start.39 = (f32[4,1,32,1024]{3,2,1,0:T(8,128)S(1)}, f32[4,1,32,1024]{3,2,1,0:T(8,128)S(1)}, u32[]{:S(2)}, u32[]{:S(2)}) collective-permute-start(f32[4,1,32,1024]{3,2,1,0:T(8,128)S(1)} %pad_maximum_fusion.3.refs_0_), channel_id=1, source_target_pairs={{0,6},{1,25},{2,0},{3,27},{4,2},{5,29},{6,4},{7,31},{8,14},{9,1},{... | collective-permute-start | bytes 1572872 | tf_op jit(solution)/shard_map/ppermute | solution.py:218
  161.9 12.3 %collective-permute-start.38 = (f32[4,1,32,1024]{3,2,1,0:T(8,128)S(1)}, f32[4,1,32,1024]{3,2,1,0:T(8,128)S(1)}, u32[]{:S(2)}, u32[]{:S(2)}) collective-permute-start(f32[4,1,32,1024]{3,2,1,0:T(8,128)S(1)} %pad_maximum_fusion.3.refs_0_), channel_id=1, source_target_pairs={{0,2},{1,9},{2,4},{3,11},{4,6},{5,13},{6,0},{7,15},{8,10},{9,17},{... | collective-permute-start | bytes 1572872 | tf_op jit(solution)/shard_map/ppermute | solution.py:218
  174.2 1.8 %collective-permute-start.46 = (f32[32,1024]{1,0:T(8,128)S(1)}, f32[32,1024]{1,0:T(8,128)S(1)}, u32[]{:S(2)}, u32[]{:S(2)}) collective-permute-start(f32[32,1024]{1,0:T(8,128)S(1)} %shard_map.57.refs_5_), channel_id=1, source_target_pairs={{0,1},{1,0},{2,3},{3,2},{4,5},{5,4},{6,7},{7,6},{8,9},{9,8},{10,11... | collective-permute-start | bytes 393224 | tf_op jit(solution)/shard_map/ppermute | solution.py:230
  177.8 1.4 collective-permute-start.47

commit v6 on v5

--- a/solution.py
+++ b/solution.py
@@ -257,6 +257,7 @@
     inner_flag = inner.astype(jnp.int32)[None]
     facts = jnp.stack([panel * panel_rows, material[0]])
     own = lax.dynamic_index_in_dim(reflections, material[0], 0, keepdims=False)
+    own, places, facts = lax.optimization_barrier((own, places, facts))
     block = pltpu.VMEM(rows, jnp.float32)
     refl, trans, decays, *halved = call(
         layer_kernel, 10, 2 * TERMS, (block, block, pltpu.VMEM((1, order), jnp.float32), *matrices(1, order, pltpu.HBM)),
@@ -286,7 +287,6 @@
     blocks = jnp.stack(
         [jnp.where(inner, cross, near), jnp.where(inner, refl, far), jnp.where(inner, far, trans)]
     )
-    trans, blocks = lax.optimization_barrier((trans, blocks))
     near_trans = lax.ppermute(trans, "layer", [(1, 0), (2, 3)])
     line = line_of(blocks)
     mine = spread(jnp.stack([part[:2] for part in line]))

time: 181 us -> 190 us (1.050)
  waiting for transfers between devices: 65.4 us -> 71.1 us
  starting transfers between devices: 66.6 us -> 72.2 us
    ppermute x1, waiting for transfers between devices: 0.01 us -> 5.62 us  [local(): near_trans = lax.ppermute(trans, 'layer', [(1, 0), (2, 3)])]
    ppermute x18, starting transfers between devices: 27.6 us -> 30.9 us  [other_core(): lax.ppermute(block, 'panel', [(i, i ^ 1) for i in range(2 * SIDE * SIDE)])]
    ppermute x1, starting transfers between devices: 3.5 us -> 6.71 us  [local(): far = lax.ppermute(away, 'layer', [(0, 2), (2, 0), (1, 3), (3, 1)])]
    ppermute x1, waiting for transfers between devices: 3.05 us -> 0.01 us  [local(): near = lax.ppermute(refl, 'layer', [(1, 0), (2, 3)])]
    ppermute x1, waiting for transfers between devices: 1.6 us -> 4.05 us  [local(): far = lax.ppermute(away, 'layer', [(0, 2), (2, 0), (1, 3), (3, 1)])]
  transfers between devices with their start and end apart: 48 -> 48, of which waited for: 25 -> 28; matrix products, arithmetic and copies ran while one was open for 1% -> 0% of each run, Pallas kernels for 6% -> 5%
where the time goes in v6:
time: 190 us
  starting transfers between devices  72.2 us (38%)
  waiting for transfers between devices  71.1 us (37%)
  Pallas kernels  41.7 us (22%)
    ppermute x24, waiting for transfers between devices, moved(): return lax.ppermute(block, 'panel', route)  54.3 us
    pallas_call x4, Pallas kernels, call(): pl.pallas_call(kernel, out_shape=tuple((out if placed else jax.ShapeDtype...  41.7 us
    ppermute x18, starting transfers between devices, other_core(): lax.ppermute(block, 'panel', [(i, i ^ 1) for i in range(2 * SIDE * SIDE)])  30.9 us
    ppermute x24, starting transfers between devices, moved(): return lax.ppermute(block, 'panel', route)  28.1 us
    ppermute x1, starting transfers between devices, local(): far = lax.ppermute(away, 'layer', [(0, 2), (2, 0), (1, 3), (3, 1)])  6.71 us
    ppermute x1, waiting for transfers between devices, local(): near_trans = lax.ppermute(trans, 'layer', [(1, 0), (2, 3)])  5.62 us
    ppermute x18, waiting for transfers between devices, other_core(): lax.ppermute(block, 'panel', [(i, i ^ 1) for i in range(2 * SIDE * SIDE)])  5.48 us
    ppermute x1, waiting for transfers between devices, local(): far = lax.ppermute(away, 'layer', [(0, 2), (2, 0), (1, 3), (3, 1)])  4.05 us
  transfers between devices with their start and end apart: 48, of which 28 were waited for; matrix products, arithmetic and copies ran while one was open for 0% of the time, Pallas kernels for 5%

profile of v6, /device:TPU:1, one launch (start us, length us, event | category | flops | bytes accessed | tf_op | source)
XLA Modules:
  0.0 189.6 jit_solution(6423962628163304037)
XLA Ops:
  1.7 0.9 dynamic-slice_bitcast_fusion
  2.6 3.8 %collective-permute-start.2 = (f32[1,32,1024]{2,1,0:T(8,128)S(1)}, f32[1,32,1024]{2,1,0:T(8,128)S(1)}, u32[]{:S(2)}, u32[]{:S(2)}) collective-permute-start(f32[1,32,1024]{2,1,0:T(8,128)S(1)} %bitcast.46), channel_id=1, source_target_pairs={{0,16},{1,5},{2,18},{3,7},{4,20},{5,1},{6,22},{7,3},{8,24},{9,13},... | collective-permute-start | bytes 393224 | tf_op jit(solution)/shard_map/ppermute | solution.py:218
  6.5 0.8 collective-permute-start.1
  7.2 0.7 collective-permute-start
  7.9 1.2 collective-permute-done.2
  9.1 1.8 collective-permute-done.1
  10.9 1.4 collective-permute-done
  12.3 2.8 %collective-permute-start.5 = (f32[4,1,32,1024]{3,2,1,0:T(8,128)S(1)}, f32[4,1,32,1024]{3,2,1,0:T(8,128)S(1)}, u32[]{:S(2)}, u32[]{:S(2)}) collective-permute-start(f32[4,1,32,1024]{3,2,1,0:T(8,128)S(1)} %pad_maximum_fusion.1.refs_0_), channel_id=1, source_target_pairs={{0,4},{1,17},{2,6},{3,19},{4,0},{5,21},{6,2},{7,23},{8,12},{9,25},... | collective-permute-start | bytes 1572872 | tf_op jit(solution)/shard_map/ppermute | solution.py:218
  15.1 0.9 collective-permute-start.4
  16.6 3.3 %collective-permute-start.6 = (f32[4,1,32,1024]{3,2,1,0:T(8,128)S(1)}, f32[4,1,32,1024]{3,2,1,0:T(8,128)S(1)}, u32[]{:S(2)}, u32[]{:S(2)}) collective-permute-start(f32[4,1,32,1024]{3,2,1,0:T(8,128)S(1)} %pad_maximum_fusion.1.refs_0_), channel_id=1, source_target_pairs={{0,1},{1,0},{2,3},{3,2},{4,5},{5,4},{6,7},{7,6},{8,9},{9,8},{10,11... | collective-permute-start | bytes 1572872 | tf_op jit(solution)/shard_map/ppermute | solution.py:230
  19.9 2.4 %collective-permute-done.5.refs_3_ = f32[4,1,32,1024]{3,2,1,0:T(8,128)S(1)} collective-permute-done((f32[4,1,32,1024]{3,2,1,0:T(8,128)S(1)}, f32[4,1,32,1024]{3,2,1,0:T(8,128)S(1)}, u32[]{:S(2)}, u32[]{:S(2)}) %collective-permute-start.5) | collective-permute-done | bytes 524320 | tf_op jit(solution)/shard_map/ppermute | solution.py:218
  22.3 3.2 %collective-permute-start.9 = (f32[4,1,32,1024]{3,2,1,0:T(8,128)S(1)}, f32[4,1,32,1024]{3,2,1,0:T(8,128)S(1)}, u32[]{:S(2)}, u32[]{:S(2)}) collective-permute-start(f32[4,1,32,1024]{3,2,1,0:T(8,128)S(1)} %collective-permute-done.5.refs_3_), channel_id=1, source_target_pairs={{0,1},{1,0},{2,3},{3,2},{4,5},{5,4},{6,7},{7,6},{8,9},{9,8},{10,11... | collective-permute-start | bytes 1572872 | tf_op jit(solution)/shard_map/ppermute | solution.py:230
  25.5 2.5 %collective-permute-done.4.refs_2_ = f32[4,1,32,1024]{3,2,1,0:T(8,128)S(1)} collective-permute-done((f32[4,1,32,1024]{3,2,1,0:T(8,128)S(1)}, f32[4,1,32,1024]{3,2,1,0:T(8,128)S(1)}, u32[]{:S(2)}, u32[]{:S(2)}) %collective-permute-start.4) | collective-permute-done | bytes 524320 | tf_op jit(solution)/shard_map/ppermute | solution.py:218
  28.0 3.4 %collective-permute-start.8 = (f32[4,1,32,1024]{3,2,1,0:T(8,128)S(1)}, f32[4,1,32,1024]{3,2,1,0:T(8,128)S(1)}, u32[]{:S(2)}, u32[]{:S(2)}) collective-permute-start(f32[4,1,32,1024]{3,2,1,0:T(8,128)S(1)} %collective-permute-done.4.refs_2_), channel_id=1, source_target_pairs={{0,1},{1,0},{2,3},{3,2},{4,5},{5,4},{6,7},{7,6},{8,9},{9,8},{10,11... | collective-permute-start | bytes 1572872 | tf_op jit(solution)/shard_map/ppermute | solution.py:230
  32.1 0.9 collective-permute-done.8.refs_6_
  32.9 0.7 collective-permute-done.7.refs_5_
  33.7 9.9 %shard_map.55 = (f32[32,1024]{1,0:T(8,128)S(1)}, f32[32,1024]{1,0:T(8,128)S(1)}, f32[1,1024]{1,0:T(1,128)S(1)}, bf16[1,1024,1024]{2,1,0:T(8,128)(2,1)}, bf16[1,1024,1024]{2,1,0:T(8,128)(2,1)}) custom-call(f32[4,1,32,1024]{3,2,1,0:T(8,128)S(1)} %pad_maximum_fusion.1.refs_0_, f32[4,1,32,1024]{3,2,1,0:T(8,128)S(1)} %collective-permute-done.3.refs_1_, ...), custom_call_target="tpu_custom_call" | custom-call | flops 4831838208 | bytes 50331648 | tf_op jit(solution)/shard_map/pallas_call | solution.py:184
  43.5 1.9 collective-permute-start.12
  45.4 1.5 collective-permute-start.11
  46.9 1.6 collective-permute-start.16
  49.2 1.4 collective-permute-done.11
  50.6 1.5 collective-permute-done.10
  52.4 1.6 collective-permute-start.15
  54.0 2.6 %collective-permute-start.18 = (f32[4,1,32,1024]{3,2,1,0:T(8,128)S(1)}, f32[4,1,32,1024]{3,2,1,0:T(8,128)S(1)}, u32[]{:S(2)}, u32[]{:S(2)}) collective-permute-start(f32[4,1,32,1024]{3,2,1,0:T(8,128)S(1)} %pad_maximum_fusion.2.refs_0_), channel_id=1, source_target_pairs={{0,1},{1,0},{2,3},{3,2},{4,5},{5,4},{6,7},{7,6},{8,9},{9,8},{10,11... | collective-permute-start | bytes 1572872 | tf_op jit(solution)/shard_map/ppermute | solution.py:230
  56.9 1.2 collective-permute-start.13
  58.1 4.0 %collective-permute-done.17.refs_3_ = f32[4,1,32,1024]{3,2,1,0:T(8,128)S(1)} collective-permute-done((f32[4,1,32,1024]{3,2,1,0:T(8,128)S(1)}, f32[4,1,32,1024]{3,2,1,0:T(8,128)S(1)}, u32[]{:S(2)}, u32[]{:S(2)}) %collective-permute-start.17) | collective-permute-done | bytes 524320 | tf_op jit(solution)/shard_map/ppermute | solution.py:218
  62.1 1.7 collective-permute-done.15.refs_7_
  63.8 3.1 %collective-permute-start.27 = (f32[4,1,32,1024]{3,2,1,0:T(8,128)S(1)}, f32[4,1,32,1024]{3,2,1,0:T(8,128)S(1)}, u32[]{:S(2)}, u32[]{:S(2)}) collective-permute-start(f32[4,1,32,1024]{3,2,1,0:T(8,128)S(1)} %collective-permute-done.17.refs_3_), channel_id=1, source_target_pairs={{0,1},{1,0},{2,3},{3,2},{4,5},{5,4},{6,7},{7,6},{8,9},{9,8},{10,11... | collective-permute-start | bytes 1572872 | tf_op jit(solution)/shard_map/ppermute | solution.py:230
  66.9 2.2 %collective-permute-start.23 = (f32[4,1,32,1024]{3,2,1,0:T(8,128)S(1)}, f32[4,1,32,1024]{3,2,1,0:T(8,128)}, u32[]{:S(2)}, u32[]{:S(2)}) collective-permute-start(f32[4,1,32,1024]{3,2,1,0:T(8,128)S(1)} %collective-permute-done.15.refs_7_), channel_id=1, source_target_pairs={{0,4},{1,17},{2,6},{3,19},{4,0},{5,21},{6,2},{7,23},{8,12},{9,25},... | collective-permute-start | bytes 1572872 | tf_op jit(solution)/shard_map/ppermute | solution.py:218
  69.6 0.9 collective-permute-start.21
  70.5 1.2 collective-permute-start.20
  71.8 5.1 %collective-permute-done.23.refs_10_ = f32[4,1,32,1024]{3,2,1,0:T(8,128)} collective-permute-done((f32[4,1,32,1024]{3,2,1,0:T(8,128)S(1)}, f32[4,1,32,1024]{3,2,1,0:T(8,128)}, u32[]{:S(2)}, u32[]{:S(2)}) %collective-permute-start.23) | collective-permute-done | bytes 524320 | tf_op jit(solution)/shard_map/ppermute | solution.py:218
  76.8 1.4 collective-permute-start.26
  78.3 3.3 %collective-permute-done.22.refs_9_ = f32[4,1,32,1024]{3,2,1,0:T(8,128)} collective-permute-done((f32[4,1,32,1024]{3,2,1,0:T(8,128)S(1)}, f32[4,1,32,1024]{3,2,1,0:T(8,128)}, u32[]{:S(2)}, u32[]{:S(2)}) %collective-permute-start.22) | collective-permute-done | bytes 524320 | tf_op jit(solution)/shard_map/ppermute | solution.py:218
  82.4 1.4 collective-permute-start.24
  84.1 1.6 collective-permute-done.24.refs_11_
  85.7 19.6 %shard_map.56 = (f32[32,1024]{1,0:T(8,128)S(1)}, f32[32,1024]{1,0:T(8,128)S(1)}, f32[32,1024]{1,0:T(8,128)S(1)}) custom-call(f32[4,1,32,1024]{3,2,1,0:T(8,128)S(1)} %pad_maximum_fusion.2.refs_0_, f32[4,1,32,1024]{3,2,1,0:T(8,128)S(1)} %collective-permute-done.13.refs_1_, f32[4,1,32,1024]{3,2,1,0:T(8,128)S(1)} %collective-permute-done.14.refs_2_, ...), custom_call_target="tpu_custom_call" | custom-call | flops 9663676416 | bytes 100663296 | tf_op jit(solution)/shard_map/pallas_call | solution.py:184
  105.3 1.3 collective-permute-start.31
  107.3 6.7 %collective-permute-start.29 = (f32[32,1024]{1,0:T(8,128)S(1)}, f32[32,1024]{1,0:T(8,128)S(1)}, u32[]{:S(2)}, u32[]{:S(2)}) collective-permute-start(f32[32,1024]{1,0:T(8,128)S(1)} %get-tuple-element.39), channel_id=1, source_target_pairs={{0,64},{64,0},{32,96},{96,32},{1,65},{65,1},{33,97},{97,33},{2,66}... | collective-permute-start | bytes 393224 | tf_op jit(solution)/shard_map/ppermute | solution.py:284
  114.0 4.0 %collective-permute-done.29 = f32[32,1024]{1,0:T(8,128)S(1)} collective-permute-done((f32[32,1024]{1,0:T(8,128)S(1)}, f32[32,1024]{1,0:T(8,128)S(1)}, u32[]{:S(2)}, u32[]{:S(2)}) %collective-permute-start.29) | collective-permute-done | bytes 131104 | tf_op jit(solution)/shard_map/ppermute | solution.py:284
  118.1 1.1 collective-permute-start.34
  119.2 1.7 collective-permute-start.33
  121.0 5.7 %collective-permute-done.34 = f32[3,32,1024]{2,1,0:T(8,128)S(1)} collective-permute-done((f32[3,32,1024]{2,1,0:T(8,128)S(1)}, f32[3,32,1024]{2,1,0:T(8,128)S(1)}, u32[]{:S(2)}, u32[]{:S(2)}) %collective-permute-start.34) | collective-permute-done | bytes 393248 | tf_op jit(solution)/shard_map/ppermute | solution.py:218
  126.7 3.3 %collective-permute-done.33 = f32[3,32,1024]{2,1,0:T(8,128)S(1)} collective-permute-done((f32[3,32,1024]{2,1,0:T(8,128)S(1)}, f32[3,32,1024]{2,1,0:T(8,128)S(1)}, u32[]{:S(2)}, u32[]{:S(2)}) %collective-permute-start.33) | collective-permute-done | bytes 393248 | tf_op jit(solution)/shard_map/ppermute | solution.py:218
  130.0 0.8 collective-permute-done.32
  131.0 2.0 %collective-permute-start.37 = (f32[4,2,32,1024]{3,2,1,0:T(8,128)S(1)}, f32[4,2,32,1024]{3,2,1,0:T(8,128)S(1)}, u32[]{:S(2)}, u32[]{:S(2)}) collective-permute-start(f32[4,2,32,1024]{3,2,1,0:T(8,128)S(1)} %pad_maximum_fusion.refs_0_), channel_id=1, source_target_pairs={{0,4},{1,17},{2,6},{3,19},{4,0},{5,21},{6,2},{7,23},{8,12},{9,25},... | collective-permute-start | bytes 3145736 | tf_op jit(solution)/shard_map/ppermute | solution.py:218
  133.5 1.0 collective-permute-start.35
  134.5 1.9 collective-permute-start.41
  136.4 10.2 %collective-permute-done.37.refs_3_ = f32[4,2,32,1024]{3,2,1,0:T(8,128)S(1)} collective-permute-done((f32[4,2,32,1024]{3,2,1,0:T(8,128)S(1)}, f32[4,2,32,1024]{3,2,1,0:T(8,128)S(1)}, u32[]{:S(2)}, u32[]{:S(2)}) %collective-permute-start.37) | collective-permute-done | bytes 1048608 | tf_op jit(solution)/shard_map/ppermute | solution.py:218
  146.5 2.9 %collective-permute-start.44 = (f32[4,2,32,1024]{3,2,1,0:T(8,128)S(1)}, f32[4,2,32,1024]{3,2,1,0:T(8,128)S(1)}, u32[]{:S(2)}, u32[]{:S(2)}) collective-permute-start(f32[4,2,32,1024]{3,2,1,0:T(8,128)S(1)} %collective-permute-done.37.refs_3_), channel_id=1, source_target_pairs={{0,1},{1,0},{2,3},{3,2},{4,5},{5,4},{6,7},{7,6},{8,9},{9,8},{10,11... | collective-permute-start | bytes 3145736 | tf_op jit(solution)/shard_map/ppermute | solution.py:230
  149.5 7.4 %collective-permute-done.36.refs_2_ = f32[4,2,32,1024]{3,2,1,0:T(8,128)S(1)} collective-permute-done((f32[4,2,32,1024]{3,2,1,0:T(8,128)S(1)}, f32[4,2,32,1024]{3,2,1,0:T(8,128)S(1)}, u32[]{:S(2)}, u32[]{:S(2)}) %collective-permute-start.36) | collective-permute-done | bytes 1048608 | tf_op jit(solution)/shard_map/ppermute | solution.py:218
  156.9 2.8 %collective-permute-start.43 = (f32[4,2,32,1024]{3,2,1,0:T(8,128)S(1)}, f32[4,2,32,1024]{3,2,1,0:T(8,128)S(1)}, u32[]{:S(2)}, u32[]{:S(2)}) collective-permute-start(f32[4,2,32,1024]{3,2,1,0:T(8,128)S(1)} %collective-permute-done.36.refs_2_), channel_id=1, source_target_pairs={{0,1},{1,0},{2,3},{3,2},{4,5},{5,4},{6,7},{7,6},{8,9},{9,8},{10,11... | collective-permute-start | bytes 3145736 | tf_op jit(solution)/shard_map/ppermute | solution.py:230
  159.7 0.9 collective-permute-start.42
  160.6 1.3 collective-permute-start.45
  162.0 5.6 %collective-permute-done.45.refs_11_ = f32[32,1024]{1,0:T(8,128)S(1)} collective-permute-done((f32[32,1024]{1,0:T(8,128)S(1)}, f32[32,1024]{1,0:T(8,128)S(1)}, u32[]{:S(2)}, u32[]{:S(2)}) %collective-permute-start.45) | collective-permute-done | bytes 131104 | tf_op jit(solution)/shard_map/ppermute | solution.py:290
  167.6 2.1 %collective-permute-start.40 = (f32[4,1,32,1024]{3,2,1,0:T(8,128)S(1)}, f32[4,1,32,1024]{3,2,1,0:T(8,128)S(1)}, u32[]{:S(2)}, u32[]{:S(2)}) collective-permute-start(f32[4,1,32,1024]{3,2,1,0:T(8,128)S(1)} %pad_maximum_fusion.3.refs_0_), channel_id=1, source_target_pairs={{0,4},{1,17},{2,6},{3,19},{4,0},{5,21},{6,2},{7,23},{8,12},{9,25},... | collective-permute-start | bytes 1572872 | tf_op jit(solution)/shard_map/ppermute | solution.py:218
  169.7 0.9 collective-permute-start.39
  171.1 10.4 %shard_map.57.refs_5_ = f32[32,1024]{1,0:T(8,128)S(1)} custom-call(f32[4,2,32,1024]{3,2,1,0:T(8,128)S(1)} %pad_maximum_fusion.refs_0_, f32[4,2,32,1024]{3,2,1,0:T(8,128)S(1)} %collective-permute-done.35.refs_1_, f32[4,2,32,1024]{3,2,1,0:T(8,128)S(1)} %collective-permute-done.36.refs_2_, f32[4,2,32,1024]{3,2,1,0:T(8,128)S(1)} %collective-permute-done.37.refs_3_, ...), custom_call_target="tpu_custom_call" | custom-call | flops 4831838208 | bytes 50331648 | tf_op jit(solution)/shard_map/pallas_call | solution.py:184
  181.6 0.7 collective-permute-done.39.refs_2_
  182.2 0.8 collective-permute-done.38.refs_1_
  183.0 1.6 collective-permute-start.46
  184.7 1.0 collective-permute-done.46.refs_6_
  185.7 1.8 shard_map.58
  187.9 1.0 collective-permute-done.47
  (62 shorter events, 7.8 us)
Async XLA Ops:
  2.6 6.5 %collective-permute-start.2 = (f32[1,32,1024]{2,1,0:T(8,128)S(1)}, f32[1,32,1024]{2,1,0:T(8,128)S(1)}, u32[]{:S(2)}, u32[]{:S(2)}) collective-permute-start(f32[1,32,1024]{2,1,0:T(8,128)S(1)} %bitcast.46), channel_id=1, source_target_pairs={{0,16},{1,5},{2,18},{3,7},{4,20},{5,1},{6,22},{7,3},{8,24},{9,13},... | collective-permute-start | bytes 393224 | tf_op jit(solution)/shard_map/ppermute | solution.py:218
  6.5 4.4 %collective-permute-start.1 = (f32[1,32,1024]{2,1,0:T(8,128)S(1)}, f32[1,32,1024]{2,1,0:T(8,128)S(1)}, u32[]{:S(2)}, u32[]{:S(2)}) collective-permute-start(f32[1,32,1024]{2,1,0:T(8,128)S(1)} %bitcast.47), channel_id=1, source_target_pairs={{0,24},{1,7},{2,26},{3,1},{4,28},{5,3},{6,30},{7,5},{8,0},{9,15},{... | collective-permute-start | bytes 393224 | tf_op jit(solution)/shard_map/ppermute | solution.py:218
  7.2 5.0 %collective-permute-start = (f32[1,32,1024]{2,1,0:T(8,128)S(1)}, f32[1,32,1024]{2,1,0:T(8,128)S(1)}, u32[]{:S(2)}, u32[]{:S(2)}) collective-permute-start(f32[1,32,1024]{2,1,0:T(8,128)S(1)} %bitcast.48), channel_id=1, source_target_pairs={{0,8},{1,3},{2,10},{3,5},{4,12},{5,7},{6,14},{7,1},{8,16},{9,11},{... | collective-permute-start | bytes 393224 | tf_op jit(solution)/shard_map/ppermute | solution.py:218
  12.3 10.0 %collective-permute-start.5 = (f32[4,1,32,1024]{3,2,1,0:T(8,128)S(1)}, f32[4,1,32,1024]{3,2,1,0:T(8,128)S(1)}, u32[]{:S(2)}, u32[]{:S(2)}) collective-permute-start(f32[4,1,32,1024]{3,2,1,0:T(8,128)S(1)} %pad_maximum_fusion.1.refs_0_), channel_id=1, source_target_pairs={{0,4},{1,17},{2,6},{3,19},{4,0},{5,21},{6,2},{7,23},{8,12},{9,25},... | collective-permute-start | bytes 1572872 | tf_op jit(solution)/shard_map/ppermute | solution.py:218
  15.1 12.8 %collective-permute-start.4 = (f32[4,1,32,1024]{3,2,1,0:T(8,128)S(1)}, f32[4,1,32,1024]{3,2,1,0:T(8,128)S(1)}, u32[]{:S(2)}, u32[]{:S(2)}) collective-permute-start(f32[4,1,32,1024]{3,2,1,0:T(8,128)S(1)} %pad_maximum_fusion.1.refs_0_), channel_id=1, source_target_pairs={{0,6},{1,25},{2,0},{3,27},{4,2},{5,29},{6,4},{7,31},{8,14},{9,1},{... | collective-permute-start | bytes 1572872 | tf_op jit(solution)/shard_map/ppermute | solution.py:218
  16.0 15.4 %collective-permute-start.3 = (f32[4,1,32,1024]{3,2,1,0:T(8,128)S(1)}, f32[4,1,32,1024]{3,2,1,0:T(8,128)S(1)}, u32[]{:S(2)}, u32[]{:S(2)}) collective-permute-start(f32[4,1,32,1024]{3,2,1,0:T(8,128)S(1)} %pad_maximum_fusion.1.refs_0_), channel_id=1, source_target_pairs={{0,2},{1,9},{2,4},{3,11},{4,6},{5,13},{6,0},{7,15},{8,10},{9,17},{... | collective-permute-start | bytes 1572872 | tf_op jit(solution)/shard_map/ppermute | solution.py:218
  16.6 15.4 %collective-permute-start.6 = (f32[4,1,32,1024]{3,2,1,0:T(8,128)S(1)}, f32[4,1,32,1024]{3,2,1,0:T(8,128)S(1)}, u32[]{:S(2)}, u32[]{:S(2)}) collective-permute-start(f32[4,1,32,1024]{3,2,1,0:T(8,128)S(1)} %pad_maximum_fusion.1.refs_0_), channel_id=1, source_target_pairs={{0,1},{1,0},{2,3},{3,2},{4,5},{5,4},{6,7},{7,6},{8,9},{9,8},{10,11... | collective-permute-start | bytes 1572872 | tf_op jit(solution)/shard_map/ppermute | solution.py:230
  22.3 9.8 %collective-permute-start.9 = (f32[4,1,32,1024]{3,2,1,0:T(8,128)S(1)}, f32[4,1,32,1024]{3,2,1,0:T(8,128)S(1)}, u32[]{:S(2)}, u32[]{:S(2)}) collective-permute-start(f32[4,1,32,1024]{3,2,1,0:T(8,128)S(1)} %collective-permute-done.5.refs_3_), channel_id=1, source_target_pairs={{0,1},{1,0},{2,3},{3,2},{4,5},{5,4},{6,7},{7,6},{8,9},{9,8},{10,11... | collective-permute-start | bytes 1572872 | tf_op jit(solution)/shard_map/ppermute | solution.py:230
  28.0 4.9 %collective-permute-start.8 = (f32[4,1,32,1024]{3,2,1,0:T(8,128)S(1)}, f32[4,1,32,1024]{3,2,1,0:T(8,128)S(1)}, u32[]{:S(2)}, u32[]{:S(2)}) collective-permute-start(f32[4,1,32,1024]{3,2,1,0:T(8,128)S(1)} %collective-permute-done.4.refs_2_), channel_id=1, source_target_pairs={{0,1},{1,0},{2,3},{3,2},{4,5},{5,4},{6,7},{7,6},{8,9},{9,8},{10,11... | collective-permute-start | bytes 1572872 | tf_op jit(solution)/shard_map/ppermute | solution.py:230
  31.4 2.3 %collective-permute-start.7 = (f32[4,1,32,1024]{3,2,1,0:T(8,128)S(1)}, f32[4,1,32,1024]{3,2,1,0:T(8,128)S(1)}, u32[]{:S(2)}, u32[]{:S(2)}) collective-permute-start(f32[4,1,32,1024]{3,2,1,0:T(8,128)S(1)} %collective-permute-done.3.refs_1_), channel_id=1, source_target_pairs={{0,1},{1,0},{2,3},{3,2},{4,5},{5,4},{6,7},{7,6},{8,9},{9,8},{10,11... | collective-permute-start | bytes 1572872 | tf_op jit(solution)/shard_map/ppermute | solution.py:230
  43.5 5.7 %collective-permute-start.12 = (f32[1,32,1024]{2,1,0:T(8,128)S(1)}, f32[1,32,1024]{2,1,0:T(8,128)S(1)}, u32[]{:S(2)}, u32[]{:S(2)}) collective-permute-start(f32[1,32,1024]{2,1,0:T(8,128)S(1)} %bitcast.42), channel_id=1, source_target_pairs={{0,16},{1,5},{2,18},{3,7},{4,20},{5,1},{6,22},{7,3},{8,24},{9,13},... | collective-permute-start | bytes 393224 | tf_op jit(solution)/shard_map/ppermute | solution.py:218
  45.4 5.2 %collective-permute-start.11 = (f32[1,32,1024]{2,1,0:T(8,128)S(1)}, f32[1,32,1024]{2,1,0:T(8,128)S(1)}, u32[]{:S(2)}, u32[]{:S(2)}) collective-permute-start(f32[1,32,1024]{2,1,0:T(8,128)S(1)} %bitcast.43), channel_id=1, source_target_pairs={{0,24},{1,7},{2,26},{3,1},{4,28},{5,3},{6,30},{7,5},{8,0},{9,15},{... | collective-permute-start | bytes 393224 | tf_op jit(solution)/shard_map/ppermute | solution.py:218
  46.9 5.2 %collective-permute-start.10 = (f32[1,32,1024]{2,1,0:T(8,128)S(1)}, f32[1,32,1024]{2,1,0:T(8,128)S(1)}, u32[]{:S(2)}, u32[]{:S(2)}) collective-permute-start(f32[1,32,1024]{2,1,0:T(8,128)S(1)} %bitcast.44), channel_id=1, source_target_pairs={{0,8},{1,3},{2,10},{3,5},{4,12},{5,7},{6,14},{7,1},{8,16},{9,11},{... | collective-permute-start | bytes 393224 | tf_op jit(solution)/shard_map/ppermute | solution.py:218
  46.9 10.0 %collective-permute-start.16 = (f32[32,1024]{1,0:T(8,128)S(1)}, f32[32,1024]{1,0:T(8,128)S(1)}, u32[]{:S(2)}, u32[]{:S(2)}) collective-permute-start(f32[32,1024]{1,0:T(8,128)S(1)} %get-tuple-element.31.refs_21_), channel_id=1, source_target_pairs={{0,32},{32,0},{64,96},{96,64},{1,33},{33,1},{65,97},{97,65},{2,34}... | collective-permute-start | bytes 393224 | tf_op jit(solution)/shard_map/ppermute | solution.py:273
  52.2 9.9 %collective-permute-start.17 = (f32[4,1,32,1024]{3,2,1,0:T(8,128)S(1)}, f32[4,1,32,1024]{3,2,1,0:T(8,128)S(1)}, u32[]{:S(2)}, u32[]{:S(2)}) collective-permute-start(f32[4,1,32,1024]{3,2,1,0:T(8,128)S(1)} %pad_maximum_fusion.2.refs_0_), channel_id=1, source_target_pairs={{0,4},{1,17},{2,6},{3,19},{4,0},{5,21},{6,2},{7,23},{8,12},{9,25},... | collective-permute-start | bytes 1572872 | tf_op jit(solution)/shard_map/ppermute | solution.py:218
  52.4 11.4 %collective-permute-start.15 = (f32[4,1,32,1024]{3,2,1,0:T(8,128)S(1)}, f32[4,1,32,1024]{3,2,1,0:T(8,128)S(1)}, u32[]{:S(2)}, u32[]{:S(2)}) collective-permute-start(f32[4,1,32,1024]{3,2,1,0:T(8,128)S(1)} %pad_maximum_fusion.2.refs_0_), channel_id=1, source_target_pairs={{0,32},{32,0},{64,96},{96,64},{1,33},{33,1},{65,97},{97,65},{2,34}... | collective-permute-start | bytes 1572872 | tf_op jit(solution)/shard_map/ppermute | solution.py:272
  54.0 12.9 %collective-permute-start.18 = (f32[4,1,32,1024]{3,2,1,0:T(8,128)S(1)}, f32[4,1,32,1024]{3,2,1,0:T(8,128)S(1)}, u32[]{:S(2)}, u32[]{:S(2)}) collective-permute-start(f32[4,1,32,1024]{3,2,1,0:T(8,128)S(1)} %pad_maximum_fusion.2.refs_0_), channel_id=1, source_target_pairs={{0,1},{1,0},{2,3},{3,2},{4,5},{5,4},{6,7},{7,6},{8,9},{9,8},{10,11... | collective-permute-start | bytes 1572872 | tf_op jit(solution)/shard_map/ppermute | solution.py:230
  56.6 12.4 %collective-permute-start.14 = (f32[4,1,32,1024]{3,2,1,0:T(8,128)S(1)}, f32[4,1,32,1024]{3,2,1,0:T(8,128)S(1)}, u32[]{:S(2)}, u32[]{:S(2)}) collective-permute-start(f32[4,1,32,1024]{3,2,1,0:T(8,128)S(1)} %pad_maximum_fusion.2.refs_0_), channel_id=1, source_target_pairs={{0,6},{1,25},{2,0},{3,27},{4,2},{5,29},{6,4},{7,31},{8,14},{9,1},{... | collective-permute-start | bytes 1572872 | tf_op jit(solution)/shard_map/ppermute | solution.py:218
  56.9 12.7 %collective-permute-start.13 = (f32[4,1,32,1024]{3,2,1,0:T(8,128)S(1)}, f32[4,1,32,1024]{3,2,1,0:T(8,128)S(1)}, u32[]{:S(2)}, u32[]{:S(2)}) collective-permute-start(f32[4,1,32,1024]{3,2,1,0:T(8,128)S(1)} %pad_maximum_fusion.2.refs_0_), channel_id=1, source_target_pairs={{0,2},{1,9},{2,4},{3,11},{4,6},{5,13},{6,0},{7,15},{8,10},{9,17},{... | collective-permute-start | bytes 1572872 | tf_op jit(solution)/shard_map/ppermute | solution.py:218
  63.8 6.7 %collective-permute-start.27 = (f32[4,1,32,1024]{3,2,1,0:T(8,128)S(1)}, f32[4,1,32,1024]{3,2,1,0:T(8,128)S(1)}, u32[]{:S(2)}, u32[]{:S(2)}) collective-permute-start(f32[4,1,32,1024]{3,2,1,0:T(8,128)S(1)} %collective-permute-done.17.refs_3_), channel_id=1, source_target_pairs={{0,1},{1,0},{2,3},{3,2},{4,5},{5,4},{6,7},{7,6},{8,9},{9,8},{10,11... | collective-permute-start | bytes 1572872 | tf_op jit(solution)/shard_map/ppermute | solution.py:230
  66.9 4.8 %collective-permute-start.28 = (f32[4,1,32,1024]{3,2,1,0:T(8,128)S(1)}, f32[4,1,32,1024]{3,2,1,0:T(8,128)S(1)}, u32[]{:S(2)}, u32[]{:S(2)}) collective-permute-start(f32[4,1,32,1024]{3,2,1,0:T(8,128)S(1)} %collective-permute-done.15.refs_7_), channel_id=1, source_target_pairs={{0,1},{1,0},{2,3},{3,2},{4,5},{5,4},{6,7},{7,6},{8,9},{9,8},{10,11... | collective-permute-start | bytes 1572872 | tf_op jit(solution)/shard_map/ppermute | solution.py:230
  66.9 10.0 %collective-permute-start.23 = (f32[4,1,32,1024]{3,2,1,0:T(8,128)S(1)}, f32[4,1,32,1024]{3,2,1,0:T(8,128)}, u32[]{:S(2)}, u32[]{:S(2)}) collective-permute-start(f32[4,1,32,1024]{3,2,1,0:T(8,128)S(1)} %collective-permute-done.15.refs_7_), channel_id=1, source_target_pairs={{0,4},{1,17},{2,6},{3,19},{4,0},{5,21},{6,2},{7,23},{8,12},{9,25},... | collective-permute-start | bytes 1572872 | tf_op jit(solution)/shard_map/ppermute | solution.py:218
  69.0 12.6 %collective-permute-start.22 = (f32[4,1,32,1024]{3,2,1,0:T(8,128)S(1)}, f32[4,1,32,1024]{3,2,1,0:T(8,128)}, u32[]{:S(2)}, u32[]{:S(2)}) collective-permute-start(f32[4,1,32,1024]{3,2,1,0:T(8,128)S(1)} %collective-permute-done.15.refs_7_), channel_id=1, source_target_pairs={{0,6},{1,25},{2,0},{3,27},{4,2},{5,29},{6,4},{7,31},{8,14},{9,1},{... | collective-permute-start | bytes 1572872 | tf_op jit(solution)/shard_map/ppermute | solution.py:218
  69.6 12.8 %collective-permute-start.21 = (f32[4,1,32,1024]{3,2,1,0:T(8,128)S(1)}, f32[4,1,32,1024]{3,2,1,0:T(8,128)}, u32[]{:S(2)}, u32[]{:S(2)}) collective-permute-start(f32[4,1,32,1024]{3,2,1,0:T(8,128)S(1)} %collective-permute-done.15.refs_7_), channel_id=1, source_target_pairs={{0,2},{1,9},{2,4},{3,11},{4,6},{5,13},{6,0},{7,15},{8,10},{9,17},{... | collective-permute-start | bytes 1572872 | tf_op jit(solution)/shard_map/ppermute | solution.py:218
  70.5 11.9 %copy-start = (f32[4,1,32,1024]{3,2,1,0:T(8,128)}, f32[4,1,32,1024]{3,2,1,0:T(8,128)S(1)}, u32[]{:S(2)}) copy-start(f32[4,1,32,1024]{3,2,1,0:T(8,128)S(1)} %collective-permute-done.27.refs_16_) | copy-start | bytes 1572868
  70.5 13.3 %collective-permute-start.20 = (f32[4,1,32,1024]{3,2,1,0:T(8,128)S(1)}, f32[4,1,32,1024]{3,2,1,0:T(8,128)}, u32[]{:S(2)}, u32[]{:S(2)}) collective-permute-start(f32[4,1,32,1024]{3,2,1,0:T(8,128)S(1)} %collective-permute-done.14.refs_2_), channel_id=1, source_target_pairs={{0,1},{1,0},{2,3},{3,2},{4,5},{5,4},{6,7},{7,6},{8,9},{9,8},{10,11... | collective-permute-start | bytes 1572872 | tf_op jit(solution)/shard_map/ppermute | solution.py:230
  71.7 10.8 %copy-start.1 = (f32[4,1,32,1024]{3,2,1,0:T(8,128)}, f32[4,1,32,1024]{3,2,1,0:T(8,128)S(1)}, u32[]{:S(2)}) copy-start(f32[4,1,32,1024]{3,2,1,0:T(8,128)S(1)} %collective-permute-done.28.refs_17_) | copy-start | bytes 1572868
  71.7 12.1 %collective-permute-start.19 = (f32[4,1,32,1024]{3,2,1,0:T(8,128)S(1)}, f32[4,1,32,1024]{3,2,1,0:T(8,128)}, u32[]{:S(2)}, u32[]{:S(2)}) collective-permute-start(f32[4,1,32,1024]{3,2,1,0:T(8,128)S(1)} %collective-permute-done.13.refs_1_), channel_id=1, source_target_pairs={{0,1},{1,0},{2,3},{3,2},{4,5},{5,4},{6,7},{7,6},{8,9},{9,8},{10,11... | collective-permute-start | bytes 1572872 | tf_op jit(solution)/shard_map/ppermute | solution.py:230
  76.8 7.0 %collective-permute-start.26 = (f32[4,1,32,1024]{3,2,1,0:T(8,128)}, f32[4,1,32,1024]{3,2,1,0:T(8,128)}, u32[]{:S(2)}, u32[]{:S(2)}) collective-permute-start(f32[4,1,32,1024]{3,2,1,0:T(8,128)} %collective-permute-done.23.refs_10_), channel_id=1, source_target_pairs={{0,1},{1,0},{2,3},{3,2},{4,5},{5,4},{6,7},{7,6},{8,9},{9,8},{10,11... | collective-permute-start | bytes 1572872 | tf_op jit(solution)/shard_map/ppermute | solution.py:230
  81.6 2.5 %collective-permute-start.25 = (f32[4,1,32,1024]{3,2,1,0:T(8,128)}, f32[4,1,32,1024]{3,2,1,0:T(8,128)}, u32[]{:S(2)}, u32[]{:S(2)}) collective-permute-start(f32[4,1,32,1024]{3,2,1,0:T(8,128)} %collective-permute-done.22.refs_9_), channel_id=1, source_target_pairs={{0,1},{1,0},{2,3},{3,2},{4,5},{5,4},{6,7},{7,6},{8,9},{9,8},{10,11... | collective-permute-start | bytes 1572872 | tf_op jit(solution)/shard_map/ppermute | solution.py:230
  82.4 3.2 %collective-permute-start.24 = (f32[4,1,32,1024]{3,2,1,0:T(8,128)}, f32[4,1,32,1024]{3,2,1,0:T(8,128)}, u32[]{:S(2)}, u32[]{:S(2)}) collective-permute-start(f32[4,1,32,1024]{3,2,1,0:T(8,128)} %collective-permute-done.21.refs_8_), channel_id=1, source_target_pairs={{0,1},{1,0},{2,3},{3,2},{4,5},{5,4},{6,7},{7,6},{8,9},{9,8},{10,11... | collective-permute-start | bytes 1572872 | tf_op jit(solution)/shard_map/ppermute | solution.py:230
  105.3 8.7 %collective-permute-start.31 = (f32[32,1024]{1,0:T(8,128)S(1)}, f32[32,1024]{1,0:T(8,128)S(1)}, u32[]{:S(2)}, u32[]{:S(2)}) collective-permute-start(f32[32,1024]{1,0:T(8,128)S(1)} %get-tuple-element.38), channel_id=1, source_target_pairs={{32,0},{64,96},{33,1},{65,97},{34,2},{66,98},{35,3},{67,99},{36,4}... | collective-permute-start | bytes 393224 | tf_op jit(solution)/shard_map/ppermute | solution.py:285
  106.6 7.4 %collective-permute-start.30 = (f32[32,1024]{1,0:T(8,128)S(1)}, f32[32,1024]{1,0:T(8,128)S(1)}, u32[]{:S(2)}, u32[]{:S(2)}) collective-permute-start(f32[32,1024]{1,0:T(8,128)S(1)} %get-tuple-element.38), channel_id=1, source_target_pairs={{32,64},{64,32},{33,65},{65,33},{34,66},{66,34},{35,67},{67,35},{3... | collective-permute-start | bytes 393224 | tf_op jit(solution)/shard_map/ppermute | solution.py:286
  107.3 10.8 %collective-permute-start.29 = (f32[32,1024]{1,0:T(8,128)S(1)}, f32[32,1024]{1,0:T(8,128)S(1)}, u32[]{:S(2)}, u32[]{:S(2)}) collective-permute-start(f32[32,1024]{1,0:T(8,128)S(1)} %get-tuple-element.39), channel_id=1, source_target_pairs={{0,64},{64,0},{32,96},{96,32},{1,65},{65,1},{33,97},{97,33},{2,66}... | collective-permute-start | bytes 393224 | tf_op jit(solution)/shard_map/ppermute | solution.py:284
  118.1 8.5 %collective-permute-start.34 = (f32[3,32,1024]{2,1,0:T(8,128)S(1)}, f32[3,32,1024]{2,1,0:T(8,128)S(1)}, u32[]{:S(2)}, u32[]{:S(2)}) collective-permute-start(f32[3,32,1024]{2,1,0:T(8,128)S(1)} %pad_maximum_fusion.4), channel_id=1, source_target_pairs={{0,16},{1,5},{2,18},{3,7},{4,20},{5,1},{6,22},{7,3},{8,24},{9,13},... | collective-permute-start | bytes 1179656 | tf_op jit(solution)/shard_map/ppermute | solution.py:218
  119.2 10.8 %collective-permute-start.33 = (f32[3,32,1024]{2,1,0:T(8,128)S(1)}, f32[3,32,1024]{2,1,0:T(8,128)S(1)}, u32[]{:S(2)}, u32[]{:S(2)}) collective-permute-start(f32[3,32,1024]{2,1,0:T(8,128)S(1)} %pad_maximum_fusion.4), channel_id=1, source_target_pairs={{0,24},{1,7},{2,26},{3,1},{4,28},{5,3},{6,30},{7,5},{8,0},{9,15},{... | collective-permute-start | bytes 1179656 | tf_op jit(solution)/shard_map/ppermute | solution.py:218
  120.9 9.9 %collective-permute-start.32 = (f32[3,32,1024]{2,1,0:T(8,128)S(1)}, f32[3,32,1024]{2,1,0:T(8,128)S(1)}, u32[]{:S(2)}, u32[]{:S(2)}) collective-permute-start(f32[3,32,1024]{2,1,0:T(8,128)S(1)} %pad_maximum_fusion.4), channel_id=1, source_target_pairs={{0,8},{1,3},{2,10},{3,5},{4,12},{5,7},{6,14},{7,1},{8,16},{9,11},{... | collective-permute-start | bytes 1179656 | tf_op jit(solution)/shard_map/ppermute | solution.py:218
  131.0 15.6 %collective-permute-start.37 = (f32[4,2,32,1024]{3,2,1,0:T(8,128)S(1)}, f32[4,2,32,1024]{3,2,1,0:T(8,128)S(1)}, u32[]{:S(2)}, u32[]{:S(2)}) collective-permute-start(f32[4,2,32,1024]{3,2,1,0:T(8,128)S(1)} %pad_maximum_fusion.refs_0_), channel_id=1, source_target_pairs={{0,4},{1,17},{2,6},{3,19},{4,0},{5,21},{6,2},{7,23},{8,12},{9,25},... | collective-permute-start | bytes 3145736 | tf_op jit(solution)/shard_map/ppermute | solution.py:218
  133.0 23.9 %collective-permute-start.36 = (f32[4,2,32,1024]{3,2,1,0:T(8,128)S(1)}, f32[4,2,32,1024]{3,2,1,0:T(8,128)S(1)}, u32[]{:S(2)}, u32[]{:S(2)}) collective-permute-start(f32[4,2,32,1024]{3,2,1,0:T(8,128)S(1)} %pad_maximum_fusion.refs_0_), channel_id=1, source_target_pairs={{0,6},{1,25},{2,0},{3,27},{4,2},{5,29},{6,4},{7,31},{8,14},{9,1},{... | collective-permute-start | bytes 3145736 | tf_op jit(solution)/shard_map/ppermute | solution.py:218
  133.5 26.3 %collective-permute-start.35 = (f32[4,2,32,1024]{3,2,1,0:T(8,128)S(1)}, f32[4,2,32,1024]{3,2,1,0:T(8,128)S(1)}, u32[]{:S(2)}, u32[]{:S(2)}) collective-permute-start(f32[4,2,32,1024]{3,2,1,0:T(8,128)S(1)} %pad_maximum_fusion.refs_0_), channel_id=1, source_target_pairs={{0,2},{1,9},{2,4},{3,11},{4,6},{5,13},{6,0},{7,15},{8,10},{9,17},{... | collective-permute-start | bytes 3145736 | tf_op jit(solution)/shard_map/ppermute | solution.py:218
  134.5 35.2 %collective-permute-start.41 = (f32[4,2,32,1024]{3,2,1,0:T(8,128)S(1)}, f32[4,2,32,1024]{3,2,1,0:T(8,128)S(1)}, u32[]{:S(2)}, u32[]{:S(2)}) collective-permute-start(f32[4,2,32,1024]{3,2,1,0:T(8,128)S(1)} %pad_maximum_fusion.refs_0_), channel_id=1, source_target_pairs={{0,1},{1,0},{2,3},{3,2},{4,5},{5,4},{6,7},{7,6},{8,9},{9,8},{10,11... | collective-permute-start | bytes 3145736 | tf_op jit(solution)/shard_map/ppermute | solution.py:230
  146.5 24.1 %collective-permute-start.44 = (f32[4,2,32,1024]{3,2,1,0:T(8,128)S(1)}, f32[4,2,32,1024]{3,2,1,0:T(8,128)S(1)}, u32[]{:S(2)}, u32[]{:S(2)}) collective-permute-start(f32[4,2,32,1024]{3,2,1,0:T(8,128)S(1)} %collective-permute-done.37.refs_3_), channel_id=1, source_target_pairs={{0,1},{1,0},{2,3},{3,2},{4,5},{5,4},{6,7},{7,6},{8,9},{9,8},{10,11... | collective-permute-start | bytes 3145736 | tf_op jit(solution)/shard_map/ppermute | solution.py:230
  156.9 14.2 %collective-permute-start.43 = (f32[4,2,32,1024]{3,2,1,0:T(8,128)S(1)}, f32[4,2,32,1024]{3,2,1,0:T(8,128)S(1)}, u32[]{:S(2)}, u32[]{:S(2)}) collective-permute-start(f32[4,2,32,1024]{3,2,1,0:T(8,128)S(1)} %collective-permute-done.36.refs_2_), channel_id=1, source_target_pairs={{0,1},{1,0},{2,3},{3,2},{4,5},{5,4},{6,7},{7,6},{8,9},{9,8},{10,11... | collective-permute-start | bytes 3145736 | tf_op jit(solution)/shard_map/ppermute | solution.py:230
  159.7 11.4 %collective-permute-start.42 = (f32[4,2,32,1024]{3,2,1,0:T(8,128)S(1)}, f32[4,2,32,1024]{3,2,1,0:T(8,128)S(1)}, u32[]{:S(2)}, u32[]{:S(2)}) collective-permute-start(f32[4,2,32,1024]{3,2,1,0:T(8,128)S(1)} %collective-permute-done.35.refs_1_), channel_id=1, source_target_pairs={{0,1},{1,0},{2,3},{3,2},{4,5},{5,4},{6,7},{7,6},{8,9},{9,8},{10,11... | collective-permute-start | bytes 3145736 | tf_op jit(solution)/shard_map/ppermute | solution.py:230
  160.6 7.0 %collective-permute-start.45 = (f32[32,1024]{1,0:T(8,128)S(1)}, f32[32,1024]{1,0:T(8,128)S(1)}, u32[]{:S(2)}, u32[]{:S(2)}) collective-permute-start(f32[32,1024]{1,0:T(8,128)S(1)} %get-tuple-element.40.refs_10_), channel_id=1, source_target_pairs={{32,0},{64,96},{33,1},{65,97},{34,2},{66,98},{35,3},{67,99},{36,4}... | collective-permute-start | bytes 393224 | tf_op jit(solution)/shard_map/ppermute | solution.py:290
  167.6 14.0 %collective-permute-start.40 = (f32[4,1,32,1024]{3,2,1,0:T(8,128)S(1)}, f32[4,1,32,1024]{3,2,1,0:T(8,128)S(1)}, u32[]{:S(2)}, u32[]{:S(2)}) collective-permute-start(f32[4,1,32,1024]{3,2,1,0:T(8,128)S(1)} %pad_maximum_fusion.3.refs_0_), channel_id=1, source_target_pairs={{0,4},{1,17},{2,6},{3,19},{4,0},{5,21},{6,2},{7,23},{8,12},{9,25},... | collective-permute-start | bytes 1572872 | tf_op jit(solution)/shard_map/ppermute | solution.py:218
  169.7 12.6 %collective-permute-start.39 = (f32[4,1,32,1024]{3,2,1,0:T(8,128)S(1)}, f32[4,1,32,1024]{3,2,1,0:T(8,128)S(1)}, u32[]{:S(2)}, u32[]{:S(2)}) collective-permute-start(f32[4,1,32,1024]{3,2,1,0:T(8,128)S(1)} %pad_maximum_fusion.3.refs_0_), channel_id=1, source_target_pairs={{0,6},{1,25},{2,0},{3,27},{4,2},{5,29},{6,4},{7,31},{8,14},{9,1},{... | collective-permute-start | bytes 1572872 | tf_op jit(solution)/shard_map/ppermute | solution.py:218
  170.6 12.4 %collective-permute-start.38 = (f32[4,1,32,1024]{3,2,1,0:T(8,128)S(1)}, f32[4,1,32,1024]{3,2,1,0:T(8,128)S(1)}, u32[]{:S(2)}, u32[]{:S(2)}) collective-permute-start(f32[4,1,32,1024]{3,2,1,0:T(8,128)S(1)} %pad_maximum_fusion.3.refs_0_), channel_id=1, source_target_pairs={{0,2},{1,9},{2,4},{3,11},{4,6},{5,13},{6,0},{7,15},{8,10},{9,17},{... | collective-permute-start | bytes 1572872 | tf_op jit(solution)/shard_map/ppermute | solution.py:218
  183.0 2.6 %collective-permute-start.46 = (f32[32,1024]{1,0:T(8,128)S(1)}, f32[32,1024]{1,0:T(8,128)S(1)}, u32[]{:S(2)}, u32[]{:S(2)}) collective-permute-start(f32[32,1024]{1,0:T(8,128)S(1)} %shard_map.57.refs_5_), channel_id=1, source_target_pairs={{0,1},{1,0},{2,3},{3,2},{4,5},{5,4},{6,7},{7,6},{8,9},{9,8},{10,11... | collective-permute-start | bytes 393224 | tf_op jit(solution)/shard_map/ppermute | solution.py:230
  187.5 1.4 collective-permute-start.47
